TPU v7x, 512 devices: a whole 4x8x8 slice. The times are simulated.
512 devices in a mesh: chan: 32 (over x, z), tm: 16 (over y, core).
Axes of the slice: x: 4, y: 8, z: 8, core: 2. Of those that a mesh axis runs over, the one named last changes fastest.
Arguments:
- samples: bfloat16 [8192, 65536], P('chan', 'tm'), may hold values from -40 to 40, as said below
- start_chan: float32 [8192, 64], P('chan'), may hold values from 0.1 to 1
- start_freq: float32 [512, 64], replicated, may hold values from 0.1 to 1
- start_time: float32 [128, 64], P('tm'), may hold values from 0.1 to 1
Outputs:
- factor_chan: float32 [8192, 64], P('chan')
- factor_freq: float32 [512, 64], replicated
- factor_time: float32 [128, 64], P('tm')
Inputs may be any that keep to these rules, and one draw needn't show every extreme that they name: `samples`: channel amplitudes differ from channel to channel and along the fibre; values lie within the stated bounds.
All inputs are finite; a program needn't handle non-finite values.
Results may differ from a plain program's by a relative error of at most 0.003.
Values may be sent and summed in bfloat16 or wider, within the bound.
No kernel may reach another device: no remote copies, remote signals or barrier semaphores. Data moves between devices by JAX's collectives and lax.ppermute only.
A program may use at most 64 MiB of HBM per device.

v0:
```python
import jax
import jax.numpy as jnp
from jax import lax
from jax.sharding import Mesh
from jax.sharding import PartitionSpec as P

FRAME = 1024
ITERS = 5
TM = ("tm_0", "tm_1")
CHAN = ("chan_0", "chan_1")


def shifted(block, axis, distance):
    devices = range(lax.axis_size(axis))
    route = [(i - distance, i) for i in devices if i - distance in devices]
    return lax.ppermute(block, axis, route)


def total_of_pieces(shard, axis):
    parts = lax.all_gather(shard, axis)
    return parts.sum(axis=0)


def rows_for(lines, devices):
    spare = -len(lines) % devices
    return jnp.pad(lines, [(0, spare)] + [(0, 0)] * (lines.ndim - 1))


def copy_for_each(shard, axis):
    devices = lax.axis_size(axis)
    return lax.all_to_all(
        jnp.broadcast_to(shard[None], (devices, *shard.shape)), axis, 0, 0, tiled=True
    )


def laid_out(parts, dim):
    lengths = list(parts.shape[1:])
    lengths[dim] *= parts.shape[0]
    return jnp.moveaxis(parts, 0, dim).reshape(lengths)


def gathered_by_axis(shard, axes, dim):
    far, near = axes
    first = copy_for_each(shard, far)
    parts = jnp.swapaxes(copy_for_each(first, near), 0, 1)
    return laid_out(parts.reshape(-1, *shard.shape), dim)


def cut_along(shard, dim, devices):
    lengths = shard.shape
    parts = shard.reshape(*lengths[:dim], devices, lengths[dim] // devices, *lengths[dim + 1 :])
    return jnp.moveaxis(parts, dim, 0)


def summed_on_arrival(shard, axis, dim):
    parts = cut_along(shard, dim, lax.axis_size(axis))
    arrived = lax.all_to_all(parts, axis, split_axis=0, concat_axis=0, tiled=True)
    return arrived.sum(axis=0)


def summed_rows(shard, axes, dim):
    far, near = axes
    parts = cut_along(shard, dim, lax.axis_size(far))
    nearer = summed_on_arrival(parts, near, dim + 1)
    arrived = lax.all_to_all(nearer, far, split_axis=0, concat_axis=0, tiled=True)
    return arrived.sum(axis=0)


def total_of(shard, axes):
    lines = shard.reshape(-1)
    padded = rows_for(lines, lax.axis_size(axes[0]) * lax.axis_size(axes[1]))
    whole = gathered_by_axis(summed_rows(padded, axes, 0), axes, 0)
    return lax.slice_in_dim(whole, 0, len(lines)).reshape(shard.shape)


def of_everyone(shard, axis):
    everything = copy_for_each(shard, axis)
    return jnp.sum(everything, axis=0)


def make_table(frame_len):
    half = frame_len // 2
    index_n = jnp.arange(frame_len, dtype=jnp.int32)
    index_k = jnp.arange(half, dtype=jnp.int32)
    phase = (index_n[:, None] * index_k[None, :] % frame_len).astype(jnp.float32)
    angle = 2.0 * jnp.pi * phase / frame_len
    window = 0.5 - 0.5 * jnp.cos(2.0 * jnp.pi * index_n.astype(jnp.float32) / frame_len)
    cosine = window[:, None] * jnp.cos(angle)
    sine = -window[:, None] * jnp.sin(angle)
    return jnp.concatenate([cosine, sine], axis=1).astype(jnp.bfloat16)


def admm_sweep(product, previous, gram):
    rank_size = gram.shape[0]
    penalty = jnp.trace(gram) / rank_size
    identity = jnp.eye(rank_size, dtype=gram.dtype)
    lower = jnp.linalg.cholesky(gram + penalty * identity)
    inverse = jax.scipy.linalg.cho_solve((lower, True), identity)
    current = previous
    dual_var = jnp.zeros_like(previous)
    for step in range(ITERS):
        target = jnp.dot(
            product + penalty * (current + dual_var), inverse, precision=lax.Precision.HIGHEST
        )
        current = jnp.maximum(target - dual_var, 0.0)
        dual_var = dual_var + current - target
    return current


def local(samples, start_chan, start_freq, start_time):
    high = lax.Precision.HIGHEST
    chan_count = samples.shape[0]
    half_frame = FRAME // 2
    frame_count = samples.shape[1] // half_frame
    following = shifted(samples[:, :half_frame], TM, -1)
    extended = jnp.concatenate([samples, following], axis=1)
    pieces = extended.reshape(chan_count, frame_count + 1, half_frame)
    frames = jnp.concatenate([pieces[:, :-1], pieces[:, 1:]], axis=2).reshape(-1, FRAME)
    spectrum = jnp.dot(frames, make_table(FRAME), preferred_element_type=jnp.float32)
    power_spec = (spectrum[:, :half_frame] ** 2 + spectrum[:, half_frame:] ** 2) / (
        3.0 * FRAME / 8.0
    )
    spec = power_spec.reshape(chan_count, frame_count, half_frame)
    gram_time = total_of_pieces(jnp.dot(start_time.T, start_time, precision=high), TM)
    gram_freq = jnp.dot(start_freq.T, start_freq, precision=high)
    gram_first = gram_freq * gram_time
    mixed = jnp.einsum("ctf,fr->ctr", spec, start_freq, precision=high)
    m_chan = total_of_pieces(jnp.sum(mixed * start_time[None], axis=1), TM)
    factor_chan = admm_sweep(m_chan, start_chan, gram_first)
    weights = factor_chan[:, None, :] * start_time[None]
    m_freq_local = jnp.einsum("ctf,ctr->fr", spec, weights, precision=high)
    gram_local = jnp.dot(factor_chan.T, factor_chan, precision=high)
    m_freq, gram_chan = (
        total_of(m_freq_local, (("chan_0", "chan_1"), ("tm_0", "tm_1"))),
        total_of(gram_local / lax.axis_size(TM), (("chan_0", "chan_1"), ("tm_0", "tm_1"))),
    )
    factor_freq = admm_sweep(m_freq, start_freq, gram_chan * gram_time)
    mixed_two = jnp.einsum("ctf,fr->ctr", spec, factor_freq, precision=high)
    m_time_local = jnp.einsum("ctr,cr->tr", mixed_two, factor_chan, precision=high)
    m_time = of_everyone(m_time_local, CHAN)
    gram_new = jnp.dot(factor_freq.T, factor_freq, precision=high)
    factor_time = admm_sweep(m_time, start_time, gram_chan * gram_new)
    return (factor_chan, factor_freq, factor_time)


def solution(mesh):
    finer = Mesh(mesh.devices.reshape(4, 8, 8, 2), ("chan_0", "chan_1", "tm_0", "tm_1"))
    return jax.shard_map(
        local,
        mesh=finer,
        in_specs=(P(CHAN, TM), P(CHAN, None), P(), P(TM, None)),
        out_specs=(P(CHAN, None), P(), P(TM, None)),
        check_vma=False,
    )
```

profile of v0, /device:TPU:1, one launch (start us, length us, event | category | flops | bytes accessed | tf_op | source)
XLA Modules:
  0.0 260.3 jit_solution(15677041083137782868)
XLA Ops:
  7.2 3.3 %copy.178 = bf16[256,4096]{0,1:T(8,128)(2,1)S(1)} copy(bf16[256,4096]{1,0:T(8,128)(2,1)} %param.7) | data formatting | bytes 4194304 | tf_op args[0]
  10.5 8.7 %collective-permute-start = (bf16[256,512]{0,1:T(8,128)(2,1)S(1)}, bf16[256,512]{0,1:T(8,128)(2,1)S(1)}, u32[]{:S(2)}, u32[]{:S(2)}) collective-permute-start(bf16[256,512]{0,1:T(8,128)(2,1)S(1)} %slice.32), channel_id=1, source_target_pairs={{1,0},{2,1},{3,2},{4,3},{5,4},{6,5},{7,6},{8,7},{9,8},{10,9},{11,1... | collective-permute-start | bytes 786440 | tf_op jit(solution)/shard_map/ppermute | solution.py:16
  19.4 9.7 %multiply_convert_fusion = (bf16[1024,512]{1,0:T(8,128)(2,1)S(1)}, bf16[1024,512]{1,0:T(8,128)(2,1)}) fusion(f32[1024]{0:T(1024)S(1)} %fusion.163, f32[1024]{0:T(1024)S(1)} %multiply_subtract_fusion), kind=kLoop, calls=%fused_computation.20 | loop fusion | flops 9437184 | bytes 2105344 | tf_op jit(solution)/shard_map/convert.1
  29.5 0.4 fusion.180
  29.9 2.2 pad_maximum_fusion
  32.1 6.9 %copy.179 = bf16[256,8,1024]{2,1,0:T(8,128)(2,1)} copy(bf16[256,8,1024]{0,2,1:T(8,128)(2,1)} %pad_maximum_fusion) | data formatting | bytes 8388608 | tf_op jit(solution)/shard_map/concatenate | solution.py:118
  39.0 6.3 %fusion.3 = f32[2048,1024]{1,0:T(8,128)S(1)} fusion(bf16[256,8,1024]{2,1,0:T(8,128)(2,1)} %copy.179, bf16[1024,512]{1,0:T(8,128)(2,1)S(1)} %get-tuple-element.11, bf16[1024,512]{1,0:T(8,128)(2,1)S(1)} %copy-done.4), kind=kOutput, calls=%fused_computation.6 | convolution fusion | flops 4299161600 | bytes 14680064 | tf_op jit(solution)/shard_map/dot_general | solution.py:119
  45.3 1.0 fusion.2
  46.4 1.9 copy-done
  48.3 4.1 %fusion.17 = f32[256,64]{1,0:T(8,128)} fusion(f32[256,8,512]{2,1,0:T(8,128)S(1)} %fusion.2, f32[8,64]{1,0:T(8,128)S(1)} %copy-done.5, f32[512,64]{0,1:T(8,128)S(1)} %copy-done.1), kind=kOutput, calls=%fused_computation.28 | convolution fusion | flops 805552128 | bytes 4392960 | tf_op jit(solution)/shard_map/ctf,fr->ctr/dot_general | solution.py:127
  52.4 16.1 %all-gather.1 = f32[1024,64]{1,0:T(8,128)S(1)} all-gather(f32[64,64]{1,0:T(8,128)S(1)} %fusion.181), channel_id=3, replica_groups=mesh['chan_0'=4,'chan_1'=8,'tm_0'=8,'tm_1'=2] {'tm_0','tm_1'}, dimensions={0}, use_global_device_ids=true | all-gather | bytes 278528 | tf_op jit(solution)/shard_map/all_gather | solution.py:20
  68.6 0.9 select_reduce_fusion.5
  70.2 5.8 %cholesky.59 = f32[64,64]{1,0:T(8,128)S(1)} custom-call(f32[64,64]{1,0:T(8,128)S(1)} %fusion.111), custom_call_target="Cholesky" | custom-call | tf_op jit(solution)/shard_map/jit(cholesky)/cholesky | solution.py:97
  76.1 0.6 compare_reduce_fusion.2
  76.8 0.7 fusion.97
  77.4 4.9 %custom-call.9 = f32[1,64,64]{1,2,0:T(8,128)S(1)} custom-call(f32[1,64,64]{2,1,0:T(8,128)S(1)} %fusion.97), custom_call_target="InvertDiagBlocksLowerTriangular" | custom-call | tf_op jit(solution)/shard_map/jit(_cho_solve)/triangular_solve | solution.py:98
  82.8 10.8 %all-gather.4.cloned.1.call-done = f32[4096,64]{1,0:T(8,128)} async-done(((f32[256,64]{1,0:T(8,128)}), f32[4096,64]{1,0:T(8,128)}) %all-gather.4.cloned.1.call-update) | async-done | bytes 1048592 | tf_op jit(solution)/shard_map/all_gather | solution.py:20
  93.6 1.7 reduce_sum.97
  97.3 0.7 reshape.81
  98.0 4.7 %all-to-all-start.4 = ((f32[16,1,256]{2,1,0:T(1,128)}), f32[16,1,256]{2,1,0:T(1,128)S(1)}, u32[]{:S(2)}, u32[]{:S(2)}) async-start(f32[16,1,256]{2,1,0:T(1,128)} %reshape.81), calls=%async_computation.4 | async-start | bytes 32768 | tf_op jit(solution)/shard_map/all_to_all | solution.py:57
  102.7 7.3 %all-to-all-done.4 = f32[16,1,256]{2,1,0:T(1,128)S(1)} async-done(((f32[16,1,256]{2,1,0:T(1,128)}), f32[16,1,256]{2,1,0:T(1,128)S(1)}, u32[]{:S(2)}, u32[]{:S(2)}) %all-to-all-start.4) | async-done | bytes 16416 | tf_op jit(solution)/shard_map/all_to_all | solution.py:57
  110.0 0.5 broadcast.218
  110.5 0.7 reduce.9
  111.3 0.7 copy.194
  112.0 9.9 %all-to-all-start.5 = ((f32[32,1,8]{2,1,0:T(1,128)}), f32[32,1,8]{2,1,0:T(1,128)S(1)}, u32[]{:S(2)}, u32[]{:S(2)}) async-start(f32[32,1,8]{2,1,0:T(1,128)} %copy.194), calls=%async_computation.5 | async-start | bytes 32768 | tf_op jit(solution)/shard_map/all_to_all | solution.py:65
  122.1 5.6 %copy.185 = f32[256,8,512]{0,1,2:T(8,128)} copy(f32[256,8,512]{2,1,0:T(8,128)} %copy-done) | data formatting | bytes 8388608 | tf_op jit(solution)/shard_map/reshape | solution.py:123
  127.7 2.7 %all-to-all-done.5 = f32[32,1,8]{2,1,0:T(1,128)S(1)} async-done(((f32[32,1,8]{2,1,0:T(1,128)}), f32[32,1,8]{2,1,0:T(1,128)S(1)}, u32[]{:S(2)}, u32[]{:S(2)}) %all-to-all-start.5) | async-done | bytes 1056 | tf_op jit(solution)/shard_map/all_to_all | solution.py:65
  130.5 0.6 broadcast_in_dim.27
  131.1 6.5 %all-to-all-start.6 = ((f32[32,1,8]{2,1,0:T(1,128)}), f32[32,1,8]{2,1,0:T(1,128)S(1)}, u32[]{:S(2)}, u32[]{:S(2)}) async-start(f32[32,1,8]{2,1,0:T(1,128)} %broadcast_in_dim.27), calls=%async_computation.6 | async-start | bytes 32768 | tf_op jit(solution)/shard_map/all_to_all | solution.py:31
  137.7 0.4 copy.188
  138.1 8.1 %all-to-all-done.6 = f32[32,1,8]{2,1,0:T(1,128)S(1)} async-done(((f32[32,1,8]{2,1,0:T(1,128)}), f32[32,1,8]{2,1,0:T(1,128)S(1)}, u32[]{:S(2)}, u32[]{:S(2)}) %all-to-all-start.6) | async-done | bytes 1056 | tf_op jit(solution)/shard_map/all_to_all | solution.py:31
  146.3 0.7 reshape.83
  147.0 5.6 %all-to-all-start.7 = ((f32[16,1,256]{2,1,0:T(1,128)}), f32[16,1,256]{2,1,0:T(1,128)S(1)}, u32[]{:S(2)}, u32[]{:S(2)}) async-start(f32[16,1,256]{2,1,0:T(1,128)} %reshape.83), calls=%async_computation.7 | async-start | bytes 32768 | tf_op jit(solution)/shard_map/all_to_all | solution.py:31
  152.6 6.4 %fusion.19 = f32[16,32,64]{2,0,1:T(8,128)S(1)} fusion(f32[32,16,256,8]{2,3,1,0:T(8,128)} %bitcast.114, f32[256,8,64]{0,2,1:T(8,128)S(1)} %copy.188), kind=kOutput, calls=%fused_computation.30 | convolution fusion | flops 805306368 | bytes 4849664 | tf_op jit(solution)/shard_map/ctf,ctr->fr/dot_general | solution.py:131
  159.1 0.8 reshape.85
  160.1 7.3 %all-to-all-start = ((f32[16,1,2048]{2,1,0:T(1,128)}), f32[16,1,2048]{2,1,0:T(1,128)S(1)}, u32[]{:S(2)}, u32[]{:S(2)}) async-start(f32[16,1,2048]{2,1,0:T(1,128)} %reshape.85), calls=%async_computation | async-start | bytes 262144 | tf_op jit(solution)/shard_map/all_to_all | solution.py:57
  167.3 0.7 reduce.10
  168.3 0.7 select_reduce_fusion
  170.0 5.8 %cholesky.70 = f32[64,64]{1,0:T(8,128)S(1)} custom-call(f32[64,64]{1,0:T(8,128)S(1)} %fusion.107), custom_call_target="Cholesky" | custom-call | tf_op jit(solution)/shard_map/jit(cholesky)/cholesky | solution.py:97
  175.9 0.4 all-to-all-done
  176.2 0.9 reduce.11
  177.3 0.6 reduce_sum.100
  177.9 4.0 %all-to-all-start.1 = ((f32[32,1,64]{2,1,0:T(1,128)}), f32[32,1,64]{2,1,0:T(1,128)S(1)}, u32[]{:S(2)}, u32[]{:S(2)}) async-start(f32[32,1,64]{2,1,0:T(1,128)} %bitcast.17), calls=%async_computation.1 | async-start | bytes 32768 | tf_op jit(solution)/shard_map/all_to_all | solution.py:65
  182.0 0.6 compare_reduce_fusion.1
  182.6 7.7 %all-to-all-done.1 = f32[32,1,64]{2,1,0:T(1,128)S(1)} async-done(((f32[32,1,64]{2,1,0:T(1,128)}), f32[32,1,64]{2,1,0:T(1,128)S(1)}, u32[]{:S(2)}, u32[]{:S(2)}) %all-to-all-start.1) | async-done | bytes 8224 | tf_op jit(solution)/shard_map/all_to_all | solution.py:65
  190.4 0.6 broadcast_in_dim.24
  191.0 3.8 %all-to-all-start.2 = ((f32[32,1,64]{2,1,0:T(1,128)}), f32[32,1,64]{2,1,0:T(1,128)S(1)}, u32[]{:S(2)}, u32[]{:S(2)}) async-start(f32[32,1,64]{2,1,0:T(1,128)} %broadcast_in_dim.24), calls=%async_computation.2 | async-start | bytes 32768 | tf_op jit(solution)/shard_map/all_to_all | solution.py:31
  194.9 0.6 fusion.98
  195.5 4.9 %custom-call.10 = f32[1,64,64]{1,2,0:T(8,128)S(1)} custom-call(f32[1,64,64]{2,1,0:T(8,128)S(1)} %fusion.98), custom_call_target="InvertDiagBlocksLowerTriangular" | custom-call | tf_op jit(solution)/shard_map/jit(_cho_solve)/triangular_solve | solution.py:98
  200.4 3.1 %all-to-all-done.2 = f32[32,1,64]{2,1,0:T(1,128)S(1)} async-done(((f32[32,1,64]{2,1,0:T(1,128)}), f32[32,1,64]{2,1,0:T(1,128)S(1)}, u32[]{:S(2)}, u32[]{:S(2)}) %all-to-all-start.2) | async-done | bytes 8224 | tf_op jit(solution)/shard_map/all_to_all | solution.py:31
  203.5 0.8 reshape.87
  204.3 9.2 %all-to-all-start.3 = ((f32[16,1,2048]{2,1,0:T(1,128)}), f32[16,1,2048]{2,1,0:T(1,128)S(1)}, u32[]{:S(2)}, u32[]{:S(2)}) async-start(f32[16,1,2048]{2,1,0:T(1,128)} %reshape.87), calls=%async_computation.3 | async-start | bytes 262144 | tf_op jit(solution)/shard_map/all_to_all | solution.py:31
  213.9 8.5 %all-to-all-done.3 = f32[16,1,2048]{2,1,0:T(1,128)S(1)} async-done(((f32[16,1,2048]{2,1,0:T(1,128)}), f32[16,1,2048]{2,1,0:T(1,128)S(1)}, u32[]{:S(2)}, u32[]{:S(2)}) %all-to-all-start.3) | async-done | bytes 131104 | tf_op jit(solution)/shard_map/all_to_all | solution.py:31
  222.4 0.9 reduce.12
  225.4 0.9 select_reduce_fusion.4
  226.3 5.6 %fusion.18 = f32[64,8]{0,1:T(8,128)S(1)} fusion(f32[256,8,512]{2,1,0:T(8,128)} %copy-done, f32[64,256]{0,1:T(8,128)S(1)} %copy.223, f32[512,64]{0,1:T(8,128)S(1)} %fusion.22), kind=kOutput, calls=%fused_computation.29 | convolution fusion | flops 805568000 | bytes 4392960 | tf_op jit(solution)/shard_map/ctf,fr->ctr/dot_general | solution.py:138
  231.9 0.7 reshape.89
  232.6 5.3 %all-to-all-start.8 = ((f32[32,1,512]{2,1,0:T(1,128)}), f32[32,1,512]{2,1,0:T(1,128)S(1)}, u32[]{:S(2)}, u32[]{:S(2)}) async-start(f32[32,1,512]{2,1,0:T(1,128)} %reshape.89), calls=%async_computation.8 | async-start | bytes 131072 | tf_op jit(solution)/shard_map/all_to_all | solution.py:31
  238.7 5.8 %cholesky.81 = f32[64,64]{1,0:T(8,128)S(1)} custom-call(f32[64,64]{1,0:T(8,128)S(1)} %fusion.103), custom_call_target="Cholesky" | custom-call | tf_op jit(solution)/shard_map/jit(cholesky)/cholesky | solution.py:97
  244.6 0.7 compare_reduce_fusion
  245.3 0.6 fusion.99
  245.9 4.9 %custom-call.11 = f32[1,64,64]{1,2,0:T(8,128)S(1)} custom-call(f32[1,64,64]{2,1,0:T(8,128)S(1)} %fusion.99), custom_call_target="InvertDiagBlocksLowerTriangular" | custom-call | tf_op jit(solution)/shard_map/jit(_cho_solve)/triangular_solve | solution.py:98
  251.2 0.8 reduce.13
  252.7 0.8 fusion.24
  (90 shorter events, 8.3 us)
Async XLA Ops:
  7.2 86.5 %all-gather.4.cloned.1.call-start = ((), (), s32[]{:S(2)}) async-start(), calls=%async_computation.9 | async-start | bytes 2228224 | tf_op jit(solution)/shard_map/all_gather | solution.py:20
  10.5 18.6 %copy-start.5 = (f32[8,64]{1,0:T(8,128)S(1)}, f32[8,64]{1,0:T(8,128)}, u32[]{:S(2)}) copy-start(f32[8,64]{1,0:T(8,128)} %param.10) | copy-start | bytes 6148
  10.5 18.8 %collective-permute-start = (bf16[256,512]{0,1:T(8,128)(2,1)S(1)}, bf16[256,512]{0,1:T(8,128)(2,1)S(1)}, u32[]{:S(2)}, u32[]{:S(2)}) collective-permute-start(bf16[256,512]{0,1:T(8,128)(2,1)S(1)} %slice.32), channel_id=1, source_target_pairs={{1,0},{2,1},{3,2},{4,3},{5,4},{6,5},{7,6},{8,7},{9,8},{10,9},{11,1... | collective-permute-start | bytes 786440 | tf_op jit(solution)/shard_map/ppermute | solution.py:16
  32.1 6.9 %copy-start.4 = (bf16[1024,512]{1,0:T(8,128)(2,1)S(1)}, bf16[1024,512]{1,0:T(8,128)(2,1)}, u32[]{:S(2)}) copy-start(bf16[1024,512]{1,0:T(8,128)(2,1)} %get-tuple-element.12) | copy-start | bytes 3145732
  45.3 3.0 %copy-start.1 = (f32[512,64]{0,1:T(8,128)S(1)}, f32[512,64]{0,1:T(8,128)}, u32[]{:S(2)}) copy-start(f32[512,64]{0,1:T(8,128)} %param.9) | copy-start | bytes 393220
  46.4 1.9 copy-start
  52.4 43.1 %copy-start.6 = (f32[256,64]{0,1:T(8,128)S(1)}, f32[256,64]{0,1:T(8,128)}, u32[]{:S(2)}) copy-start(f32[256,64]{0,1:T(8,128)} %param.8) | copy-start | bytes 196612
  96.8 63.2 %copy-start.3 = (f32[256,64]{0,1:T(8,128)}, f32[256,64]{0,1:T(8,128)S(1)}, u32[]{:S(2)}) copy-start(f32[256,64]{0,1:T(8,128)S(1)} %fusion.23) | copy-start | bytes 196612
  98.0 12.0 %all-to-all-start.4 = ((f32[16,1,256]{2,1,0:T(1,128)}), f32[16,1,256]{2,1,0:T(1,128)S(1)}, u32[]{:S(2)}, u32[]{:S(2)}) async-start(f32[16,1,256]{2,1,0:T(1,128)} %reshape.81), calls=%async_computation.4 | async-start | bytes 32768 | tf_op jit(solution)/shard_map/all_to_all | solution.py:57
  112.0 18.5 %all-to-all-start.5 = ((f32[32,1,8]{2,1,0:T(1,128)}), f32[32,1,8]{2,1,0:T(1,128)S(1)}, u32[]{:S(2)}, u32[]{:S(2)}) async-start(f32[32,1,8]{2,1,0:T(1,128)} %copy.194), calls=%async_computation.5 | async-start | bytes 32768 | tf_op jit(solution)/shard_map/all_to_all | solution.py:65
  131.1 15.1 %all-to-all-start.6 = ((f32[32,1,8]{2,1,0:T(1,128)}), f32[32,1,8]{2,1,0:T(1,128)S(1)}, u32[]{:S(2)}, u32[]{:S(2)}) async-start(f32[32,1,8]{2,1,0:T(1,128)} %broadcast_in_dim.27), calls=%async_computation.6 | async-start | bytes 32768 | tf_op jit(solution)/shard_map/all_to_all | solution.py:31
  147.0 13.0 %all-to-all-start.7 = ((f32[16,1,256]{2,1,0:T(1,128)}), f32[16,1,256]{2,1,0:T(1,128)S(1)}, u32[]{:S(2)}, u32[]{:S(2)}) async-start(f32[16,1,256]{2,1,0:T(1,128)} %reshape.83), calls=%async_computation.7 | async-start | bytes 32768 | tf_op jit(solution)/shard_map/all_to_all | solution.py:31
  160.1 16.2 %all-to-all-start = ((f32[16,1,2048]{2,1,0:T(1,128)}), f32[16,1,2048]{2,1,0:T(1,128)S(1)}, u32[]{:S(2)}, u32[]{:S(2)}) async-start(f32[16,1,2048]{2,1,0:T(1,128)} %reshape.85), calls=%async_computation | async-start | bytes 262144 | tf_op jit(solution)/shard_map/all_to_all | solution.py:57
  177.9 12.4 %all-to-all-start.1 = ((f32[32,1,64]{2,1,0:T(1,128)}), f32[32,1,64]{2,1,0:T(1,128)S(1)}, u32[]{:S(2)}, u32[]{:S(2)}) async-start(f32[32,1,64]{2,1,0:T(1,128)} %bitcast.17), calls=%async_computation.1 | async-start | bytes 32768 | tf_op jit(solution)/shard_map/all_to_all | solution.py:65
  191.0 12.4 %all-to-all-start.2 = ((f32[32,1,64]{2,1,0:T(1,128)}), f32[32,1,64]{2,1,0:T(1,128)S(1)}, u32[]{:S(2)}, u32[]{:S(2)}) async-start(f32[32,1,64]{2,1,0:T(1,128)} %broadcast_in_dim.24), calls=%async_computation.2 | async-start | bytes 32768 | tf_op jit(solution)/shard_map/all_to_all | solution.py:31
  204.3 18.1 %all-to-all-start.3 = ((f32[16,1,2048]{2,1,0:T(1,128)}), f32[16,1,2048]{2,1,0:T(1,128)S(1)}, u32[]{:S(2)}, u32[]{:S(2)}) async-start(f32[16,1,2048]{2,1,0:T(1,128)} %reshape.87), calls=%async_computation.3 | async-start | bytes 262144 | tf_op jit(solution)/shard_map/all_to_all | solution.py:31
  225.4 6.5 %copy-start.2 = (f32[512,64]{0,1:T(8,128)}, f32[512,64]{0,1:T(8,128)S(1)}, u32[]{:S(2)}) copy-start(f32[512,64]{0,1:T(8,128)S(1)} %fusion.22) | copy-start | bytes 393220
  232.6 18.6 %all-to-all-start.8 = ((f32[32,1,512]{2,1,0:T(1,128)}), f32[32,1,512]{2,1,0:T(1,128)S(1)}, u32[]{:S(2)}, u32[]{:S(2)}) async-start(f32[32,1,512]{2,1,0:T(1,128)} %reshape.89), calls=%async_computation.8 | async-start | bytes 131072 | tf_op jit(solution)/shard_map/all_to_all | solution.py:31
Sparse Core Ops, SparseCore 0:
  52.5 41.0 all-gather.3
where the time goes:
time: 261 us; the launch traced here: 260 us
  starting transfers between devices  65 us (25%)
  other arithmetic  56.9 us (22%)
  waiting for transfers between devices  48.7 us (19%)
  matrix products  30 us (11%)
  local copies, waits for them, and re-layouts  27.1 us (10%)
  between operations  16.5 us (6%)
  blocking collectives  16.1 us (6%)
    all_to_all x5, starting transfers between devices, copy_for_each(): lax.all_to_all(jnp.broadcast_to(shard[None], (devices, *shard.shape)), ax...  30.4 us
    all_to_all x5, waiting for transfers between devices, copy_for_each(): lax.all_to_all(jnp.broadcast_to(shard[None], (devices, *shard.shape)), ax...  19.7 us
    another operation x9, other arithmetic, admm_sweep(): lower = jnp.linalg.cholesky(gram + penalty * identity)  19.6 us
    another operation x6, other arithmetic, admm_sweep(): inverse = jax.scipy.linalg.cho_solve((lower, True), identity)  16.6 us
    all_gather x1, blocking collectives, total_of_pieces(): parts = lax.all_gather(shard, axis)  16.1 us
    all_to_all x2, starting transfers between devices, summed_rows(): lax.all_to_all(nearer, far, split_axis=0, concat_axis=0, tiled=True)  13.9 us
    all_to_all x2, starting transfers between devices, summed_on_arrival(): lax.all_to_all(parts, axis, split_axis=0, concat_axis=0, tiled=True)  11.9 us
    all_gather x1, waiting for transfers between devices, total_of_pieces(): parts = lax.all_gather(shard, axis)  10.8 us
  transfers between devices with their start and end apart: 11, of which 8 were waited for; matrix products, arithmetic and copies ran while one was open for 25% of the time, Pallas kernels for 0%

commit v1 on v0

v1 whole, which is shorter than its diff:
```python
import numpy as np
import jax
import jax.numpy as jnp
from jax import lax
from jax.experimental import pallas as pl
from jax.experimental.pallas import tpu as pltpu
from jax.sharding import Mesh
from jax.sharding import PartitionSpec as P

FRAME = 1024
HALF = FRAME // 2
BINS = 512
RANK = 64
ITERS = 5
FRAMES_HERE = 8
CHANS_HERE = 256
PACK = 2 * RANK
TM = ("tm_0", "tm_1")
N_TM = 16
N_X = 4
N_Z = 8
SCALE = 1.0 / (3.0 * FRAME / 8.0)
F32 = jnp.float32
BF16 = jnp.bfloat16
HIGH = lax.Precision.HIGHEST


def half_tables():
    n = np.arange(HALF)[None, :]
    j = np.arange(BINS // 2)[:, None]
    even = 2.0 * np.pi * ((n * (2 * j)) % FRAME) / FRAME
    odd = 2.0 * np.pi * ((n * (2 * j + 1)) % FRAME) / FRAME
    stack = lambda a: np.concatenate([np.cos(a), np.sin(a)], axis=0)
    return stack(even).astype(BF16), stack(odd).astype(BF16)


def window_row():
    n = np.arange(HALF)[None, :]
    return (0.5 - 0.5 * np.cos(2.0 * np.pi * n / FRAME)).astype(np.float32)


def lane_is_low(shape):
    return lax.broadcasted_iota(jnp.int32, shape, 1) < RANK


def both_halves(x):
    other = pltpu.roll(x, RANK, 1)
    low = lane_is_low(x.shape)
    return jnp.concatenate([jnp.where(low, x, other), jnp.where(low, other, x)], axis=0)


def side_by_side(x):
    m = x.shape[0] // 2
    return jnp.where(lane_is_low((m, PACK)), x[:m], x[m:])


def high_low(x):
    high = x.astype(BF16).astype(F32)
    return jnp.where(lane_is_low(x.shape), high, x - high).astype(BF16)


def doubled(x):
    return jnp.concatenate([x, x], axis=1)


def gram_of(x):
    return lax.dot_general(x, x, (((0,), (0,)), ((), ())), precision=HIGH,
                           preferred_element_type=F32)


def inverse_of(gram):
    row = lax.broadcasted_iota(jnp.int32, gram.shape, 0)
    col = lax.broadcasted_iota(jnp.int32, gram.shape, 1)
    eye = jnp.where(row == col, 1.0, 0.0).astype(F32)
    penalty = jnp.sum(gram * eye) / PACK
    block = (row < RANK) == (col < RANK)
    a = jnp.where(block, gram * (1.0 / penalty), 0.0) + eye
    spread = (RANK / 2.0) / (RANK / 2.0 + 1.0)
    mid = RANK / 2.0 + 1.0
    centre = 1.0 - spread * spread / 2.0
    x = (eye * (2.0 / mid) - a * (1.0 / (mid * mid))) * (1.0 / centre)
    spread = (spread * spread / 2.0) / centre
    for _ in range(5):
        s = jnp.dot(a, x, precision=HIGH, preferred_element_type=F32)
        centre = 1.0 - spread * spread / 2.0
        x = jnp.dot(x, (2.0 * eye - s) * (1.0 / centre), precision=HIGH,
                    preferred_element_type=F32)
        spread = (spread * spread / 2.0) / centre
    return penalty, x


def admm(product, previous, penalty, inverse):
    scaled = product * (1.0 / penalty)
    carried = previous
    dual = jnp.zeros_like(previous)
    value = previous
    for _ in range(ITERS):
        target = jnp.dot(scaled + carried, inverse, precision=HIGH, preferred_element_type=F32)
        value = target - dual
        dual = jnp.maximum(-value, 0.0)
        carried = jnp.abs(value)
    return jnp.maximum(value, 0.0)


def prep_kernel(freq_ref, time_ref, packed_ref, gram_ref, rows_ref, time2_ref):
    half = BINS // 2
    even = freq_ref[pl.ds(0, half, stride=2), :]
    odd = freq_ref[pl.ds(1, half, stride=2), :]
    packed_ref[...] = jnp.concatenate([even, odd], axis=1)
    twice = jnp.concatenate([doubled(even), doubled(odd)], axis=0)
    gram_ref[...] = gram_of(twice)
    rows_ref[...] = high_low(twice).astype(F32).T.astype(BF16)
    time2_ref[...] = doubled(time_ref[...])


def frame_power(first, second, window, even_ref, odd_ref):
    first = first.astype(F32) * window
    second = second.astype(F32)
    second = second - second * window
    total = (first + second).astype(BF16)
    change = (first - second).astype(BF16)
    dims = (((1,), (1,)), ((), ()))
    half = BINS // 2
    out = []
    for table, side in ((even_ref, total), (odd_ref, change)):
        wave = lax.dot_general(table[...], side, dims, preferred_element_type=F32)
        out.append((wave[:half] * wave[:half] + wave[half:] * wave[half:]).astype(BF16))
    return jnp.concatenate(out, axis=0)


def chan_term(rows_ref, power, time_row):
    q = jnp.dot(rows_ref[...], power, preferred_element_type=F32)
    row = lax.broadcasted_iota(jnp.int32, (PACK, PACK), 0)
    col = lax.broadcasted_iota(jnp.int32, (PACK, PACK), 1)
    column = jnp.sum(jnp.where(row == col, time_row, 0.0), axis=1, keepdims=True)
    return q * column


def early_kernel(first_ref, second_ref, window_ref, even_ref, odd_ref, rows_ref, time2_ref,
                 power_ref, sum_ref):
    t = pl.program_id(0)
    power = frame_power(first_ref[...], second_ref[...], window_ref[...], even_ref, odd_ref)
    power_ref[0] = power
    term = chan_term(rows_ref, power, time2_ref[pl.ds(t, 1), :])

    @pl.when(t == 0)
    def _():
        sum_ref[...] = term

    @pl.when(t > 0)
    def _():
        sum_ref[...] += term


def last_kernel(first_ref, second_ref, window_ref, even_ref, odd_ref, rows_ref, time2_ref,
                sum_ref, old_ref, power_ref, send_ref):
    power = frame_power(first_ref[...], second_ref[...], window_ref[...], even_ref, odd_ref)
    power_ref[0] = power
    total = sum_ref[...] + chan_term(rows_ref, power, time2_ref[FRAMES_HERE - 1:, :])
    total = total[:RANK] + total[RANK:]
    half = CHANS_HERE // 2
    packed = jnp.concatenate([total[:, :half], total[:, half:]], axis=0).T
    per = half // N_TM
    for d in range(N_TM):
        send_ref[d, :per] = packed[d * per:(d + 1) * per]
        send_ref[d, per:] = time2_ref[...]


def chan_kernel(got_ref, gram_freq_ref, start_ref, send_ref, gram_time_ref):
    me = lax.axis_index(TM)
    per = CHANS_HERE // 2 // N_TM
    total = jnp.sum(got_ref[:, :per], axis=0)
    times = got_ref[:, per:].reshape(N_TM * FRAMES_HERE, PACK)
    gram_time = gram_of(times)
    gram_time_ref[...] = gram_time
    penalty, inverse = inverse_of(gram_time * gram_freq_ref[...])
    at = pl.multiple_of(me * per, per)
    top = start_ref[pl.ds(at, per), :]
    bottom = start_ref[pl.ds(at + CHANS_HERE // 2, per), :]
    start = jnp.concatenate([top, bottom], axis=1)
    new = admm(total * SCALE, start, penalty, inverse)
    send_ref[...] = jnp.broadcast_to(new[None], send_ref.shape)


FRAMES_STEP = 4


def freq_kernel(chan_ref, power_ref, time2_ref, part_ref, send_ref, gram_ref, chan_out_ref,
                sides, total):
    step = pl.program_id(0)

    @pl.when(step == 0)
    def _():
        rows = both_halves(chan_ref[...].reshape(CHANS_HERE // 2, PACK))
        chan_out_ref[...] = rows[:, :RANK]
        sides[...] = high_low(rows)
        gram_ref[...] = side_by_side(gram_of(rows)[:RANK])
        total[...] = jnp.zeros_like(total)

    for t in range(FRAMES_STEP):
        part = jnp.dot(power_ref[t], sides[...], preferred_element_type=F32)
        part_ref[t] = part
        total[...] += part * time2_ref[pl.ds(step * FRAMES_STEP + t, 1), :]

    @pl.when(step == FRAMES_HERE // FRAMES_STEP - 1)
    def _():
        whole = total[...]
        packed = side_by_side(whole + pltpu.roll(whole, RANK, 1))
        send_ref[...] = packed.reshape(send_ref.shape)


def rows_kernel(got_ref, gram_ref, send_ref):
    rows = got_ref.shape[1]
    total = jnp.sum(got_ref[...], axis=0)
    for d in range(send_ref.shape[0]):
        send_ref[d, :rows] = total
        send_ref[d, rows:] = gram_ref[...]


def relay_kernel(got_ref, send_ref):
    send_ref[...] = jnp.broadcast_to(jnp.sum(got_ref[...], axis=0)[None], send_ref.shape)


def freq_admm_kernel(got_ref, gram_time_ref, packed_ref, send_ref, gram_chan_ref):
    me = lax.axis_index(TM)
    total = jnp.sum(got_ref[...], axis=0)
    per = BINS // 2 // N_TM
    gram = both_halves(total[per:])
    gram = jnp.concatenate([gram, gram], axis=0)
    gram_chan_ref[...] = gram
    penalty, inverse = inverse_of(gram * gram_time_ref[...])
    start = packed_ref[pl.ds(pl.multiple_of(me * per, per), per), :]
    new = admm(total[:per] * SCALE, start, penalty, inverse)
    send_ref[...] = jnp.broadcast_to(new[None], send_ref.shape)


def time_kernel(freq_ref, part_ref, send_ref, freq_out_ref):
    half = BINS // 2
    rows = both_halves(freq_ref[...].reshape(half, PACK))
    freq_out_ref[pl.ds(0, half, stride=2), :] = rows[:half, :RANK]
    freq_out_ref[pl.ds(1, half, stride=2), :] = rows[half:, :RANK]
    sums = [jnp.sum(part_ref[t] * rows, axis=0, keepdims=True) for t in range(FRAMES_HERE)]
    product = jnp.concatenate(sums, axis=0)
    send_ref[...] = jnp.broadcast_to(product[None], send_ref.shape)


def time_inverse_kernel(freq_ref, gram_chan_ref, inverse_ref, penalty_ref):
    rows = both_halves(freq_ref[...].reshape(BINS // 2, PACK))
    penalty, inverse = inverse_of(gram_of(rows) * gram_chan_ref[...])
    inverse_ref[...] = inverse
    penalty_ref[...] = jnp.full(penalty_ref.shape, penalty, F32)


def time_admm_kernel(got_ref, inverse_ref, penalty_ref, start2_ref, out_ref):
    total = jnp.sum(got_ref[...], axis=0)
    total = total + pltpu.roll(total, RANK, 1)
    new = admm(total * SCALE, start2_ref[...], penalty_ref[...], inverse_ref[...])
    out_ref[...] = new[:, :RANK]


def shape(*dims, dtype=F32):
    return jax.ShapeDtypeStruct(dims, dtype)


def exchanged(parts, axis):
    return lax.all_to_all(parts, axis, split_axis=0, concat_axis=0, tiled=True)


def fixed(*dims):
    return pl.BlockSpec(dims, lambda t: (0,) * len(dims))


def local(samples, start_chan, start_freq, start_time):
    even_table, odd_table = (jnp.asarray(t) for t in half_tables())
    window = jnp.asarray(window_row())
    route = [(i, i - 1) for i in range(1, N_TM)]
    following = lax.ppermute(samples[:, :HALF], TM, route)

    packed_freq, gram_freq, freq_rows, time2 = pl.pallas_call(
        prep_kernel,
        out_shape=(shape(BINS // 2, PACK), shape(PACK, PACK), shape(PACK, BINS, dtype=BF16),
                   shape(FRAMES_HERE, PACK)),
        name="prep",
    )(start_freq, start_time)

    table_specs = [fixed(1, HALF), fixed(BINS, HALF), fixed(BINS, HALF), fixed(PACK, BINS),
                   fixed(FRAMES_HERE, PACK)]
    early = FRAMES_HERE - 1
    power, early_sum = pl.pallas_call(
        early_kernel,
        grid=(early,),
        in_specs=[pl.BlockSpec((CHANS_HERE, HALF), lambda t: (0, t)),
                  pl.BlockSpec((CHANS_HERE, HALF), lambda t: (0, t + 1))] + table_specs,
        out_specs=[pl.BlockSpec((1, BINS, CHANS_HERE), lambda t: (t, 0, 0)),
                   fixed(PACK, CHANS_HERE)],
        out_shape=(shape(FRAMES_HERE, BINS, CHANS_HERE, dtype=BF16), shape(PACK, CHANS_HERE)),
        cost_estimate=pl.CostEstimate(flops=2500000000, bytes_accessed=8000000,
                                      transcendentals=0),
        name="early",
    )(samples, samples, window, even_table, odd_table, freq_rows, time2)

    power, to_chan = pl.pallas_call(
        last_kernel,
        grid=(1,),
        in_specs=[pl.BlockSpec((CHANS_HERE, HALF), lambda t: (0, early)),
                  fixed(CHANS_HERE, HALF)] + table_specs
        + [fixed(PACK, CHANS_HERE), pl.BlockSpec(memory_space=pl.ANY)],
        out_specs=[pl.BlockSpec((1, BINS, CHANS_HERE), lambda t: (early, 0, 0)),
                   fixed(N_TM, 16, PACK)],
        out_shape=(shape(FRAMES_HERE, BINS, CHANS_HERE, dtype=BF16), shape(N_TM, 16, PACK)),
        input_output_aliases={8: 0},
        name="last",
    )(samples, following, window, even_table, odd_table, freq_rows, time2, early_sum, power)

    got = exchanged(to_chan, TM)
    chan_rows, gram_time = pl.pallas_call(
        chan_kernel,
        out_shape=(shape(N_TM, 8, PACK), shape(PACK, PACK)),
        name="chan",
    )(got, gram_freq, start_chan)
    chan_all = exchanged(chan_rows, TM)

    part, to_freq, gram_part, factor_chan = pl.pallas_call(
        freq_kernel,
        grid=(FRAMES_HERE // FRAMES_STEP,),
        in_specs=[fixed(N_TM, 8, PACK),
                  pl.BlockSpec((FRAMES_STEP, BINS, CHANS_HERE), lambda t: (t, 0, 0)),
                  fixed(FRAMES_HERE, PACK)],
        out_specs=[pl.BlockSpec((FRAMES_STEP, BINS, PACK), lambda t: (t, 0, 0)),
                   fixed(N_TM, 16, PACK), fixed(RANK // 2, PACK), fixed(CHANS_HERE, RANK)],
        out_shape=(shape(FRAMES_HERE, BINS, PACK), shape(N_TM, 16, PACK),
                   shape(RANK // 2, PACK), shape(CHANS_HERE, RANK)),
        scratch_shapes=[pltpu.VMEM((CHANS_HERE, PACK), BF16), pltpu.VMEM((BINS, PACK), F32)],
        name="freq",
    )(chan_all, power, time2)

    got = exchanged(to_freq, TM)
    rows = 16 + RANK // 2
    to_z = pl.pallas_call(rows_kernel, out_shape=shape(N_Z, rows, PACK), name="rows")(
        got, gram_part)
    got = exchanged(to_z, "chan_1")
    to_x = pl.pallas_call(relay_kernel, out_shape=shape(N_X, rows, PACK), name="relay")(got)
    got = exchanged(to_x, "chan_0")
    freq_rows_new, gram_chan = pl.pallas_call(
        freq_admm_kernel,
        out_shape=(shape(N_TM, 16, PACK), shape(PACK, PACK)),
        name="freq_admm",
    )(got, gram_time, packed_freq)
    freq_all = exchanged(freq_rows_new, TM)

    to_z, factor_freq = pl.pallas_call(
        time_kernel,
        out_shape=(shape(N_Z, FRAMES_HERE, PACK), shape(BINS, RANK)),
        name="time",
    )(freq_all, part)
    got = exchanged(to_z, "chan_1")
    inverse, penalty = pl.pallas_call(
        time_inverse_kernel,
        out_shape=(shape(PACK, PACK), shape(1, PACK)),
        name="time_inverse",
    )(freq_all, gram_chan)
    to_x = pl.pallas_call(relay_kernel, out_shape=shape(N_X, FRAMES_HERE, PACK),
                          name="relay_time")(got)
    got = exchanged(to_x, "chan_0")
    factor_time = pl.pallas_call(
        time_admm_kernel, out_shape=shape(FRAMES_HERE, RANK), name="time_admm"
    )(got, inverse, penalty, time2)
    return factor_chan, factor_freq, factor_time


def solution(mesh):
    finer = Mesh(mesh.devices.reshape(4, 8, 8, 2), ("chan_0", "chan_1", "tm_0", "tm_1"))
    chan = ("chan_0", "chan_1")
    return jax.shard_map(
        local,
        mesh=finer,
        in_specs=(P(chan, TM), P(chan, None), P(), P(TM, None)),
        out_specs=(P(chan, None), P(), P(TM, None)),
        check_vma=False,
    )
```

time: 261 us -> 154 us (0.59)
  blocking collectives: 16.1 us -> 80.1 us
  other arithmetic: 56.9 us -> 0 us
  starting transfers between devices: 65 us -> 15.4 us
  Pallas kernels: 0 us -> 41.5 us
  waiting for transfers between devices: 48.7 us -> 7.45 us
  matrix products: 30 us -> 0 us
  local copies, waits for them, and re-layouts: 27.1 us -> 7.82 us
  between operations: 16.5 us -> 0.7 us
    all_to_all x0 -> x6, blocking collectives: none -> 80.1 us  [exchanged(): return lax.all_to_all(parts, axis, split_axis=0, concat_axis=0, tiled=True)]
    all_to_all x9 -> x2, starting transfers between devices: 56.3 us -> 6.64 us  [exchanged(): return lax.all_to_all(parts, axis, split_axis=0, concat_axis=0, tiled=True)]
    another operation x16 -> x0, other arithmetic: 45.8 us -> none  [the longest x9 19.6 us: admm_sweep(): lower = jnp.linalg.cholesky(gram + penalty * identity)]
    pallas_call x0 -> x12, Pallas kernels: none -> 41.5 us  [the longest x1 8.28 us: local(): pl.pallas_call(early_kernel, grid=(early,), in_specs=[pl.BlockSpec((CHANS...]
    all_to_all x9 -> x2, waiting for transfers between devices: 37.8 us -> 7.45 us  [exchanged(): return lax.all_to_all(parts, axis, split_axis=0, concat_axis=0, tiled=True)]
    dot_general x23 -> x0, matrix products: 28.8 us -> none  [the longest x1 6.41 us: local(): m_freq_local = jnp.einsum('ctf,ctr->fr', spec, weights, precision=high)]
    all_gather x1 -> x0, blocking collectives: 16.1 us -> none  [total_of_pieces(): parts = lax.all_gather(shard, axis)]
    all_gather x1 -> x0, waiting for transfers between devices: 10.8 us -> none  [total_of_pieces(): parts = lax.all_gather(shard, axis)]
  transfers between devices with their start and end apart: 11 -> 3, of which waited for: 8 -> 1; matrix products, arithmetic and copies ran while one was open for 25% -> 3% of each run, Pallas kernels for 0% -> 10%
where the time goes in v1:
time: 154 us; the launch traced here: 153 us
  blocking collectives  80.1 us (52%)
  Pallas kernels  41.5 us (27%)
  starting transfers between devices  15.4 us (10%)
  local copies, waits for them, and re-layouts  7.82 us (5%)
  waiting for transfers between devices  7.45 us (5%)
    all_to_all x6, blocking collectives, exchanged(): return lax.all_to_all(parts, axis, split_axis=0, concat_axis=0, tiled=True)  80.1 us
    ppermute x1, starting transfers between devices, local(): following = lax.ppermute(samples[:, :HALF], TM, route)  8.75 us
    pallas_call x1, Pallas kernels, local(): pl.pallas_call(early_kernel, grid=(early,), in_specs=[pl.BlockSpec((CHANS...  8.28 us
    all_to_all x2, waiting for transfers between devices, exchanged(): return lax.all_to_all(parts, axis, split_axis=0, concat_axis=0, tiled=True)  7.45 us
    unnamed x14, local copies, waits for them, and re-layouts  6.85 us
    all_to_all x2, starting transfers between devices, exchanged(): return lax.all_to_all(parts, axis, split_axis=0, concat_axis=0, tiled=True)  6.64 us
    pallas_call x1, Pallas kernels, local(): pl.pallas_call(chan_kernel, out_shape=(shape(N_TM, 8, PACK), shape(PACK,...  5.33 us
    pallas_call x1, Pallas kernels, local(): pl.pallas_call(freq_admm_kernel, out_shape=(shape(N_TM, 16, PACK), shape(...  5.11 us
  transfers between devices with their start and end apart: 3, of which 1 were waited for; matrix products, arithmetic and copies ran while one was open for 3% of the time, Pallas kernels for 10%

profile of v1, /device:TPU:1, one launch (start us, length us, event | category | flops | bytes accessed | tf_op | source)
XLA Modules:
  0.0 152.9 jit_solution(885326264940268230)
XLA Ops:
  0.6 1.0 slice.3
  1.6 8.7 %collective-permute-start = (bf16[256,512]{1,0:T(8,128)(2,1)S(1)}, bf16[256,512]{1,0:T(8,128)(2,1)S(1)}, u32[]{:S(2)}, u32[]{:S(2)}) collective-permute-start(bf16[256,512]{1,0:T(8,128)(2,1)S(1)} %slice.3), channel_id=1, source_target_pairs={{1,0},{2,1},{3,2},{4,3},{5,4},{6,5},{7,6},{8,7},{9,8},{10,9},{11,1... | collective-permute-start | bytes 786440 | tf_op jit(solution)/shard_map/ppermute | solution.py:277
  10.4 1.7 %copy.11.freq_ref = f32[512,64]{1,0:T(8,128)} copy(f32[512,64]{0,1:T(8,128)} %param.9) | data formatting | bytes 262144 | tf_op args[2]
  12.1 2.2 %prep.1 = (f32[256,128]{1,0:T(8,128)}, f32[128,128]{1,0:T(8,128)}, bf16[128,512]{1,0:T(8,128)(2,1)}, f32[8,128]{1,0:T(8,128)}) custom-call(f32[512,64]{1,0:T(8,128)} %copy.11.freq_ref, f32[8,64]{1,0:T(8,128)} %time_ref.1), custom_call_target="tpu_custom_call" | custom-call | tf_op jit(solution)/shard_map/prep/pallas_call | solution.py:279
  14.2 8.3 %early.1 = (bf16[8,512,256]{2,1,0:T(8,128)(2,1)}, f32[128,256]{1,0:T(8,128)}) custom-call(bf16[256,4096]{1,0:T(8,128)(2,1)} %first_ref.3, bf16[256,4096]{1,0:T(8,128)(2,1)} %first_ref.3, f32[1,512]{1,0:T(1,128)} %constant.8.clone.window_ref, bf16[512,512]{1,0:T(8,128)(2,1)} %constant.6.clone.even_ref, bf16[512,512]{1,0:T(8,128)(2,1)} %constant.7.clone.odd_ref, ...), custom_call_target="tpu_custom_call" | custom-call | flops 2500000000 | bytes 8000000 | tf_op jit(solution)/shard_map/early/pallas_call | solution.py:289
  22.5 0.0 collective-permute-done.second_ref
  22.5 0.0 copy-start.1
  22.5 0.7 copy-done.1
  23.2 0.0 copy-start.3
  23.2 2.9 %last.1 = (bf16[8,512,256]{2,1,0:T(8,128)(2,1)}, f32[16,16,128]{2,1,0:T(8,128)}) custom-call(bf16[256,4096]{1,0:T(8,128)(2,1)} %first_ref.3, bf16[256,512]{1,0:T(8,128)(2,1)} %copy-done.1, f32[1,512]{1,0:T(1,128)} %constant.8.clone.window_ref, bf16[512,512]{1,0:T(8,128)(2,1)} %constant.6.clone.even_ref, ...), custom_call_target="tpu_custom_call", output_to_operand_aliasing={{0}: (8, {})} | custom-call | tf_op jit(solution)/shard_map/last/pallas_call | solution.py:302
  26.1 3.4 %all-to-all-start = ((f32[16,16,128]{2,1,0:T(8,128)}), f32[16,16,128]{2,1,0:T(8,128)S(1)}, u32[]{:S(2)}, u32[]{:S(2)}) async-start(f32[16,16,128]{2,1,0:T(8,128)} %get-tuple-element.27), calls=%async_computation | async-start | bytes 262144 | tf_op jit(solution)/shard_map/all_to_all | solution.py:266
  29.5 0.0 copy-done.3
  29.5 0.8 copy.12.start_ref
  30.3 7.4 %all-to-all-done.got_ref = f32[16,16,128]{2,1,0:T(8,128)S(1)} async-done(((f32[16,16,128]{2,1,0:T(8,128)}), f32[16,16,128]{2,1,0:T(8,128)S(1)}, u32[]{:S(2)}, u32[]{:S(2)}) %all-to-all-start) | async-done | bytes 131104 | tf_op jit(solution)/shard_map/all_to_all | solution.py:266
  37.7 0.0 copy-start
  37.7 0.6 copy-done
  38.3 5.3 %chan.1 = (f32[16,8,128]{2,1,0:T(8,128)}, f32[128,128]{1,0:T(8,128)}) custom-call(f32[16,16,128]{2,1,0:T(8,128)} %copy-done, f32[128,128]{1,0:T(8,128)} %get-tuple-element.28.gram_freq_ref, f32[256,64]{1,0:T(8,128)} %copy.12.start_ref), custom_call_target="tpu_custom_call" | custom-call | tf_op jit(solution)/shard_map/chan/pallas_call | solution.py:316
  43.7 11.7 %all_to_all.40.chan_ref = f32[16,8,128]{2,1,0:T(8,128)} all-to-all(f32[16,8,128]{2,1,0:T(8,128)} %get-tuple-element.29), channel_id=1, replica_groups=mesh['chan_0'=4,'chan_1'=8,'tm_0'=8,'tm_1'=2] {'tm_0','tm_1'}, dimensions={0} | all-to-all | bytes 131072 | tf_op jit(solution)/shard_map/all_to_all | solution.py:266
  55.3 3.7 %freq.1 = (f32[8,512,128]{2,1,0:T(8,128)}, f32[16,16,128]{2,1,0:T(8,128)}, f32[32,128]{1,0:T(8,128)}, f32[256,64]{1,0:T(8,128)}) custom-call(f32[16,8,128]{2,1,0:T(8,128)} %all_to_all.40.chan_ref, bf16[8,512,256]{2,1,0:T(8,128)(2,1)} %get-tuple-element.30.power_ref, f32[8,128]{1,0:T(8,128)} %get-tuple-element.24.time2_ref.start2_ref), custom_call_target="tpu_custom_call" | custom-call | tf_op jit(solution)/shard_map/freq/pallas_call | solution.py:323
  59.0 13.3 %all_to_all.41.got_ref = f32[16,16,128]{2,1,0:T(8,128)} all-to-all(f32[16,16,128]{2,1,0:T(8,128)} %get-tuple-element.32), channel_id=1, replica_groups=mesh['chan_0'=4,'chan_1'=8,'tm_0'=8,'tm_1'=2] {'tm_0','tm_1'}, dimensions={0} | all-to-all | bytes 262144 | tf_op jit(solution)/shard_map/all_to_all | solution.py:266
  72.3 0.0 copy-start.2
  72.3 1.6 %rows.1 = f32[8,48,128]{2,1,0:T(8,128)} custom-call(f32[16,16,128]{2,1,0:T(8,128)} %all_to_all.41.got_ref, f32[32,128]{1,0:T(8,128)} %get-tuple-element.33.gram_ref), custom_call_target="tpu_custom_call" | custom-call | tf_op jit(solution)/shard_map/rows/pallas_call | solution.py:339
  74.0 20.3 %all_to_all.42.got_ref = f32[8,48,128]{2,1,0:T(8,128)} all-to-all(f32[8,48,128]{2,1,0:T(8,128)} %rows.1), channel_id=1, replica_groups=mesh['chan_0'=4,'chan_1'=8,'tm_0'=8,'tm_1'=2] {'chan_1'}, dimensions={0} | all-to-all | bytes 393216 | tf_op jit(solution)/shard_map/all_to_all | solution.py:266
  94.2 1.6 %relay.1 = f32[4,48,128]{2,1,0:T(8,128)} custom-call(f32[8,48,128]{2,1,0:T(8,128)} %all_to_all.42.got_ref), custom_call_target="tpu_custom_call" | custom-call | tf_op jit(solution)/shard_map/relay/pallas_call | solution.py:342
  95.8 8.8 %all_to_all.43.got_ref = f32[4,48,128]{2,1,0:T(8,128)} all-to-all(f32[4,48,128]{2,1,0:T(8,128)} %relay.1), channel_id=1, replica_groups=mesh['chan_0'=4,'chan_1'=8,'tm_0'=8,'tm_1'=2] {'chan_0'}, dimensions={0} | all-to-all | bytes 196608 | tf_op jit(solution)/shard_map/all_to_all | solution.py:266
  104.6 5.1 %freq_admm.1 = (f32[16,16,128]{2,1,0:T(8,128)}, f32[128,128]{1,0:T(8,128)}) custom-call(f32[4,48,128]{2,1,0:T(8,128)} %all_to_all.43.got_ref, f32[128,128]{1,0:T(8,128)} %get-tuple-element.34.gram_time_ref, f32[256,128]{1,0:T(8,128)} %get-tuple-element.35.packed_ref), custom_call_target="tpu_custom_call" | custom-call | tf_op jit(solution)/shard_map/freq_admm/pallas_call | solution.py:344
  109.7 15.0 %all_to_all.44.freq_ref = f32[16,16,128]{2,1,0:T(8,128)} all-to-all(f32[16,16,128]{2,1,0:T(8,128)} %get-tuple-element.36), channel_id=1, replica_groups=mesh['chan_0'=4,'chan_1'=8,'tm_0'=8,'tm_1'=2] {'tm_0','tm_1'}, dimensions={0} | all-to-all | bytes 262144 | tf_op jit(solution)/shard_map/all_to_all | solution.py:266
  124.7 2.6 %time.1 = (f32[8,8,128]{2,1,0:T(8,128)}, f32[512,64]{1,0:T(8,128)}) custom-call(f32[16,16,128]{2,1,0:T(8,128)} %all_to_all.44.freq_ref, f32[8,512,128]{2,1,0:T(8,128)} %get-tuple-element.37.part_ref), custom_call_target="tpu_custom_call" | custom-call | tf_op jit(solution)/shard_map/time/pallas_call | solution.py:351
  127.3 11.1 %all_to_all.45.got_ref = f32[8,8,128]{2,1,0:T(8,128)} all-to-all(f32[8,8,128]{2,1,0:T(8,128)} %get-tuple-element.39), channel_id=1, replica_groups=mesh['chan_0'=4,'chan_1'=8,'tm_0'=8,'tm_1'=2] {'chan_1'}, dimensions={0} | all-to-all | bytes 65536 | tf_op jit(solution)/shard_map/all_to_all | solution.py:266
  138.3 1.4 relay_time.1
  139.7 3.2 %all-to-all-start.7 = ((f32[4,8,128]{2,1,0:T(8,128)}), f32[4,8,128]{2,1,0:T(8,128)S(1)}, u32[]{:S(2)}, u32[]{:S(2)}) async-start(f32[4,8,128]{2,1,0:T(8,128)} %relay_time.1), calls=%async_computation.7 | async-start | bytes 32768 | tf_op jit(solution)/shard_map/all_to_all | solution.py:266
  143.0 0.0 copy-done.2
  143.0 0.7 copy.13
  143.7 1.7 %copy.14 = f32[512,64]{0,1:T(8,128)} copy(f32[512,64]{1,0:T(8,128)} %get-tuple-element.44) | data formatting | bytes 262144
  145.4 4.4 %time_inverse.1 = (f32[128,128]{1,0:T(8,128)}, f32[1,128]{1,0:T(1,128)}) custom-call(f32[16,16,128]{2,1,0:T(8,128)} %all_to_all.44.freq_ref, f32[128,128]{1,0:T(8,128)} %get-tuple-element.40.gram_chan_ref), custom_call_target="tpu_custom_call" | custom-call | tf_op jit(solution)/shard_map/time_inverse/pallas_call | solution.py:357
  149.8 0.0 all-to-all-done.7.got_ref
  149.8 0.0 copy-start.4
  149.8 0.6 copy-done.4
  150.4 2.5 %time_admm.1 = f32[8,64]{1,0:T(8,128)} custom-call(f32[4,8,128]{2,1,0:T(8,128)} %copy-done.4, f32[128,128]{1,0:T(8,128)} %get-tuple-element.41.inverse_ref, f32[1,128]{1,0:T(1,128)} %get-tuple-element.42.penalty_ref, f32[8,128]{1,0:T(8,128)} %get-tuple-element.24.time2_ref.start2_ref), custom_call_target="tpu_custom_call" | custom-call | tf_op jit(solution)/shard_map/time_admm/pallas_call | solution.py:365
Async XLA Ops:
  1.6 20.9 %collective-permute-start = (bf16[256,512]{1,0:T(8,128)(2,1)S(1)}, bf16[256,512]{1,0:T(8,128)(2,1)S(1)}, u32[]{:S(2)}, u32[]{:S(2)}) collective-permute-start(bf16[256,512]{1,0:T(8,128)(2,1)S(1)} %slice.3), channel_id=1, source_target_pairs={{1,0},{2,1},{3,2},{4,3},{5,4},{6,5},{7,6},{8,7},{9,8},{10,9},{11,1... | collective-permute-start | bytes 786440 | tf_op jit(solution)/shard_map/ppermute | solution.py:277
  22.5 0.7 copy-start.1
  23.2 6.3 %copy-start.3 = (f32[256,64]{0,1:T(8,128)S(1)}, f32[256,64]{0,1:T(8,128)}, u32[]{:S(2)}) copy-start(f32[256,64]{0,1:T(8,128)} %param.8) | copy-start | bytes 196612
  26.1 11.6 %all-to-all-start = ((f32[16,16,128]{2,1,0:T(8,128)}), f32[16,16,128]{2,1,0:T(8,128)S(1)}, u32[]{:S(2)}, u32[]{:S(2)}) async-start(f32[16,16,128]{2,1,0:T(8,128)} %get-tuple-element.27), calls=%async_computation | async-start | bytes 262144 | tf_op jit(solution)/shard_map/all_to_all | solution.py:266
  37.7 0.6 copy-start
  72.3 70.6 %copy-start.2 = (f32[256,64]{1,0:T(8,128)S(1)}, f32[256,64]{1,0:T(8,128)}, u32[]{:S(2)}) copy-start(f32[256,64]{1,0:T(8,128)} %get-tuple-element.43) | copy-start | bytes 196612
  139.7 10.1 %all-to-all-start.7 = ((f32[4,8,128]{2,1,0:T(8,128)}), f32[4,8,128]{2,1,0:T(8,128)S(1)}, u32[]{:S(2)}, u32[]{:S(2)}) async-start(f32[4,8,128]{2,1,0:T(8,128)} %relay_time.1), calls=%async_computation.7 | async-start | bytes 32768 | tf_op jit(solution)/shard_map/all_to_all | solution.py:266
  149.8 0.6 copy-start.4

commit v2 on v1

v2 whole, which is shorter than its diff:
```python
import numpy as np
import jax
import jax.numpy as jnp
from jax import lax
from jax.experimental import pallas as pl
from jax.experimental.pallas import tpu as pltpu
from jax.sharding import Mesh
from jax.sharding import PartitionSpec as P

FRAME = 1024
HALF = FRAME // 2
BINS = 512
RANK = 64
ITERS = 5
FRAMES_HERE = 8
CHANS_HERE = 256
PACK = 2 * RANK
TM = ("tm_0", "tm_1")
N_TM = 16
N_X = 4
N_Z = 8
SCALE = 1.0 / (3.0 * FRAME / 8.0)
F32 = jnp.float32
BF16 = jnp.bfloat16
HIGH = lax.Precision.HIGHEST


def half_tables():
    n = np.arange(HALF)[None, :]
    j = np.arange(BINS // 2)[:, None]
    even = 2.0 * np.pi * ((n * (2 * j)) % FRAME) / FRAME
    odd = 2.0 * np.pi * ((n * (2 * j + 1)) % FRAME) / FRAME
    stack = lambda a: np.concatenate([np.cos(a), np.sin(a)], axis=0)
    return stack(even).astype(BF16), stack(odd).astype(BF16)


def window_row():
    n = np.arange(HALF)[None, :]
    return (0.5 - 0.5 * np.cos(2.0 * np.pi * n / FRAME)).astype(np.float32)


def lane_is_low(shape):
    return lax.broadcasted_iota(jnp.int32, shape, 1) < RANK


def both_halves(x):
    other = pltpu.roll(x, RANK, 1)
    low = lane_is_low(x.shape)
    return jnp.concatenate([jnp.where(low, x, other), jnp.where(low, other, x)], axis=0)


def side_by_side(x):
    m = x.shape[0] // 2
    return jnp.where(lane_is_low((m, PACK)), x[:m], x[m:])


def split(x):
    high = x.astype(BF16)
    return high, (x - high.astype(F32)).astype(BF16)


def high_low(x):
    high = x.astype(BF16).astype(F32)
    return jnp.where(lane_is_low(x.shape), high, x - high).astype(BF16)


def doubled(x):
    return jnp.concatenate([x, x], axis=1)


def times(left, right):
    a, b = split(left)
    c, d = split(right)
    both = jnp.concatenate([c, d], axis=1)
    out = jnp.dot(jnp.concatenate([a, b], axis=1), jnp.concatenate([both, both], axis=0),
                  preferred_element_type=F32)
    return out[:, :PACK] + out[:, PACK:]


def times_small(left, right):
    c, d = split(right)
    both = jnp.concatenate([c, d], axis=1)
    out = jnp.dot(high_low(left), jnp.concatenate([both, both], axis=0),
                  preferred_element_type=F32)
    return out[:, :PACK] + out[:, PACK:]


def gram_of(x):
    return times(x.T[:RANK], x)


def inverse_of(gram):
    row = lax.broadcasted_iota(jnp.int32, gram.shape, 0)
    col = lax.broadcasted_iota(jnp.int32, gram.shape, 1)
    eye = jnp.where((row == col) | (row + RANK == col), 1.0, 0.0).astype(F32)
    penalty = jnp.sum(gram * eye) / PACK
    a = gram * (1.0 / penalty) + eye
    mid = RANK / 2.0 + 1.0
    spread = (RANK / 2.0) / mid
    x = eye * (1.0 / mid)
    s = a * (1.0 / mid)
    for step in range(5):
        factor = (2.0 * eye - s) * (1.0 / (1.0 - spread * spread / 2.0))
        spread = (spread * spread / 2.0) / (1.0 - spread * spread / 2.0)
        if step == 0:
            s, x = times_small(s, factor), factor * (1.0 / mid)
        elif step < 4:
            both = times_small(jnp.concatenate([s, x], axis=0), factor)
            s, x = both[:RANK], both[RANK:]
        else:
            x = times_small(x, factor)
    s = times_small(a, x)
    x = times_small(x, 2.0 * eye - s)
    low = lane_is_low(x.shape)
    return penalty, jnp.concatenate([jnp.where(low, x, 0.0), jnp.where(low, 0.0, x)], axis=0)


def admm(product, previous, penalty, inverse):
    scaled = product * (1.0 / penalty)
    carried = previous
    dual = jnp.zeros_like(previous)
    value = previous
    for _ in range(ITERS):
        target = times(scaled + carried, inverse)
        value = target - dual
        dual = jnp.maximum(-value, 0.0)
        carried = jnp.abs(value)
    return jnp.maximum(value, 0.0)


def stacked(x):
    m = x.shape[1] // 2
    return jnp.concatenate([x[:, :m], x[:, m:]], axis=0)


def start_kernel(freq_ref, chan_ref, gram_ref, freq_packed_ref, chan_packed_ref, natural):
    half = BINS // 2
    natural[...] = doubled(freq_ref[...].T)
    even = natural[pl.ds(0, half, stride=2), :]
    odd = natural[pl.ds(1, half, stride=2), :]
    freq_packed_ref[...] = jnp.where(lane_is_low(even.shape), even, odd)
    gram_ref[...] = gram_of(natural[...])
    chan_packed_ref[...] = stacked(chan_ref[...]).T


def frame_power(first, second, window, even_ref, odd_ref):
    first = first.astype(F32) * window
    second = second.astype(F32)
    second = second - second * window
    total = (first + second).astype(BF16)
    change = (first - second).astype(BF16)
    dims = (((1,), (1,)), ((), ()))
    half = BINS // 2
    out = []
    for table, side in ((even_ref, total), (odd_ref, change)):
        wave = lax.dot_general(table[...], side, dims, preferred_element_type=F32)
        out.append((wave[:half] * wave[:half] + wave[half:] * wave[half:]).astype(BF16))
    return jnp.concatenate(out, axis=0)


def chan_term(rows_ref, power, time_row):
    q = jnp.dot(rows_ref[...], power, preferred_element_type=F32)
    row = lax.broadcasted_iota(jnp.int32, (PACK, PACK), 0)
    col = lax.broadcasted_iota(jnp.int32, (PACK, PACK), 1)
    column = jnp.sum(jnp.where(row == col, time_row, 0.0), axis=1, keepdims=True)
    return q * column


EARLY = FRAMES_HERE - 1


def early_kernel(first_ref, second_ref, freq_ref, time_ref, window_ref, even_ref, odd_ref,
                 power_ref, sum_ref, rows_ref, time2_ref, natural):
    t = pl.program_id(0)

    @pl.when(t == 0)
    def _():
        half = BINS // 2
        time2_ref[...] = doubled(time_ref[...])
        natural[...] = doubled(freq_ref[...].T)
        even = natural[pl.ds(0, half, stride=2), :]
        odd = natural[pl.ds(1, half, stride=2), :]
        rows = high_low(jnp.concatenate([even, odd], axis=0))
        rows_ref[...] = rows.astype(F32).T.astype(BF16)
        sum_ref[...] = jnp.zeros_like(sum_ref)

    power = frame_power(first_ref[...], second_ref[...], window_ref[...], even_ref, odd_ref)
    power_ref[0] = power
    sum_ref[...] += chan_term(rows_ref, power, time2_ref[pl.ds(t, 1), :])


def last_kernel(halo_ref, rows_ref, time2_ref, sum_ref, samples_ref, even_in, odd_in, window_ref,
                power_ref, send_ref, held, even_ref, odd_ref, half_sem, even_sem, odd_sem):
    load = pltpu.make_async_copy(samples_ref.at[:, EARLY * HALF:], held, half_sem)
    even_load = pltpu.make_async_copy(even_in, even_ref, even_sem)
    odd_load = pltpu.make_async_copy(odd_in, odd_ref, odd_sem)
    load.start()
    even_load.start()
    odd_load.start()
    load.wait()
    even_load.wait()
    odd_load.wait()
    power = frame_power(held[...], halo_ref[...], window_ref[...], even_ref, odd_ref)
    power_ref[...] = power
    total = sum_ref[...] + chan_term(rows_ref, power, time2_ref[EARLY:, :])
    packed = stacked(total[:RANK] + total[RANK:]).T
    per = CHANS_HERE // 2 // N_TM
    for d in range(N_TM):
        send_ref[d, :per] = packed[d * per:(d + 1) * per]
        send_ref[d, per:] = time2_ref[...]


def chan_kernel(got_ref, gram_freq_ref, start_ref, send_ref, gram_time_ref):
    me = lax.axis_index(TM)
    per = CHANS_HERE // 2 // N_TM
    total = jnp.sum(got_ref[:, :per], axis=0)
    gram_time = gram_of(got_ref[:, per:].reshape(N_TM * FRAMES_HERE, PACK))
    gram_time_ref[...] = gram_time
    penalty, inverse = inverse_of(gram_time * gram_freq_ref[...])
    start = start_ref[pl.ds(pl.multiple_of(me * per, per), per), :]
    new = admm(total * SCALE, start, penalty, inverse)
    send_ref[...] = jnp.broadcast_to(new[None], send_ref.shape)


FIRST_PART = 3


def freq_kernel(chan_ref, time2_ref, last_ref, early_ref, part_ref, send_ref, sides, held, sems):
    loads = [pltpu.make_async_copy(early_ref.at[t], held.at[t], sems.at[t])
             for t in range(EARLY)]
    for load in loads:
        load.start()
    sides[...] = high_low(both_halves(chan_ref[...].reshape(CHANS_HERE // 2, PACK)))
    part_ref[EARLY] = jnp.dot(last_ref[...], sides[...], preferred_element_type=F32)
    for low, high in ((0, FIRST_PART), (FIRST_PART, EARLY)):
        for t in range(low, high):
            loads[t].wait()
        for t in range(low, high):
            part_ref[t] = jnp.dot(held[t], sides[...], preferred_element_type=F32)
    for d in range(N_TM):
        sums = []
        for at in (d * 16, BINS // 2 + d * 16):
            whole = part_ref[0, at:at + 16] * time2_ref[0:1, :]
            for t in range(1, FRAMES_HERE):
                whole = whole + part_ref[t, at:at + 16] * time2_ref[t:t + 1, :]
            sums.append(whole + pltpu.roll(whole, RANK, 1))
        send_ref[d] = jnp.where(lane_is_low((16, PACK)), *sums)


def chan_out_kernel(chan_ref, gram_ref, chan_out_ref):
    packed = chan_ref[...].reshape(CHANS_HERE // 2, PACK)
    gram_ref[...] = side_by_side(gram_of(both_halves(packed)))
    turned = packed.T
    chan_out_ref[...] = jnp.concatenate([turned[:RANK], turned[RANK:]], axis=1)


def spread_kernel(got_ref, gram_ref, send_ref):
    rows = got_ref.shape[1]
    total = jnp.sum(got_ref[...], axis=0)
    for d in range(send_ref.shape[0]):
        send_ref[d, :rows] = total
        send_ref[d, rows:] = gram_ref[...]


def relay_kernel(got_ref, send_ref):
    send_ref[...] = jnp.broadcast_to(jnp.sum(got_ref[...], axis=0)[None], send_ref.shape)


def freq_admm_kernel(got_ref, gram_time_ref, start_ref, send_ref, gram_chan_ref):
    me = lax.axis_index(TM)
    total = jnp.sum(got_ref[...], axis=0)
    per = BINS // 2 // N_TM
    gram = both_halves(total[per:])
    gram_chan_ref[...] = gram
    penalty, inverse = inverse_of(gram * gram_time_ref[...])
    start = start_ref[pl.ds(pl.multiple_of(me * per, per), per), :]
    new = admm(total[:per] * SCALE, start, penalty, inverse)
    send_ref[...] = jnp.broadcast_to(new[None], send_ref.shape)


def time_kernel(freq_ref, part_ref, send_ref):
    rows = both_halves(freq_ref[...].reshape(BINS // 2, PACK))
    sums = [jnp.sum(part_ref[t] * rows, axis=0, keepdims=True) for t in range(FRAMES_HERE)]
    product = jnp.concatenate(sums, axis=0)
    send_ref[...] = jnp.broadcast_to(product[None], send_ref.shape)


def freq_out_kernel(freq_ref, gram_chan_ref, inverse_ref, penalty_ref, freq_out_ref, natural):
    half = BINS // 2
    rows = both_halves(freq_ref[...].reshape(half, PACK))
    natural[pl.ds(0, half, stride=2), :] = rows[:half]
    natural[pl.ds(1, half, stride=2), :] = rows[half:]
    freq_out_ref[...] = natural[...].T[:RANK]
    penalty, inverse = inverse_of(gram_of(rows) * gram_chan_ref[...])
    inverse_ref[...] = inverse
    penalty_ref[...] = jnp.full(penalty_ref.shape, penalty, F32)


def time_admm_kernel(got_ref, inverse_ref, penalty_ref, start2_ref, out_ref):
    total = jnp.sum(got_ref[...], axis=0)
    total = total + pltpu.roll(total, RANK, 1)
    new = admm(total * SCALE, start2_ref[...], penalty_ref[...], inverse_ref[...])
    out_ref[...] = new[:, :RANK]


def shape(*dims, dtype=F32):
    return jax.ShapeDtypeStruct(dims, dtype)


def exchanged(parts, axis):
    return lax.all_to_all(parts, axis, split_axis=0, concat_axis=0, tiled=True)


NEAR = pl.BlockSpec(memory_space=pltpu.VMEM)


def near_call(body, name, outs, args, scratch=(), far=(), outside=(), flops=0, others=(),
              kinds_of_others=()):
    def kind(i, o):
        if i in far:
            return o
        return (pltpu.HBM if i in outside else pltpu.VMEM)(o.shape, o.dtype)

    args = [pltpu.with_memory_space_constraint(a, pltpu.VMEM) for a in args]
    args += [pltpu.with_memory_space_constraint(a, pltpu.HBM) for a in others]
    size = sum(a.size * a.dtype.itemsize for a in list(args) + list(outs))
    away = pl.BlockSpec(memory_space=pltpu.HBM)
    return pl.pallas_call(
        body,
        in_specs=[NEAR] * (len(args) - len(others)) + list(kinds_of_others),
        out_specs=tuple(away if i in outside else NEAR for i in range(len(outs))),
        out_shape=tuple(kind(i, o) for i, o in enumerate(outs)),
        scratch_shapes=list(scratch),
        compiler_params=pltpu.CompilerParams(vmem_limit_bytes=32 * 1024 * 1024),
        cost_estimate=pl.CostEstimate(flops=flops, bytes_accessed=size, transcendentals=0),
        name=name,
    )(*args)


def local(samples, start_chan, start_freq, start_time):
    even_table, odd_table = (jnp.asarray(t) for t in half_tables())
    window = jnp.asarray(window_row())
    route = [(i, i - 1) for i in range(1, N_TM)]
    following = lax.ppermute(samples[:, :HALF], TM, route)
    natural = [pltpu.VMEM((BINS, PACK), F32)]
    table = pltpu.VMEM((BINS, HALF), BF16)
    flag = pltpu.SemaphoreType.DMA
    outside = pl.BlockSpec(memory_space=pltpu.HBM)

    def fixed(*dims):
        return pl.BlockSpec(dims, lambda t: (0,) * len(dims))

    power, early_sum, freq_rows, time2 = pl.pallas_call(
        early_kernel,
        grid=(EARLY,),
        in_specs=[pl.BlockSpec((CHANS_HERE, HALF), lambda t: (0, t)),
                  pl.BlockSpec((CHANS_HERE, HALF), lambda t: (0, t + 1)),
                  fixed(RANK, BINS), fixed(FRAMES_HERE, RANK), fixed(1, HALF),
                  fixed(BINS, HALF), fixed(BINS, HALF)],
        out_specs=[pl.BlockSpec((1, BINS, CHANS_HERE), lambda t: (t, 0, 0)),
                   fixed(PACK, CHANS_HERE), fixed(PACK, BINS), fixed(FRAMES_HERE, PACK)],
        out_shape=(shape(EARLY, BINS, CHANS_HERE, dtype=BF16), shape(PACK, CHANS_HERE),
                   shape(PACK, BINS, dtype=BF16), shape(FRAMES_HERE, PACK)),
        scratch_shapes=natural,
        cost_estimate=pl.CostEstimate(flops=2500000000, bytes_accessed=8000000,
                                      transcendentals=0),
        name="early",
    )(samples, samples, start_freq.T, start_time, window, even_table, odd_table)
    power_last, to_chan = near_call(
        last_kernel, "last", (shape(BINS, CHANS_HERE, dtype=BF16), shape(N_TM, 16, PACK)),
        (following,),
        [pltpu.VMEM((CHANS_HERE, HALF), BF16), table, table, flag(()), flag(()), flag(())],
        far=(1,),
        others=(freq_rows, time2, early_sum, samples, even_table, odd_table, window),
        kinds_of_others=[NEAR] * 3 + [outside] * 3 + [NEAR])

    got = exchanged(to_chan, TM)
    gram_freq, freq_packed, chan_packed = near_call(
        start_kernel, "start",
        (shape(RANK, PACK), shape(BINS // 2, PACK), shape(CHANS_HERE // 2, PACK)),
        (start_freq.T, start_chan.T), natural)
    chan_rows, gram_time = near_call(
        chan_kernel, "chan", (shape(N_TM, 8, PACK), shape(RANK, PACK)),
        (got, gram_freq, chan_packed))
    chan_all = exchanged(chan_rows, TM)

    part, to_freq = near_call(
        freq_kernel, "freq", (shape(FRAMES_HERE, BINS, PACK), shape(N_TM, 16, PACK)),
        (chan_all, time2, power_last),
        [pltpu.VMEM((CHANS_HERE, PACK), BF16), pltpu.VMEM((EARLY, BINS, CHANS_HERE), BF16),
         flag((EARLY,))], far=(1,), others=(power,), kinds_of_others=[outside])
    got = exchanged(to_freq, TM)
    gram_part, chan_out = near_call(
        chan_out_kernel, "chan_out", (shape(RANK // 2, PACK), shape(RANK, CHANS_HERE)),
        (chan_all,), far=(1,))

    rows = 16 + RANK // 2
    (to_z,) = near_call(spread_kernel, "spread", (shape(N_Z, rows, PACK),), (got, gram_part))
    got = exchanged(to_z, "chan_1")
    (to_x,) = near_call(relay_kernel, "relay", (shape(N_X, rows, PACK),), (got,))
    got = exchanged(to_x, "chan_0")
    freq_rows_new, gram_chan = near_call(
        freq_admm_kernel, "freq_admm", (shape(N_TM, 16, PACK), shape(RANK, PACK)),
        (got, gram_time, freq_packed))
    freq_all = exchanged(freq_rows_new, TM)

    (to_z,) = near_call(time_kernel, "time", (shape(N_Z, FRAMES_HERE, PACK),), (freq_all, part),
                        far=(0,))
    got = exchanged(to_z, "chan_1")
    inverse, penalty, freq_out = near_call(
        freq_out_kernel, "freq_out",
        (shape(PACK, PACK), shape(1, PACK), shape(RANK, BINS)), (freq_all, gram_chan),
        natural, far=(2,))
    (to_x,) = near_call(relay_kernel, "relay_time", (shape(N_X, FRAMES_HERE, PACK),), (got,),
                        far=(0,))
    got = exchanged(to_x, "chan_0")
    (factor_time,) = near_call(time_admm_kernel, "time_admm", (shape(FRAMES_HERE, RANK),),
                               (got, inverse, penalty, time2), far=(0,))
    return chan_out.T, freq_out.T, factor_time


def solution(mesh):
    finer = Mesh(mesh.devices.reshape(4, 8, 8, 2), ("chan_0", "chan_1", "tm_0", "tm_1"))
    chan = ("chan_0", "chan_1")
    return jax.shard_map(
        local,
        mesh=finer,
        in_specs=(P(chan, TM), P(chan, None), P(), P(TM, None)),
        out_specs=(P(chan, None), P(), P(TM, None)),
        check_vma=False,
    )
```

time: 154 us -> 126 us (0.82)
  blocking collectives: 80.1 us -> 61.8 us
  Pallas kernels: 41.5 us -> 24.3 us
  waiting for transfers between devices: 7.45 us -> 18.1 us
  local copies, waits for them, and re-layouts: 7.82 us -> 0.99 us
  starting transfers between devices: 15.4 us -> 18.8 us
    all_to_all x6 -> x5, blocking collectives: 80.1 us -> 61.8 us  [exchanged(): return lax.all_to_all(parts, axis, split_axis=0, concat_axis=0, tiled=True)]
    pallas_call x12 -> x13, Pallas kernels: 41.5 us -> 24.3 us  [the longest x12 16.1 us: near_call(): pl.pallas_call(body, in_specs=[NEAR] * (len(args) - len(others)) + list(k...]
    all_to_all x2 -> x3, waiting for transfers between devices: 7.45 us -> 18.1 us  [exchanged(): return lax.all_to_all(parts, axis, split_axis=0, concat_axis=0, tiled=True)]
    unnamed x14 -> x6, local copies, waits for them, and re-layouts: 6.85 us -> 0.02 us
    all_to_all x2 -> x3, starting transfers between devices: 6.64 us -> 10.1 us  [exchanged(): return lax.all_to_all(parts, axis, split_axis=0, concat_axis=0, tiled=True)]
  transfers between devices with their start and end apart: 3 -> 4, of which waited for: 1 -> 3; matrix products, arithmetic and copies ran while one was open for 3% -> 0% of each run, Pallas kernels for 10% -> 9%
where the time goes in v2:
time: 126 us; the launch traced here: 125 us
  blocking collectives  61.8 us (49%)
  Pallas kernels  24.3 us (19%)
  starting transfers between devices  18.8 us (15%)
  waiting for transfers between devices  18.1 us (14%)
    all_to_all x5, blocking collectives, exchanged(): return lax.all_to_all(parts, axis, split_axis=0, concat_axis=0, tiled=True)  61.8 us
    all_to_all x3, waiting for transfers between devices, exchanged(): return lax.all_to_all(parts, axis, split_axis=0, concat_axis=0, tiled=True)  18.1 us
    pallas_call x12, Pallas kernels, near_call(): pl.pallas_call(body, in_specs=[NEAR] * (len(args) - len(others)) + list(k...  16.1 us
    all_to_all x3, starting transfers between devices, exchanged(): return lax.all_to_all(parts, axis, split_axis=0, concat_axis=0, tiled=True)  10.1 us
    ppermute x1, starting transfers between devices, local(): following = lax.ppermute(samples[:, :HALF], TM, route)  8.75 us
    pallas_call x1, Pallas kernels, local(): pl.pallas_call(early_kernel, grid=(EARLY,), in_specs=[pl.BlockSpec((CHANS...  8.29 us
  transfers between devices with their start and end apart: 4, of which 3 were waited for; matrix products, arithmetic and copies ran while one was open for 0% of the time, Pallas kernels for 9%

profile of v2, /device:TPU:1, one launch (start us, length us, event | category | flops | bytes accessed | tf_op | source)
XLA Modules:
  0.0 124.9 jit_solution(14795318086751277164)
XLA Ops:
  0.6 1.0 slice.3
  1.6 8.7 %collective-permute-start = (bf16[256,512]{1,0:T(8,128)(2,1)S(1)}, bf16[256,512]{1,0:T(8,128)(2,1)S(1)}, u32[]{:S(2)}, u32[]{:S(2)}) collective-permute-start(bf16[256,512]{1,0:T(8,128)(2,1)S(1)} %slice.3), channel_id=1, source_target_pairs={{1,0},{2,1},{3,2},{4,3},{5,4},{6,5},{7,6},{8,7},{9,8},{10,9},{11,1... | collective-permute-start | bytes 786440 | tf_op jit(solution)/shard_map/ppermute | solution.py:344
  10.4 8.3 %early.1 = (bf16[7,512,256]{2,1,0:T(8,128)(2,1)}, f32[128,256]{1,0:T(8,128)}, bf16[128,512]{1,0:T(8,128)(2,1)}, f32[8,128]{1,0:T(8,128)}) custom-call(bf16[256,4096]{1,0:T(8,128)(2,1)} %samples_ref.1, bf16[256,4096]{1,0:T(8,128)(2,1)} %samples_ref.1, f32[64,512]{1,0:T(8,128)} %bitcast.4, f32[8,64]{1,0:T(8,128)} %time_ref.1, ...), custom_call_target="tpu_custom_call" | custom-call | flops 2500000000 | bytes 8000000 | tf_op jit(solution)/shard_map/early/pallas_call | solution.py:353
  18.6 0.0 copy-start
  18.7 0.0 copy-start.1
  18.7 0.0 collective-permute-done.halo_ref
  18.7 0.0 copy-start.2
  18.7 3.7 %last.1 = (bf16[512,256]{1,0:T(8,128)(2,1)S(1)}, f32[16,16,128]{2,1,0:T(8,128)}) custom-call(bf16[256,512]{1,0:T(8,128)(2,1)S(1)} %collective-permute-done.halo_ref, bf16[128,512]{1,0:T(8,128)(2,1)} %get-tuple-element.23.rows_ref, f32[8,128]{1,0:T(8,128)} %get-tuple-element.24.time2_ref.start2_ref, f32[128,256]{1,0:T(8,128)} %get-tuple-element.25.sum_ref, ...), custom_call_target="tpu_custom_call" | custom-call | bytes 4069376 | tf_op jit(solution)/shard_map/last/pallas_call | solution.py:328
  22.4 3.4 %all-to-all-start = ((f32[16,16,128]{2,1,0:T(8,128)}), f32[16,16,128]{2,1,0:T(8,128)S(1)}, u32[]{:S(2)}, u32[]{:S(2)}) async-start(f32[16,16,128]{2,1,0:T(8,128)} %get-tuple-element.26), calls=%async_computation | async-start | bytes 262144 | tf_op jit(solution)/shard_map/all_to_all | solution.py:311
  25.9 0.0 copy-done
  25.9 0.0 copy-done.1
  25.9 0.5 start.1
  26.3 7.7 %all-to-all-done.got_ref = f32[16,16,128]{2,1,0:T(8,128)S(1)} async-done(((f32[16,16,128]{2,1,0:T(8,128)}), f32[16,16,128]{2,1,0:T(8,128)S(1)}, u32[]{:S(2)}, u32[]{:S(2)}) %all-to-all-start) | async-done | bytes 131104 | tf_op jit(solution)/shard_map/all_to_all | solution.py:311
  34.1 2.0 %chan.1 = (f32[16,8,128]{2,1,0:T(8,128)S(1)}, f32[64,128]{1,0:T(8,128)S(1)}) custom-call(f32[16,16,128]{2,1,0:T(8,128)S(1)} %all-to-all-done.got_ref, f32[64,128]{1,0:T(8,128)S(1)} %get-tuple-element.27.gram_freq_ref, f32[128,128]{1,0:T(8,128)S(1)} %get-tuple-element.28.start_ref), custom_call_target="tpu_custom_call" | custom-call | bytes 327680 | tf_op jit(solution)/shard_map/chan/pallas_call | solution.py:328
  36.1 10.4 %all_to_all.40.chan_ref = f32[16,8,128]{2,1,0:T(8,128)S(1)} all-to-all(f32[16,8,128]{2,1,0:T(8,128)S(1)} %get-tuple-element.29), channel_id=1, replica_groups=mesh['chan_0'=4,'chan_1'=8,'tm_0'=8,'tm_1'=2] {'tm_0','tm_1'}, dimensions={0} | all-to-all | bytes 131072 | tf_op jit(solution)/shard_map/all_to_all | solution.py:311
  46.5 0.0 copy-done.2
  46.5 2.8 %freq.1 = (f32[8,512,128]{2,1,0:T(8,128)S(1)}, f32[16,16,128]{2,1,0:T(8,128)}) custom-call(f32[16,8,128]{2,1,0:T(8,128)S(1)} %all_to_all.40.chan_ref, f32[8,128]{1,0:T(8,128)S(1)} %copy-done.2, bf16[512,256]{1,0:T(8,128)(2,1)S(1)} %get-tuple-element.31.last_ref, bf16[7,512,256]{2,1,0:T(8,128)(2,1)} %get-tuple-element.32.early_ref), custom_call_target="tpu_custom_call" | custom-call | bytes 4395008 | tf_op jit(solution)/shard_map/freq/pallas_call | solution.py:328
  49.3 3.4 %all-to-all-start.2 = ((f32[16,16,128]{2,1,0:T(8,128)}), f32[16,16,128]{2,1,0:T(8,128)S(1)}, u32[]{:S(2)}, u32[]{:S(2)}) async-start(f32[16,16,128]{2,1,0:T(8,128)} %get-tuple-element.33), calls=%async_computation.2 | async-start | bytes 262144 | tf_op jit(solution)/shard_map/all_to_all | solution.py:311
  52.8 0.8 chan_out.1
  53.6 8.4 %all-to-all-done.2.got_ref = f32[16,16,128]{2,1,0:T(8,128)S(1)} async-done(((f32[16,16,128]{2,1,0:T(8,128)}), f32[16,16,128]{2,1,0:T(8,128)S(1)}, u32[]{:S(2)}, u32[]{:S(2)}) %all-to-all-start.2) | async-done | bytes 131104 | tf_op jit(solution)/shard_map/all_to_all | solution.py:311
  62.0 20.0 %all_to_all.41.got_ref = f32[8,48,128]{2,1,0:T(8,128)S(1)} all-to-all(f32[8,48,128]{2,1,0:T(8,128)S(1)} %spread.1), channel_id=1, replica_groups=mesh['chan_0'=4,'chan_1'=8,'tm_0'=8,'tm_1'=2] {'chan_1'}, dimensions={0} | all-to-all | bytes 393216 | tf_op jit(solution)/shard_map/all_to_all | solution.py:311
  82.0 8.5 %all_to_all.42.got_ref = f32[4,48,128]{2,1,0:T(8,128)S(1)} all-to-all(f32[4,48,128]{2,1,0:T(8,128)S(1)} %relay.1), channel_id=1, replica_groups=mesh['chan_0'=4,'chan_1'=8,'tm_0'=8,'tm_1'=2] {'chan_0'}, dimensions={0} | all-to-all | bytes 196608 | tf_op jit(solution)/shard_map/all_to_all | solution.py:311
  90.5 1.9 %freq_admm.1 = (f32[16,16,128]{2,1,0:T(8,128)S(1)}, f32[64,128]{1,0:T(8,128)S(1)}) custom-call(f32[4,48,128]{2,1,0:T(8,128)S(1)} %all_to_all.42.got_ref, f32[64,128]{1,0:T(8,128)S(1)} %get-tuple-element.35.gram_time_ref, f32[256,128]{1,0:T(8,128)S(1)} %get-tuple-element.36.start_ref), custom_call_target="tpu_custom_call" | custom-call | bytes 425984 | tf_op jit(solution)/shard_map/freq_admm/pallas_call | solution.py:328
  92.4 13.5 %all_to_all.43.freq_ref = f32[16,16,128]{2,1,0:T(8,128)S(1)} all-to-all(f32[16,16,128]{2,1,0:T(8,128)S(1)} %get-tuple-element.37), channel_id=1, replica_groups=mesh['chan_0'=4,'chan_1'=8,'tm_0'=8,'tm_1'=2] {'tm_0','tm_1'}, dimensions={0} | all-to-all | bytes 262144 | tf_op jit(solution)/shard_map/all_to_all | solution.py:311
  105.8 0.2 time.1
  106.1 9.5 %all_to_all.44.got_ref = f32[8,8,128]{2,1,0:T(8,128)S(1)} all-to-all(f32[8,8,128]{2,1,0:T(8,128)S(1)} %time.1), channel_id=1, replica_groups=mesh['chan_0'=4,'chan_1'=8,'tm_0'=8,'tm_1'=2] {'chan_1'}, dimensions={0} | all-to-all | bytes 65536 | tf_op jit(solution)/shard_map/all_to_all | solution.py:311
  115.6 0.6 relay_time.1
  116.2 3.2 %all-to-all-start.7 = ((f32[4,8,128]{2,1,0:T(8,128)}), f32[4,8,128]{2,1,0:T(8,128)S(1)}, u32[]{:S(2)}, u32[]{:S(2)}) async-start(f32[4,8,128]{2,1,0:T(8,128)} %relay_time.1), calls=%async_computation.7 | async-start | bytes 32768 | tf_op jit(solution)/shard_map/all_to_all | solution.py:311
  119.4 2.1 %freq_out.1 = (f32[128,128]{1,0:T(8,128)S(1)}, f32[1,128]{1,0:T(1,128)S(1)}, f32[64,512]{1,0:T(8,128)}) custom-call(f32[16,16,128]{2,1,0:T(8,128)S(1)} %all_to_all.43.freq_ref, f32[64,128]{1,0:T(8,128)S(1)} %get-tuple-element.38.gram_chan_ref), custom_call_target="tpu_custom_call" | custom-call | bytes 360960 | tf_op jit(solution)/shard_map/freq_out/pallas_call | solution.py:328
  121.6 2.1 %all-to-all-done.7.got_ref = f32[4,8,128]{2,1,0:T(8,128)S(1)} async-done(((f32[4,8,128]{2,1,0:T(8,128)}), f32[4,8,128]{2,1,0:T(8,128)S(1)}, u32[]{:S(2)}, u32[]{:S(2)}) %all-to-all-start.7) | async-done | bytes 16416 | tf_op jit(solution)/shard_map/all_to_all | solution.py:311
  123.6 1.3 %time_admm.1 = f32[8,64]{1,0:T(8,128)} custom-call(f32[4,8,128]{2,1,0:T(8,128)S(1)} %all-to-all-done.7.got_ref, f32[128,128]{1,0:T(8,128)S(1)} %get-tuple-element.41.inverse_ref, f32[1,128]{1,0:T(1,128)S(1)} %get-tuple-element.42.penalty_ref, f32[8,128]{1,0:T(8,128)S(1)} %copy-done.2), custom_call_target="tpu_custom_call" | custom-call | bytes 88576 | tf_op jit(solution)/shard_map/time_admm/pallas_call | solution.py:328
  (2 shorter events, 0.0 us)
Async XLA Ops:
  1.6 17.1 %collective-permute-start = (bf16[256,512]{1,0:T(8,128)(2,1)S(1)}, bf16[256,512]{1,0:T(8,128)(2,1)S(1)}, u32[]{:S(2)}, u32[]{:S(2)}) collective-permute-start(bf16[256,512]{1,0:T(8,128)(2,1)S(1)} %slice.3), channel_id=1, source_target_pairs={{1,0},{2,1},{3,2},{4,3},{5,4},{6,5},{7,6},{8,7},{9,8},{10,9},{11,1... | collective-permute-start | bytes 786440 | tf_op jit(solution)/shard_map/ppermute | solution.py:344
  18.6 7.2 %copy-start = (f32[512,64]{0,1:T(8,128)S(1)}, f32[512,64]{0,1:T(8,128)}, u32[]{:S(2)}) copy-start(f32[512,64]{0,1:T(8,128)} %param.9) | copy-start | bytes 393220
  18.7 7.2 %copy-start.1 = (f32[256,64]{0,1:T(8,128)S(1)}, f32[256,64]{0,1:T(8,128)}, u32[]{:S(2)}) copy-start(f32[256,64]{0,1:T(8,128)} %param.8) | copy-start | bytes 196612
  18.7 27.9 %copy-start.2 = (f32[8,128]{1,0:T(8,128)S(1)}, f32[8,128]{1,0:T(8,128)}, u32[]{:S(2)}) copy-start(f32[8,128]{1,0:T(8,128)} %get-tuple-element.24.time2_ref.start2_ref) | copy-start | bytes 12292
  22.4 11.6 %all-to-all-start = ((f32[16,16,128]{2,1,0:T(8,128)}), f32[16,16,128]{2,1,0:T(8,128)S(1)}, u32[]{:S(2)}, u32[]{:S(2)}) async-start(f32[16,16,128]{2,1,0:T(8,128)} %get-tuple-element.26), calls=%async_computation | async-start | bytes 262144 | tf_op jit(solution)/shard_map/all_to_all | solution.py:311
  49.3 12.6 %all-to-all-start.2 = ((f32[16,16,128]{2,1,0:T(8,128)}), f32[16,16,128]{2,1,0:T(8,128)S(1)}, u32[]{:S(2)}, u32[]{:S(2)}) async-start(f32[16,16,128]{2,1,0:T(8,128)} %get-tuple-element.33), calls=%async_computation.2 | async-start | bytes 262144 | tf_op jit(solution)/shard_map/all_to_all | solution.py:311
  116.2 7.4 %all-to-all-start.7 = ((f32[4,8,128]{2,1,0:T(8,128)}), f32[4,8,128]{2,1,0:T(8,128)S(1)}, u32[]{:S(2)}, u32[]{:S(2)}) async-start(f32[4,8,128]{2,1,0:T(8,128)} %relay_time.1), calls=%async_computation.7 | async-start | bytes 32768 | tf_op jit(solution)/shard_map/all_to_all | solution.py:311

commit v3 on v2

--- a/solution.py
+++ b/solution.py
@@ -17,8 +17,8 @@
 PACK = 2 * RANK
 TM = ("tm_0", "tm_1")
 N_TM = 16
-N_X = 4
-N_Z = 8
+CHAN = ("chan_0", "chan_1")
+N_CHAN = 32
 SCALE = 1.0 / (3.0 * FRAME / 8.0)
 F32 = jnp.float32
 BF16 = jnp.bfloat16
@@ -255,39 +255,38 @@
 
 
 def spread_kernel(got_ref, gram_ref, send_ref):
+    me = lax.axis_index(TM)
     rows = got_ref.shape[1]
     total = jnp.sum(got_ref[...], axis=0)
+    block = gram_ref[pl.ds(pl.multiple_of(me // (N_TM // 4) * 8, 8), 8), :]
     for d in range(send_ref.shape[0]):
         send_ref[d, :rows] = total
-        send_ref[d, rows:] = gram_ref[...]
+        send_ref[d, rows:] = block
 
 
 def relay_kernel(got_ref, send_ref):
     send_ref[...] = jnp.broadcast_to(jnp.sum(got_ref[...], axis=0)[None], send_ref.shape)
 
 
-def freq_admm_kernel(got_ref, gram_time_ref, start_ref, send_ref, gram_chan_ref):
-    me = lax.axis_index(TM)
-    total = jnp.sum(got_ref[...], axis=0)
-    per = BINS // 2 // N_TM
-    gram = both_halves(total[per:])
+def freq_admm_kernel(got_ref, gram_time_ref, start_ref, part_ref, send_ref, new_ref,
+                     gram_chan_ref):
+    rows = BINS // 2 // N_TM
+    product = got_ref[:, :rows].reshape(BINS // 2, PACK)
+    gram = both_halves(jnp.concatenate(
+        [got_ref[d, rows:] for d in range(0, N_TM, N_TM // 4)], axis=0))
     gram_chan_ref[...] = gram
     penalty, inverse = inverse_of(gram * gram_time_ref[...])
-    start = start_ref[pl.ds(pl.multiple_of(me * per, per), per), :]
-    new = admm(total[:per] * SCALE, start, penalty, inverse)
-    send_ref[...] = jnp.broadcast_to(new[None], send_ref.shape)
-
-
-def time_kernel(freq_ref, part_ref, send_ref):
-    rows = both_halves(freq_ref[...].reshape(BINS // 2, PACK))
-    sums = [jnp.sum(part_ref[t] * rows, axis=0, keepdims=True) for t in range(FRAMES_HERE)]
+    new = admm(product * SCALE, start_ref[...], penalty, inverse)
+    new_ref[...] = new
+    twice = both_halves(new)
+    sums = [jnp.sum(part_ref[t] * twice, axis=0, keepdims=True) for t in range(FRAMES_HERE)]
     product = jnp.concatenate(sums, axis=0)
     send_ref[...] = jnp.broadcast_to(product[None], send_ref.shape)
 
 
 def freq_out_kernel(freq_ref, gram_chan_ref, inverse_ref, penalty_ref, freq_out_ref, natural):
     half = BINS // 2
-    rows = both_halves(freq_ref[...].reshape(half, PACK))
+    rows = both_halves(freq_ref[...])
     natural[pl.ds(0, half, stride=2), :] = rows[:half]
     natural[pl.ds(1, half, stride=2), :] = rows[half:]
     freq_out_ref[...] = natural[...].T[:RANK]
@@ -394,26 +393,20 @@
         chan_out_kernel, "chan_out", (shape(RANK // 2, PACK), shape(RANK, CHANS_HERE)),
         (chan_all,), far=(1,))
 
-    rows = 16 + RANK // 2
-    (to_z,) = near_call(spread_kernel, "spread", (shape(N_Z, rows, PACK),), (got, gram_part))
-    got = exchanged(to_z, "chan_1")
-    (to_x,) = near_call(relay_kernel, "relay", (shape(N_X, rows, PACK),), (got,))
-    got = exchanged(to_x, "chan_0")
-    freq_rows_new, gram_chan = near_call(
-        freq_admm_kernel, "freq_admm", (shape(N_TM, 16, PACK), shape(RANK, PACK)),
-        (got, gram_time, freq_packed))
-    freq_all = exchanged(freq_rows_new, TM)
-
-    (to_z,) = near_call(time_kernel, "time", (shape(N_Z, FRAMES_HERE, PACK),), (freq_all, part),
-                        far=(0,))
-    got = exchanged(to_z, "chan_1")
+    rows = 16 + 8
+    (to_all,) = near_call(spread_kernel, "spread", (shape(N_CHAN, rows, PACK),), (got, gram_part))
+    got = exchanged(to_all, CHAN)
+    (to_tm,) = near_call(relay_kernel, "relay", (shape(N_TM, rows, PACK),), (got,))
+    got = exchanged(to_tm, TM)
+    to_all, freq_all, gram_chan = near_call(
+        freq_admm_kernel, "freq_admm",
+        (shape(N_CHAN, FRAMES_HERE, PACK), shape(BINS // 2, PACK), shape(RANK, PACK)),
+        (got, gram_time, freq_packed, part), far=(0,))
+    got = exchanged(to_all, CHAN)
     inverse, penalty, freq_out = near_call(
         freq_out_kernel, "freq_out",
         (shape(PACK, PACK), shape(1, PACK), shape(RANK, BINS)), (freq_all, gram_chan),
         natural, far=(2,))
-    (to_x,) = near_call(relay_kernel, "relay_time", (shape(N_X, FRAMES_HERE, PACK),), (got,),
-                        far=(0,))
-    got = exchanged(to_x, "chan_0")
     (factor_time,) = near_call(time_admm_kernel, "time_admm", (shape(FRAMES_HERE, RANK),),
                                (got, inverse, penalty, time2), far=(0,))
     return chan_out.T, freq_out.T, factor_time
@@ -421,11 +414,10 @@
 
 def solution(mesh):
     finer = Mesh(mesh.devices.reshape(4, 8, 8, 2), ("chan_0", "chan_1", "tm_0", "tm_1"))
-    chan = ("chan_0", "chan_1")
     return jax.shard_map(
         local,
         mesh=finer,
-        in_specs=(P(chan, TM), P(chan, None), P(), P(TM, None)),
-        out_specs=(P(chan, None), P(), P(TM, None)),
+        in_specs=(P(CHAN, TM), P(CHAN, None), P(), P(TM, None)),
+        out_specs=(P(CHAN, None), P(), P(TM, None)),
         check_vma=False,
     )

time: 126 us -> 121 us (0.960)
  blocking collectives: 61.8 us -> 50 us
  waiting for transfers between devices: 18.1 us -> 23.3 us
  starting transfers between devices: 18.8 us -> 20.9 us
    all_to_all x5 -> x3, blocking collectives: 61.8 us -> 50 us  [exchanged(): return lax.all_to_all(parts, axis, split_axis=0, concat_axis=0, tiled=True)]
    all_to_all x3, waiting for transfers between devices: 18.1 us -> 23.3 us  [exchanged(): return lax.all_to_all(parts, axis, split_axis=0, concat_axis=0, tiled=True)]
    all_to_all x3, starting transfers between devices: 10.1 us -> 12.1 us  [exchanged(): return lax.all_to_all(parts, axis, split_axis=0, concat_axis=0, tiled=True)]
    pallas_call x12 -> x10, Pallas kernels: 16.1 us -> 16.2 us  [near_call(): pl.pallas_call(body, in_specs=[NEAR] * (len(args) - len(others)) + list(k...]
  transfers between devices with their start and end apart: 4 -> 4, of which waited for: 3 -> 3; matrix products, arithmetic and copies ran while one was open for 0% -> 0% of each run, Pallas kernels for 9% -> 10%
where the time goes in v3:
time: 121 us; the launch traced here: 120 us
  blocking collectives  50 us (41%)
  Pallas kernels  24.5 us (20%)
  waiting for transfers between devices  23.3 us (19%)
  starting transfers between devices  20.9 us (17%)
    all_to_all x3, blocking collectives, exchanged(): return lax.all_to_all(parts, axis, split_axis=0, concat_axis=0, tiled=True)  50 us
    all_to_all x3, waiting for transfers between devices, exchanged(): return lax.all_to_all(parts, axis, split_axis=0, concat_axis=0, tiled=True)  23.3 us
    pallas_call x10, Pallas kernels, near_call(): pl.pallas_call(body, in_specs=[NEAR] * (len(args) - len(others)) + list(k...  16.2 us
    all_to_all x3, starting transfers between devices, exchanged(): return lax.all_to_all(parts, axis, split_axis=0, concat_axis=0, tiled=True)  12.1 us
    ppermute x1, starting transfers between devices, local(): following = lax.ppermute(samples[:, :HALF], TM, route)  8.75 us
    pallas_call x1, Pallas kernels, local(): pl.pallas_call(early_kernel, grid=(EARLY,), in_specs=[pl.BlockSpec((CHANS...  8.29 us
  transfers between devices with their start and end apart: 4, of which 3 were waited for; matrix products, arithmetic and copies ran while one was open for 0% of the time, Pallas kernels for 10%

profile of v3, /device:TPU:1, one launch (start us, length us, event | category | flops | bytes accessed | tf_op | source)
XLA Modules:
  0.0 120.3 jit_solution(2739467418239213160)
XLA Ops:
  0.6 1.0 slice.3
  1.6 8.7 %collective-permute-start = (bf16[256,512]{1,0:T(8,128)(2,1)S(1)}, bf16[256,512]{1,0:T(8,128)(2,1)S(1)}, u32[]{:S(2)}, u32[]{:S(2)}) collective-permute-start(bf16[256,512]{1,0:T(8,128)(2,1)S(1)} %slice.3), channel_id=1, source_target_pairs={{1,0},{2,1},{3,2},{4,3},{5,4},{6,5},{7,6},{8,7},{9,8},{10,9},{11,1... | collective-permute-start | bytes 786440 | tf_op jit(solution)/shard_map/ppermute | solution.py:343
  10.4 8.3 %early.1 = (bf16[7,512,256]{2,1,0:T(8,128)(2,1)}, f32[128,256]{1,0:T(8,128)}, bf16[128,512]{1,0:T(8,128)(2,1)}, f32[8,128]{1,0:T(8,128)}) custom-call(bf16[256,4096]{1,0:T(8,128)(2,1)} %samples_ref.1, bf16[256,4096]{1,0:T(8,128)(2,1)} %samples_ref.1, f32[64,512]{1,0:T(8,128)} %bitcast.4, f32[8,64]{1,0:T(8,128)} %time_ref.1, ...), custom_call_target="tpu_custom_call" | custom-call | flops 2500000000 | bytes 8000000 | tf_op jit(solution)/shard_map/early/pallas_call | solution.py:352
  18.6 0.0 copy-start
  18.7 0.0 copy-start.1
  18.7 0.0 collective-permute-done.halo_ref
  18.7 0.0 copy-start.2
  18.7 3.7 %last.1 = (bf16[512,256]{1,0:T(8,128)(2,1)S(1)}, f32[16,16,128]{2,1,0:T(8,128)}) custom-call(bf16[256,512]{1,0:T(8,128)(2,1)S(1)} %collective-permute-done.halo_ref, bf16[128,512]{1,0:T(8,128)(2,1)} %get-tuple-element.24.rows_ref, f32[8,128]{1,0:T(8,128)} %get-tuple-element.25.time2_ref.start2_ref, f32[128,256]{1,0:T(8,128)} %get-tuple-element.26.sum_ref, ...), custom_call_target="tpu_custom_call" | custom-call | bytes 4069376 | tf_op jit(solution)/shard_map/last/pallas_call | solution.py:327
  22.4 3.4 %all-to-all-start = ((f32[16,16,128]{2,1,0:T(8,128)}), f32[16,16,128]{2,1,0:T(8,128)S(1)}, u32[]{:S(2)}, u32[]{:S(2)}) async-start(f32[16,16,128]{2,1,0:T(8,128)} %get-tuple-element.27), calls=%async_computation | async-start | bytes 262144 | tf_op jit(solution)/shard_map/all_to_all | solution.py:310
  25.9 0.0 copy-done
  25.9 0.0 copy-done.1
  25.9 0.5 start.1
  26.3 7.7 %all-to-all-done.got_ref = f32[16,16,128]{2,1,0:T(8,128)S(1)} async-done(((f32[16,16,128]{2,1,0:T(8,128)}), f32[16,16,128]{2,1,0:T(8,128)S(1)}, u32[]{:S(2)}, u32[]{:S(2)}) %all-to-all-start) | async-done | bytes 131104 | tf_op jit(solution)/shard_map/all_to_all | solution.py:310
  34.1 2.0 %chan.1 = (f32[16,8,128]{2,1,0:T(8,128)S(1)}, f32[64,128]{1,0:T(8,128)S(1)}) custom-call(f32[16,16,128]{2,1,0:T(8,128)S(1)} %all-to-all-done.got_ref, f32[64,128]{1,0:T(8,128)S(1)} %get-tuple-element.28.gram_freq_ref, f32[128,128]{1,0:T(8,128)S(1)} %get-tuple-element.29.start_ref), custom_call_target="tpu_custom_call" | custom-call | bytes 327680 | tf_op jit(solution)/shard_map/chan/pallas_call | solution.py:327
  36.1 10.4 %all_to_all.30.chan_ref = f32[16,8,128]{2,1,0:T(8,128)S(1)} all-to-all(f32[16,8,128]{2,1,0:T(8,128)S(1)} %get-tuple-element.30), channel_id=1, replica_groups=mesh['chan_0'=4,'chan_1'=8,'tm_0'=8,'tm_1'=2] {'tm_0','tm_1'}, dimensions={0} | all-to-all | bytes 131072 | tf_op jit(solution)/shard_map/all_to_all | solution.py:310
  46.5 0.0 copy-done.2
  46.5 2.8 %freq.1 = (f32[8,512,128]{2,1,0:T(8,128)S(1)}, f32[16,16,128]{2,1,0:T(8,128)}) custom-call(f32[16,8,128]{2,1,0:T(8,128)S(1)} %all_to_all.30.chan_ref, f32[8,128]{1,0:T(8,128)S(1)} %copy-done.2, bf16[512,256]{1,0:T(8,128)(2,1)S(1)} %get-tuple-element.32.last_ref, bf16[7,512,256]{2,1,0:T(8,128)(2,1)} %get-tuple-element.33.early_ref), custom_call_target="tpu_custom_call" | custom-call | bytes 4395008 | tf_op jit(solution)/shard_map/freq/pallas_call | solution.py:327
  49.3 3.4 %all-to-all-start.2 = ((f32[16,16,128]{2,1,0:T(8,128)}), f32[16,16,128]{2,1,0:T(8,128)S(1)}, u32[]{:S(2)}, u32[]{:S(2)}) async-start(f32[16,16,128]{2,1,0:T(8,128)} %get-tuple-element.34), calls=%async_computation.2 | async-start | bytes 262144 | tf_op jit(solution)/shard_map/all_to_all | solution.py:310
  52.8 0.8 chan_out.1
  53.6 8.4 %all-to-all-done.2.got_ref = f32[16,16,128]{2,1,0:T(8,128)S(1)} async-done(((f32[16,16,128]{2,1,0:T(8,128)}), f32[16,16,128]{2,1,0:T(8,128)S(1)}, u32[]{:S(2)}, u32[]{:S(2)}) %all-to-all-start.2) | async-done | bytes 131104 | tf_op jit(solution)/shard_map/all_to_all | solution.py:310
  62.0 25.0 %all_to_all.31.got_ref = f32[32,24,128]{2,1,0:T(8,128)S(1)} all-to-all(f32[32,24,128]{2,1,0:T(8,128)S(1)} %spread.1), channel_id=1, replica_groups=mesh['chan_0'=4,'chan_1'=8,'tm_0'=8,'tm_1'=2] {'chan_0','chan_1'}, dimensions={0} | all-to-all | bytes 786432 | tf_op jit(solution)/shard_map/all_to_all | solution.py:310
  87.1 14.6 %all_to_all.32.got_ref = f32[16,24,128]{2,1,0:T(8,128)S(1)} all-to-all(f32[16,24,128]{2,1,0:T(8,128)S(1)} %relay.1), channel_id=1, replica_groups=mesh['chan_0'=4,'chan_1'=8,'tm_0'=8,'tm_1'=2] {'tm_0','tm_1'}, dimensions={0} | all-to-all | bytes 393216 | tf_op jit(solution)/shard_map/all_to_all | solution.py:310
  101.6 2.8 %freq_admm.1 = (f32[32,8,128]{2,1,0:T(8,128)}, f32[256,128]{1,0:T(8,128)S(1)}, f32[64,128]{1,0:T(8,128)S(1)}) custom-call(f32[16,24,128]{2,1,0:T(8,128)S(1)} %all_to_all.32.got_ref, f32[64,128]{1,0:T(8,128)S(1)} %get-tuple-element.36.gram_time_ref, f32[256,128]{1,0:T(8,128)S(1)} %get-tuple-element.37.start_ref, f32[8,512,128]{2,1,0:T(8,128)S(1)} %get-tuple-element.38.part_ref), custom_call_target="tpu_custom_call" | custom-call | bytes 2752512 | tf_op jit(solution)/shard_map/freq_admm/pallas_call | solution.py:327
  104.5 5.3 %all-to-all-start.5 = ((f32[32,8,128]{2,1,0:T(8,128)}), f32[32,8,128]{2,1,0:T(8,128)S(1)}, u32[]{:S(2)}, u32[]{:S(2)}) async-start(f32[32,8,128]{2,1,0:T(8,128)} %get-tuple-element.42), calls=%async_computation.5 | async-start | bytes 262144 | tf_op jit(solution)/shard_map/all_to_all | solution.py:310
  109.7 2.1 %freq_out.1 = (f32[128,128]{1,0:T(8,128)S(1)}, f32[1,128]{1,0:T(1,128)S(1)}, f32[64,512]{1,0:T(8,128)}) custom-call(f32[256,128]{1,0:T(8,128)S(1)} %get-tuple-element.39.freq_ref, f32[64,128]{1,0:T(8,128)S(1)} %get-tuple-element.40.gram_chan_ref), custom_call_target="tpu_custom_call" | custom-call | bytes 360960 | tf_op jit(solution)/shard_map/freq_out/pallas_call | solution.py:327
  111.9 7.2 %all-to-all-done.5.got_ref = f32[32,8,128]{2,1,0:T(8,128)S(1)} async-done(((f32[32,8,128]{2,1,0:T(8,128)}), f32[32,8,128]{2,1,0:T(8,128)S(1)}, u32[]{:S(2)}, u32[]{:S(2)}) %all-to-all-start.5) | async-done | bytes 131104 | tf_op jit(solution)/shard_map/all_to_all | solution.py:310
  119.0 1.3 %time_admm.1 = f32[8,64]{1,0:T(8,128)} custom-call(f32[32,8,128]{2,1,0:T(8,128)S(1)} %all-to-all-done.5.got_ref, f32[128,128]{1,0:T(8,128)S(1)} %get-tuple-element.43.inverse_ref, f32[1,128]{1,0:T(1,128)S(1)} %get-tuple-element.44.penalty_ref, f32[8,128]{1,0:T(8,128)S(1)} %copy-done.2), custom_call_target="tpu_custom_call" | custom-call | bytes 203264 | tf_op jit(solution)/shard_map/time_admm/pallas_call | solution.py:327
  (2 shorter events, 0.1 us)
Async XLA Ops:
  1.6 17.1 %collective-permute-start = (bf16[256,512]{1,0:T(8,128)(2,1)S(1)}, bf16[256,512]{1,0:T(8,128)(2,1)S(1)}, u32[]{:S(2)}, u32[]{:S(2)}) collective-permute-start(bf16[256,512]{1,0:T(8,128)(2,1)S(1)} %slice.3), channel_id=1, source_target_pairs={{1,0},{2,1},{3,2},{4,3},{5,4},{6,5},{7,6},{8,7},{9,8},{10,9},{11,1... | collective-permute-start | bytes 786440 | tf_op jit(solution)/shard_map/ppermute | solution.py:343
  18.6 7.2 %copy-start = (f32[512,64]{0,1:T(8,128)S(1)}, f32[512,64]{0,1:T(8,128)}, u32[]{:S(2)}) copy-start(f32[512,64]{0,1:T(8,128)} %param.9) | copy-start | bytes 393220
  18.7 7.2 %copy-start.1 = (f32[256,64]{0,1:T(8,128)S(1)}, f32[256,64]{0,1:T(8,128)}, u32[]{:S(2)}) copy-start(f32[256,64]{0,1:T(8,128)} %param.8) | copy-start | bytes 196612
  18.7 27.9 %copy-start.2 = (f32[8,128]{1,0:T(8,128)S(1)}, f32[8,128]{1,0:T(8,128)}, u32[]{:S(2)}) copy-start(f32[8,128]{1,0:T(8,128)} %get-tuple-element.25.time2_ref.start2_ref) | copy-start | bytes 12292
  22.4 11.6 %all-to-all-start = ((f32[16,16,128]{2,1,0:T(8,128)}), f32[16,16,128]{2,1,0:T(8,128)S(1)}, u32[]{:S(2)}, u32[]{:S(2)}) async-start(f32[16,16,128]{2,1,0:T(8,128)} %get-tuple-element.27), calls=%async_computation | async-start | bytes 262144 | tf_op jit(solution)/shard_map/all_to_all | solution.py:310
  49.3 12.6 %all-to-all-start.2 = ((f32[16,16,128]{2,1,0:T(8,128)}), f32[16,16,128]{2,1,0:T(8,128)S(1)}, u32[]{:S(2)}, u32[]{:S(2)}) async-start(f32[16,16,128]{2,1,0:T(8,128)} %get-tuple-element.34), calls=%async_computation.2 | async-start | bytes 262144 | tf_op jit(solution)/shard_map/all_to_all | solution.py:310
  104.5 14.6 %all-to-all-start.5 = ((f32[32,8,128]{2,1,0:T(8,128)}), f32[32,8,128]{2,1,0:T(8,128)S(1)}, u32[]{:S(2)}, u32[]{:S(2)}) async-start(f32[32,8,128]{2,1,0:T(8,128)} %get-tuple-element.42), calls=%async_computation.5 | async-start | bytes 262144 | tf_op jit(solution)/shard_map/all_to_all | solution.py:310

commit v4 on v3

--- a/solution.py
+++ b/solution.py
@@ -189,17 +189,15 @@
     sum_ref[...] += chan_term(rows_ref, power, time2_ref[pl.ds(t, 1), :])
 
 
-def last_kernel(halo_ref, rows_ref, time2_ref, sum_ref, samples_ref, even_in, odd_in, window_ref,
-                power_ref, send_ref, held, even_ref, odd_ref, half_sem, even_sem, odd_sem):
-    load = pltpu.make_async_copy(samples_ref.at[:, EARLY * HALF:], held, half_sem)
-    even_load = pltpu.make_async_copy(even_in, even_ref, even_sem)
-    odd_load = pltpu.make_async_copy(odd_in, odd_ref, odd_sem)
-    load.start()
-    even_load.start()
-    odd_load.start()
-    load.wait()
-    even_load.wait()
-    odd_load.wait()
+def last_kernel(halo_ref, even_ref, odd_ref, samples_ref, window_in, rows_in, time2_in, sum_in,
+                power_ref, send_ref, held, window_ref, rows_ref, time2_ref, sum_ref, sems):
+    pairs = ((samples_ref.at[:, EARLY * HALF:], held), (window_in, window_ref),
+             (rows_in, rows_ref), (time2_in, time2_ref), (sum_in, sum_ref))
+    loads = [pltpu.make_async_copy(*pair, sems.at[i]) for i, pair in enumerate(pairs)]
+    for load in loads:
+        load.start()
+    for load in loads:
+        load.wait()
     power = frame_power(held[...], halo_ref[...], window_ref[...], even_ref, odd_ref)
     power_ref[...] = power
     total = sum_ref[...] + chan_term(rows_ref, power, time2_ref[EARLY:, :])
@@ -208,6 +206,12 @@
     for d in range(N_TM):
         send_ref[d, :per] = packed[d * per:(d + 1) * per]
         send_ref[d, per:] = time2_ref[...]
+
+
+def head_kernel(samples_ref, out_ref, sem):
+    load = pltpu.make_async_copy(samples_ref.at[:, :HALF], out_ref, sem)
+    load.start()
+    load.wait()
 
 
 def chan_kernel(got_ref, gram_freq_ref, start_ref, send_ref, gram_time_ref):
@@ -223,6 +227,7 @@
 
 
 FIRST_PART = 3
+TILE = 256
 
 
 def freq_kernel(chan_ref, time2_ref, last_ref, early_ref, part_ref, send_ref, sides, held, sems):
@@ -230,13 +235,36 @@
              for t in range(EARLY)]
     for load in loads:
         load.start()
-    sides[...] = high_low(both_halves(chan_ref[...].reshape(CHANS_HERE // 2, PACK)))
-    part_ref[EARLY] = jnp.dot(last_ref[...], sides[...], preferred_element_type=F32)
-    for low, high in ((0, FIRST_PART), (FIRST_PART, EARLY)):
-        for t in range(low, high):
-            loads[t].wait()
-        for t in range(low, high):
-            part_ref[t] = jnp.dot(held[t], sides[...], preferred_element_type=F32)
+    side = high_low(both_halves(chan_ref[...].reshape(CHANS_HERE // 2, PACK)))
+    sides[...] = jnp.concatenate([side, side], axis=1)
+    order = [EARLY] + list(range(EARLY))
+
+    def body(*accs):
+        for m in (0, 1):
+            pltpu.matmul_push_rhs(sides[...], 0, m)
+
+        def multiply(i):
+            t, m = order[i], i % 2
+            power = last_ref[...] if t == EARLY else held[t]
+            pltpu.matmul_acc_lhs(accs[i % 4], power, load_staged_rhs=0 if i < 2 else None)
+
+        def collect(i):
+            part_ref[order[i]] = pltpu.matmul_pop(accs[i % 4])[:, :PACK]
+
+        for i in range(FRAMES_HERE):
+            if i == 1:
+                for load in loads[:FIRST_PART]:
+                    load.wait()
+            if i == 1 + FIRST_PART:
+                for load in loads[FIRST_PART:]:
+                    load.wait()
+            multiply(i)
+            if i >= 2:
+                collect(i - 2)
+        collect(FRAMES_HERE - 2)
+        collect(FRAMES_HERE - 1)
+
+    pl.run_scoped(body, *[pltpu.ACC(m)((BINS, TILE), F32) for m in (0, 1, 0, 1)])
     for d in range(N_TM):
         sums = []
         for at in (d * 16, BINS // 2 + d * 16):
@@ -337,14 +365,16 @@
 
 
 def local(samples, start_chan, start_freq, start_time):
-    even_table, odd_table = (jnp.asarray(t) for t in half_tables())
+    even_table, odd_table = (
+        pltpu.with_memory_space_constraint(jnp.asarray(t), pltpu.VMEM) for t in half_tables())
     window = jnp.asarray(window_row())
-    route = [(i, i - 1) for i in range(1, N_TM)]
-    following = lax.ppermute(samples[:, :HALF], TM, route)
-    natural = [pltpu.VMEM((BINS, PACK), F32)]
-    table = pltpu.VMEM((BINS, HALF), BF16)
     flag = pltpu.SemaphoreType.DMA
     outside = pl.BlockSpec(memory_space=pltpu.HBM)
+    (head,) = near_call(head_kernel, "head", (shape(CHANS_HERE, HALF, dtype=BF16),), (),
+                        [flag(())], others=(samples,), kinds_of_others=[outside])
+    route = [(i, i - 1) for i in range(1, N_TM)]
+    following = lax.ppermute(head, TM, route)
+    natural = [pltpu.VMEM((BINS, PACK), F32)]
 
     def fixed(*dims):
         return pl.BlockSpec(dims, lambda t: (0,) * len(dims))
@@ -355,7 +385,7 @@
         in_specs=[pl.BlockSpec((CHANS_HERE, HALF), lambda t: (0, t)),
                   pl.BlockSpec((CHANS_HERE, HALF), lambda t: (0, t + 1)),
                   fixed(RANK, BINS), fixed(FRAMES_HERE, RANK), fixed(1, HALF),
-                  fixed(BINS, HALF), fixed(BINS, HALF)],
+                  NEAR, NEAR],
         out_specs=[pl.BlockSpec((1, BINS, CHANS_HERE), lambda t: (t, 0, 0)),
                    fixed(PACK, CHANS_HERE), fixed(PACK, BINS), fixed(FRAMES_HERE, PACK)],
         out_shape=(shape(EARLY, BINS, CHANS_HERE, dtype=BF16), shape(PACK, CHANS_HERE),
@@ -367,11 +397,12 @@
     )(samples, samples, start_freq.T, start_time, window, even_table, odd_table)
     power_last, to_chan = near_call(
         last_kernel, "last", (shape(BINS, CHANS_HERE, dtype=BF16), shape(N_TM, 16, PACK)),
-        (following,),
-        [pltpu.VMEM((CHANS_HERE, HALF), BF16), table, table, flag(()), flag(()), flag(())],
-        far=(1,),
-        others=(freq_rows, time2, early_sum, samples, even_table, odd_table, window),
-        kinds_of_others=[NEAR] * 3 + [outside] * 3 + [NEAR])
+        (following, even_table, odd_table),
+        [pltpu.VMEM((CHANS_HERE, HALF), BF16), pltpu.VMEM((1, HALF), F32),
+         pltpu.VMEM((PACK, BINS), BF16), pltpu.VMEM((FRAMES_HERE, PACK), F32),
+         pltpu.VMEM((PACK, CHANS_HERE), F32), flag((5,))],
+        far=(1,), others=(samples, window, freq_rows, time2, early_sum),
+        kinds_of_others=[outside] * 5)
 
     got = exchanged(to_chan, TM)
     gram_freq, freq_packed, chan_packed = near_call(
@@ -386,7 +417,7 @@
     part, to_freq = near_call(
         freq_kernel, "freq", (shape(FRAMES_HERE, BINS, PACK), shape(N_TM, 16, PACK)),
         (chan_all, time2, power_last),
-        [pltpu.VMEM((CHANS_HERE, PACK), BF16), pltpu.VMEM((EARLY, BINS, CHANS_HERE), BF16),
+        [pltpu.VMEM((CHANS_HERE, TILE), BF16), pltpu.VMEM((EARLY, BINS, CHANS_HERE), BF16),
          flag((EARLY,))], far=(1,), others=(power,), kinds_of_others=[outside])
     got = exchanged(to_freq, TM)
     gram_part, chan_out = near_call(

time: 121 us -> 119 us (0.983)
    pallas_call x10 -> x11, Pallas kernels: 16.2 us -> 15.9 us  [near_call(): pl.pallas_call(body, in_specs=[NEAR] * (len(args) - len(others)) + list(k...]
where the time goes in v4:
time: 119 us
  blocking collectives  50 us (42%)
  Pallas kernels  23.8 us (20%)
  waiting for transfers between devices  23.3 us (20%)
  starting transfers between devices  20.9 us (18%)
    all_to_all x3, blocking collectives, exchanged(): return lax.all_to_all(parts, axis, split_axis=0, concat_axis=0, tiled=True)  50 us
    all_to_all x3, waiting for transfers between devices, exchanged(): return lax.all_to_all(parts, axis, split_axis=0, concat_axis=0, tiled=True)  23.3 us
    pallas_call x11, Pallas kernels, near_call(): pl.pallas_call(body, in_specs=[NEAR] * (len(args) - len(others)) + list(k...  15.9 us
    all_to_all x3, starting transfers between devices, exchanged(): return lax.all_to_all(parts, axis, split_axis=0, concat_axis=0, tiled=True)  12.1 us
    ppermute x1, starting transfers between devices, local(): following = lax.ppermute(head, TM, route)  8.75 us
    pallas_call x1, Pallas kernels, local(): pl.pallas_call(early_kernel, grid=(EARLY,), in_specs=[pl.BlockSpec((CHANS...  7.91 us
  transfers between devices with their start and end apart: 4, of which 3 were waited for; matrix products, arithmetic and copies ran while one was open for 0% of the time, Pallas kernels for 10%

profile of v4, /device:TPU:1, one launch (start us, length us, event | category | flops | bytes accessed | tf_op | source)
XLA Modules:
  0.0 118.8 jit_solution(15739697829380271406)
XLA Ops:
  0.6 0.0 copy-start
  0.6 0.0 copy-start.1
  0.7 1.0 head.1
  1.7 8.7 %collective-permute-start = (bf16[256,512]{1,0:T(8,128)(2,1)S(1)}, bf16[256,512]{1,0:T(8,128)(2,1)S(1)}, u32[]{:S(2)}, u32[]{:S(2)}) collective-permute-start(bf16[256,512]{1,0:T(8,128)(2,1)S(1)} %head.1), channel_id=1, source_target_pairs={{1,0},{2,1},{3,2},{4,3},{5,4},{6,5},{7,6},{8,7},{9,8},{10,9},{11,1... | collective-permute-start | bytes 786440 | tf_op jit(solution)/shard_map/ppermute | solution.py:376
  10.5 0.0 copy-done
  10.5 0.0 copy-done.1
  10.5 7.9 %early.1 = (bf16[7,512,256]{2,1,0:T(8,128)(2,1)}, f32[128,256]{1,0:T(8,128)}, bf16[128,512]{1,0:T(8,128)(2,1)}, f32[8,128]{1,0:T(8,128)}) custom-call(bf16[256,4096]{1,0:T(8,128)(2,1)} %samples_ref.3, bf16[256,4096]{1,0:T(8,128)(2,1)} %samples_ref.3, f32[64,512]{1,0:T(8,128)} %bitcast.4, f32[8,64]{1,0:T(8,128)} %time_ref.1, ...), custom_call_target="tpu_custom_call" | custom-call | flops 2500000000 | bytes 8000000 | tf_op jit(solution)/shard_map/early/pallas_call | solution.py:382
  18.4 0.0 copy-start.2
  18.4 0.0 copy-start.3
  18.4 0.0 collective-permute-done.halo_ref
  18.4 0.0 copy-start.4
  18.4 2.6 %last.1 = (bf16[512,256]{1,0:T(8,128)(2,1)S(1)}, f32[16,16,128]{2,1,0:T(8,128)}) custom-call(bf16[256,512]{1,0:T(8,128)(2,1)S(1)} %collective-permute-done.halo_ref, bf16[512,512]{1,0:T(8,128)(2,1)S(1)} %copy-done, bf16[512,512]{1,0:T(8,128)(2,1)S(1)} %copy-done.1, bf16[256,4096]{1,0:T(8,128)(2,1)} %samples_ref.3, ...), custom_call_target="tpu_custom_call" | custom-call | bytes 4069376 | tf_op jit(solution)/shard_map/last/pallas_call | solution.py:355
  21.0 3.4 %all-to-all-start = ((f32[16,16,128]{2,1,0:T(8,128)}), f32[16,16,128]{2,1,0:T(8,128)S(1)}, u32[]{:S(2)}, u32[]{:S(2)}) async-start(f32[16,16,128]{2,1,0:T(8,128)} %get-tuple-element.27), calls=%async_computation | async-start | bytes 262144 | tf_op jit(solution)/shard_map/all_to_all | solution.py:338
  24.5 0.0 copy-done.2
  24.5 0.0 copy-done.3
  24.5 0.4 start.1
  24.9 7.7 %all-to-all-done.got_ref = f32[16,16,128]{2,1,0:T(8,128)S(1)} async-done(((f32[16,16,128]{2,1,0:T(8,128)}), f32[16,16,128]{2,1,0:T(8,128)S(1)}, u32[]{:S(2)}, u32[]{:S(2)}) %all-to-all-start) | async-done | bytes 131104 | tf_op jit(solution)/shard_map/all_to_all | solution.py:338
  32.7 2.0 %chan.1 = (f32[16,8,128]{2,1,0:T(8,128)S(1)}, f32[64,128]{1,0:T(8,128)S(1)}) custom-call(f32[16,16,128]{2,1,0:T(8,128)S(1)} %all-to-all-done.got_ref, f32[64,128]{1,0:T(8,128)S(1)} %get-tuple-element.28.gram_freq_ref, f32[128,128]{1,0:T(8,128)S(1)} %get-tuple-element.29.start_ref), custom_call_target="tpu_custom_call" | custom-call | bytes 327680 | tf_op jit(solution)/shard_map/chan/pallas_call | solution.py:355
  34.7 10.4 %all_to_all.30.chan_ref = f32[16,8,128]{2,1,0:T(8,128)S(1)} all-to-all(f32[16,8,128]{2,1,0:T(8,128)S(1)} %get-tuple-element.30), channel_id=1, replica_groups=mesh['chan_0'=4,'chan_1'=8,'tm_0'=8,'tm_1'=2] {'tm_0','tm_1'}, dimensions={0} | all-to-all | bytes 131072 | tf_op jit(solution)/shard_map/all_to_all | solution.py:338
  45.1 0.0 copy-done.4
  45.1 2.6 %freq.1 = (f32[8,512,128]{2,1,0:T(8,128)S(1)}, f32[16,16,128]{2,1,0:T(8,128)}) custom-call(f32[16,8,128]{2,1,0:T(8,128)S(1)} %all_to_all.30.chan_ref, f32[8,128]{1,0:T(8,128)S(1)} %copy-done.4, bf16[512,256]{1,0:T(8,128)(2,1)S(1)} %get-tuple-element.32.last_ref, bf16[7,512,256]{2,1,0:T(8,128)(2,1)} %get-tuple-element.33.early_ref), custom_call_target="tpu_custom_call" | custom-call | bytes 4395008 | tf_op jit(solution)/shard_map/freq/pallas_call | solution.py:355
  47.8 3.4 %all-to-all-start.2 = ((f32[16,16,128]{2,1,0:T(8,128)}), f32[16,16,128]{2,1,0:T(8,128)S(1)}, u32[]{:S(2)}, u32[]{:S(2)}) async-start(f32[16,16,128]{2,1,0:T(8,128)} %get-tuple-element.34), calls=%async_computation.2 | async-start | bytes 262144 | tf_op jit(solution)/shard_map/all_to_all | solution.py:338
  51.2 0.8 chan_out.1
  52.0 8.4 %all-to-all-done.2.got_ref = f32[16,16,128]{2,1,0:T(8,128)S(1)} async-done(((f32[16,16,128]{2,1,0:T(8,128)}), f32[16,16,128]{2,1,0:T(8,128)S(1)}, u32[]{:S(2)}, u32[]{:S(2)}) %all-to-all-start.2) | async-done | bytes 131104 | tf_op jit(solution)/shard_map/all_to_all | solution.py:338
  60.4 25.0 %all_to_all.31.got_ref = f32[32,24,128]{2,1,0:T(8,128)S(1)} all-to-all(f32[32,24,128]{2,1,0:T(8,128)S(1)} %spread.1), channel_id=1, replica_groups=mesh['chan_0'=4,'chan_1'=8,'tm_0'=8,'tm_1'=2] {'chan_0','chan_1'}, dimensions={0} | all-to-all | bytes 786432 | tf_op jit(solution)/shard_map/all_to_all | solution.py:338
  85.5 14.6 %all_to_all.32.got_ref = f32[16,24,128]{2,1,0:T(8,128)S(1)} all-to-all(f32[16,24,128]{2,1,0:T(8,128)S(1)} %relay.1), channel_id=1, replica_groups=mesh['chan_0'=4,'chan_1'=8,'tm_0'=8,'tm_1'=2] {'tm_0','tm_1'}, dimensions={0} | all-to-all | bytes 393216 | tf_op jit(solution)/shard_map/all_to_all | solution.py:338
  100.1 2.8 %freq_admm.1 = (f32[32,8,128]{2,1,0:T(8,128)}, f32[256,128]{1,0:T(8,128)S(1)}, f32[64,128]{1,0:T(8,128)S(1)}) custom-call(f32[16,24,128]{2,1,0:T(8,128)S(1)} %all_to_all.32.got_ref, f32[64,128]{1,0:T(8,128)S(1)} %get-tuple-element.36.gram_time_ref, f32[256,128]{1,0:T(8,128)S(1)} %get-tuple-element.37.start_ref, f32[8,512,128]{2,1,0:T(8,128)S(1)} %get-tuple-element.38.part_ref), custom_call_target="tpu_custom_call" | custom-call | bytes 2752512 | tf_op jit(solution)/shard_map/freq_admm/pallas_call | solution.py:355
  102.9 5.3 %all-to-all-start.5 = ((f32[32,8,128]{2,1,0:T(8,128)}), f32[32,8,128]{2,1,0:T(8,128)S(1)}, u32[]{:S(2)}, u32[]{:S(2)}) async-start(f32[32,8,128]{2,1,0:T(8,128)} %get-tuple-element.42), calls=%async_computation.5 | async-start | bytes 262144 | tf_op jit(solution)/shard_map/all_to_all | solution.py:338
  108.2 2.1 %freq_out.1 = (f32[128,128]{1,0:T(8,128)S(1)}, f32[1,128]{1,0:T(1,128)S(1)}, f32[64,512]{1,0:T(8,128)}) custom-call(f32[256,128]{1,0:T(8,128)S(1)} %get-tuple-element.39.freq_ref, f32[64,128]{1,0:T(8,128)S(1)} %get-tuple-element.40.gram_chan_ref), custom_call_target="tpu_custom_call" | custom-call | bytes 360960 | tf_op jit(solution)/shard_map/freq_out/pallas_call | solution.py:355
  110.3 7.2 %all-to-all-done.5.got_ref = f32[32,8,128]{2,1,0:T(8,128)S(1)} async-done(((f32[32,8,128]{2,1,0:T(8,128)}), f32[32,8,128]{2,1,0:T(8,128)S(1)}, u32[]{:S(2)}, u32[]{:S(2)}) %all-to-all-start.5) | async-done | bytes 131104 | tf_op jit(solution)/shard_map/all_to_all | solution.py:338
  117.5 1.3 %time_admm.1 = f32[8,64]{1,0:T(8,128)} custom-call(f32[32,8,128]{2,1,0:T(8,128)S(1)} %all-to-all-done.5.got_ref, f32[128,128]{1,0:T(8,128)S(1)} %get-tuple-element.43.inverse_ref, f32[1,128]{1,0:T(1,128)S(1)} %get-tuple-element.44.penalty_ref, f32[8,128]{1,0:T(8,128)S(1)} %copy-done.4), custom_call_target="tpu_custom_call" | custom-call | bytes 203264 | tf_op jit(solution)/shard_map/time_admm/pallas_call | solution.py:355
  (2 shorter events, 0.1 us)
Async XLA Ops:
  0.6 9.8 %copy-start = (bf16[512,512]{1,0:T(8,128)(2,1)S(1)}, bf16[512,512]{1,0:T(8,128)(2,1)}, u32[]{:S(2)}) copy-start(bf16[512,512]{1,0:T(8,128)(2,1)} %constant.6.clone.even_ref) | copy-start | bytes 1572868
  0.6 9.8 %copy-start.1 = (bf16[512,512]{1,0:T(8,128)(2,1)S(1)}, bf16[512,512]{1,0:T(8,128)(2,1)}, u32[]{:S(2)}) copy-start(bf16[512,512]{1,0:T(8,128)(2,1)} %constant.7.clone.odd_ref) | copy-start | bytes 1572868
  1.7 16.7 %collective-permute-start = (bf16[256,512]{1,0:T(8,128)(2,1)S(1)}, bf16[256,512]{1,0:T(8,128)(2,1)S(1)}, u32[]{:S(2)}, u32[]{:S(2)}) collective-permute-start(bf16[256,512]{1,0:T(8,128)(2,1)S(1)} %head.1), channel_id=1, source_target_pairs={{1,0},{2,1},{3,2},{4,3},{5,4},{6,5},{7,6},{8,7},{9,8},{10,9},{11,1... | collective-permute-start | bytes 786440 | tf_op jit(solution)/shard_map/ppermute | solution.py:376
  18.4 6.1 %copy-start.2 = (f32[512,64]{0,1:T(8,128)S(1)}, f32[512,64]{0,1:T(8,128)}, u32[]{:S(2)}) copy-start(f32[512,64]{0,1:T(8,128)} %param.9) | copy-start | bytes 393220
  18.4 6.1 %copy-start.3 = (f32[256,64]{0,1:T(8,128)S(1)}, f32[256,64]{0,1:T(8,128)}, u32[]{:S(2)}) copy-start(f32[256,64]{0,1:T(8,128)} %param.8) | copy-start | bytes 196612
  18.4 26.7 %copy-start.4 = (f32[8,128]{1,0:T(8,128)S(1)}, f32[8,128]{1,0:T(8,128)}, u32[]{:S(2)}) copy-start(f32[8,128]{1,0:T(8,128)} %get-tuple-element.25.time2_in.time2_ref.start2_ref) | copy-start | bytes 12292
  21.0 11.6 %all-to-all-start = ((f32[16,16,128]{2,1,0:T(8,128)}), f32[16,16,128]{2,1,0:T(8,128)S(1)}, u32[]{:S(2)}, u32[]{:S(2)}) async-start(f32[16,16,128]{2,1,0:T(8,128)} %get-tuple-element.27), calls=%async_computation | async-start | bytes 262144 | tf_op jit(solution)/shard_map/all_to_all | solution.py:338
  47.8 12.6 %all-to-all-start.2 = ((f32[16,16,128]{2,1,0:T(8,128)}), f32[16,16,128]{2,1,0:T(8,128)S(1)}, u32[]{:S(2)}, u32[]{:S(2)}) async-start(f32[16,16,128]{2,1,0:T(8,128)} %get-tuple-element.34), calls=%async_computation.2 | async-start | bytes 262144 | tf_op jit(solution)/shard_map/all_to_all | solution.py:338
  102.9 14.6 %all-to-all-start.5 = ((f32[32,8,128]{2,1,0:T(8,128)}), f32[32,8,128]{2,1,0:T(8,128)S(1)}, u32[]{:S(2)}, u32[]{:S(2)}) async-start(f32[32,8,128]{2,1,0:T(8,128)} %get-tuple-element.42), calls=%async_computation.5 | async-start | bytes 262144 | tf_op jit(solution)/shard_map/all_to_all | solution.py:338

commit v5 on v4

--- a/solution.py
+++ b/solution.py
@@ -13,6 +13,7 @@
 RANK = 64
 ITERS = 5
 FRAMES_HERE = 8
+QUAD = 4
 CHANS_HERE = 256
 PACK = 2 * RANK
 TM = ("tm_0", "tm_1")
@@ -203,9 +204,11 @@
     total = sum_ref[...] + chan_term(rows_ref, power, time2_ref[EARLY:, :])
     packed = stacked(total[:RANK] + total[RANK:]).T
     per = CHANS_HERE // 2 // N_TM
+    times = side_by_side(time2_ref[...])
     for d in range(N_TM):
-        send_ref[d, :per] = packed[d * per:(d + 1) * per]
-        send_ref[d, per:] = time2_ref[...]
+        for i in range(per // QUAD):
+            send_ref[d, i] = packed[d * per + i * QUAD:d * per + (i + 1) * QUAD]
+        send_ref[d, per // QUAD] = times
 
 
 def head_kernel(samples_ref, out_ref, sem):
@@ -217,8 +220,11 @@
 def chan_kernel(got_ref, gram_freq_ref, start_ref, send_ref, gram_time_ref):
     me = lax.axis_index(TM)
     per = CHANS_HERE // 2 // N_TM
-    total = jnp.sum(got_ref[:, :per], axis=0)
-    gram_time = gram_of(got_ref[:, per:].reshape(N_TM * FRAMES_HERE, PACK))
+    blocks = per // QUAD
+    total = jnp.concatenate(
+        [sum(got_ref[d, i] for d in range(N_TM)) for i in range(blocks)], axis=0)
+    times = jnp.concatenate([got_ref[d, blocks] for d in range(N_TM)], axis=0)
+    gram_time = gram_of(both_halves(times))
     gram_time_ref[...] = gram_time
     penalty, inverse = inverse_of(gram_time * gram_freq_ref[...])
     start = start_ref[pl.ds(pl.multiple_of(me * per, per), per), :]
@@ -275,40 +281,66 @@
         send_ref[d] = jnp.where(lane_is_low((16, PACK)), *sums)
 
 
+N_GRAM = RANK // 2 // QUAD
+
+
 def chan_out_kernel(chan_ref, gram_ref, chan_out_ref):
     packed = chan_ref[...].reshape(CHANS_HERE // 2, PACK)
-    gram_ref[...] = side_by_side(gram_of(both_halves(packed)))
+    gram = side_by_side(gram_of(both_halves(packed)))
+    for i in range(N_GRAM):
+        gram_ref[i] = gram[i * QUAD:(i + 1) * QUAD]
     turned = packed.T
     chan_out_ref[...] = jnp.concatenate([turned[:RANK], turned[RANK:]], axis=1)
 
 
 def spread_kernel(got_ref, gram_ref, send_ref):
     me = lax.axis_index(TM)
-    rows = got_ref.shape[1]
     total = jnp.sum(got_ref[...], axis=0)
-    block = gram_ref[pl.ds(pl.multiple_of(me // (N_TM // 4) * 8, 8), 8), :]
-    for d in range(send_ref.shape[0]):
-        send_ref[d, :rows] = total
-        send_ref[d, rows:] = block
+    block = gram_ref[me // (N_TM // N_GRAM)]
+    for d in range(N_CHAN):
+        for i in range(total.shape[0] // QUAD):
+            send_ref[d, i] = total[i * QUAD:(i + 1) * QUAD]
+        send_ref[d, total.shape[0] // QUAD] = block
 
 
 def relay_kernel(got_ref, send_ref):
-    send_ref[...] = jnp.broadcast_to(jnp.sum(got_ref[...], axis=0)[None], send_ref.shape)
+    for i in range(got_ref.shape[1]):
+        total = got_ref[0, i]
+        for d in range(1, N_CHAN):
+            total = total + got_ref[d, i]
+        for d in range(N_TM):
+            send_ref[d, i] = total
+
+
+PIECE = 64
 
 
 def freq_admm_kernel(got_ref, gram_time_ref, start_ref, part_ref, send_ref, new_ref,
-                     gram_chan_ref):
+                     gram_chan_ref, product_ref, packed_ref):
     rows = BINS // 2 // N_TM
-    product = got_ref[:, :rows].reshape(BINS // 2, PACK)
-    gram = both_halves(jnp.concatenate(
-        [got_ref[d, rows:] for d in range(0, N_TM, N_TM // 4)], axis=0))
+    blocks = rows // QUAD
+    for d in range(N_TM):
+        for i in range(blocks):
+            at = d * rows + i * QUAD
+            product_ref[at:at + QUAD, :] = got_ref[d, i]
+    for i in range(N_GRAM):
+        packed_ref[i * QUAD:(i + 1) * QUAD, :] = got_ref[i * (N_TM // N_GRAM), blocks]
+    product = product_ref[...]
+    gram = both_halves(packed_ref[...])
     gram_chan_ref[...] = gram
     penalty, inverse = inverse_of(gram * gram_time_ref[...])
     new = admm(product * SCALE, start_ref[...], penalty, inverse)
     new_ref[...] = new
-    twice = both_halves(new)
-    sums = [jnp.sum(part_ref[t] * twice, axis=0, keepdims=True) for t in range(FRAMES_HERE)]
-    product = jnp.concatenate(sums, axis=0)
+    sums = [jnp.zeros((8, PACK), F32)] * FRAMES_HERE
+    half = BINS // 2
+    for at in range(0, half, PIECE):
+        twice = both_halves(new_ref[at:at + PIECE, :])
+        for t in range(FRAMES_HERE):
+            for first, side in ((at, twice[:PIECE]), (half + at, twice[PIECE:])):
+                piece = part_ref[t, first:first + PIECE] * side
+                sums[t] += jnp.sum(piece.reshape(PIECE // 8, 8, PACK), axis=0)
+    product = jnp.concatenate([jnp.sum(s, axis=0, keepdims=True) for s in sums], axis=0)
+    product = side_by_side(product + pltpu.roll(product, RANK, 1))
     send_ref[...] = jnp.broadcast_to(product[None], send_ref.shape)
 
 
@@ -324,8 +356,7 @@
 
 
 def time_admm_kernel(got_ref, inverse_ref, penalty_ref, start2_ref, out_ref):
-    total = jnp.sum(got_ref[...], axis=0)
-    total = total + pltpu.roll(total, RANK, 1)
+    total = both_halves(jnp.sum(got_ref[...], axis=0))
     new = admm(total * SCALE, start2_ref[...], penalty_ref[...], inverse_ref[...])
     out_ref[...] = new[:, :RANK]
 
@@ -396,7 +427,7 @@
         name="early",
     )(samples, samples, start_freq.T, start_time, window, even_table, odd_table)
     power_last, to_chan = near_call(
-        last_kernel, "last", (shape(BINS, CHANS_HERE, dtype=BF16), shape(N_TM, 16, PACK)),
+        last_kernel, "last", (shape(BINS, CHANS_HERE, dtype=BF16), shape(N_TM, 3, QUAD, PACK)),
         (following, even_table, odd_table),
         [pltpu.VMEM((CHANS_HERE, HALF), BF16), pltpu.VMEM((1, HALF), F32),
          pltpu.VMEM((PACK, BINS), BF16), pltpu.VMEM((FRAMES_HERE, PACK), F32),
@@ -421,18 +452,19 @@
          flag((EARLY,))], far=(1,), others=(power,), kinds_of_others=[outside])
     got = exchanged(to_freq, TM)
     gram_part, chan_out = near_call(
-        chan_out_kernel, "chan_out", (shape(RANK // 2, PACK), shape(RANK, CHANS_HERE)),
+        chan_out_kernel, "chan_out", (shape(N_GRAM, QUAD, PACK), shape(RANK, CHANS_HERE)),
         (chan_all,), far=(1,))
 
-    rows = 16 + 8
-    (to_all,) = near_call(spread_kernel, "spread", (shape(N_CHAN, rows, PACK),), (got, gram_part))
+    (to_all,) = near_call(spread_kernel, "spread", (shape(N_CHAN, 5, QUAD, PACK),),
+                          (got, gram_part))
     got = exchanged(to_all, CHAN)
-    (to_tm,) = near_call(relay_kernel, "relay", (shape(N_TM, rows, PACK),), (got,))
+    (to_tm,) = near_call(relay_kernel, "relay", (shape(N_TM, 5, QUAD, PACK),), (got,))
     got = exchanged(to_tm, TM)
     to_all, freq_all, gram_chan = near_call(
         freq_admm_kernel, "freq_admm",
-        (shape(N_CHAN, FRAMES_HERE, PACK), shape(BINS // 2, PACK), shape(RANK, PACK)),
-        (got, gram_time, freq_packed, part), far=(0,))
+        (shape(N_CHAN, QUAD, PACK), shape(BINS // 2, PACK), shape(RANK, PACK)),
+        (got, gram_time, freq_packed, part),
+        [pltpu.VMEM((BINS // 2, PACK), F32), pltpu.VMEM((RANK // 2, PACK), F32)], far=(0,))
     got = exchanged(to_all, CHAN)
     inverse, penalty, freq_out = near_call(
         freq_out_kernel, "freq_out",

time: 119 us -> 116 us (0.975)
  blocking collectives: 50 us -> 47.9 us
    all_to_all x3, blocking collectives: 50 us -> 47.9 us  [exchanged(): return lax.all_to_all(parts, axis, split_axis=0, concat_axis=0, tiled=True)]
where the time goes in v5:
time: 116 us
  blocking collectives  47.9 us (41%)
  Pallas kernels  23.9 us (21%)
  waiting for transfers between devices  22.2 us (19%)
  starting transfers between devices  20.8 us (18%)
    all_to_all x3, blocking collectives, exchanged(): return lax.all_to_all(parts, axis, split_axis=0, concat_axis=0, tiled=True)  47.9 us
    all_to_all x3, waiting for transfers between devices, exchanged(): return lax.all_to_all(parts, axis, split_axis=0, concat_axis=0, tiled=True)  22.2 us
    pallas_call x11, Pallas kernels, near_call(): pl.pallas_call(body, in_specs=[NEAR] * (len(args) - len(others)) + list(k...  16 us
    all_to_all x3, starting transfers between devices, exchanged(): return lax.all_to_all(parts, axis, split_axis=0, concat_axis=0, tiled=True)  12.1 us
    ppermute x1, starting transfers between devices, local(): following = lax.ppermute(head, TM, route)  8.75 us
    pallas_call x1, Pallas kernels, local(): pl.pallas_call(early_kernel, grid=(EARLY,), in_specs=[pl.BlockSpec((CHANS...  7.91 us
  transfers between devices with their start and end apart: 4, of which 3 were waited for; matrix products, arithmetic and copies ran while one was open for 0% of the time, Pallas kernels for 10%

profile of v5, /device:TPU:1, one launch (start us, length us, event | category | flops | bytes accessed | tf_op | source)
XLA Modules:
  0.0 115.7 jit_solution(3155790336474652073)
XLA Ops:
  0.6 0.0 copy-start
  0.6 0.0 copy-start.1
  0.7 1.0 head.1
  1.7 8.7 %collective-permute-start = (bf16[256,512]{1,0:T(8,128)(2,1)S(1)}, bf16[256,512]{1,0:T(8,128)(2,1)S(1)}, u32[]{:S(2)}, u32[]{:S(2)}) collective-permute-start(bf16[256,512]{1,0:T(8,128)(2,1)S(1)} %head.1), channel_id=1, source_target_pairs={{1,0},{2,1},{3,2},{4,3},{5,4},{6,5},{7,6},{8,7},{9,8},{10,9},{11,1... | collective-permute-start | bytes 786440 | tf_op jit(solution)/shard_map/ppermute | solution.py:407
  10.5 0.0 copy-done
  10.5 0.0 copy-done.1
  10.5 7.9 %early.1 = (bf16[7,512,256]{2,1,0:T(8,128)(2,1)}, f32[128,256]{1,0:T(8,128)}, bf16[128,512]{1,0:T(8,128)(2,1)}, f32[8,128]{1,0:T(8,128)}) custom-call(bf16[256,4096]{1,0:T(8,128)(2,1)} %samples_ref.3, bf16[256,4096]{1,0:T(8,128)(2,1)} %samples_ref.3, f32[64,512]{1,0:T(8,128)} %bitcast.4, f32[8,64]{1,0:T(8,128)} %time_ref.1, ...), custom_call_target="tpu_custom_call" | custom-call | flops 2500000000 | bytes 8000000 | tf_op jit(solution)/shard_map/early/pallas_call | solution.py:413
  18.4 0.0 copy-start.2
  18.4 0.0 copy-start.3
  18.4 0.0 collective-permute-done.halo_ref
  18.4 0.0 copy-start.4
  18.4 2.6 %last.1 = (bf16[512,256]{1,0:T(8,128)(2,1)S(1)}, f32[16,3,4,128]{3,2,1,0:T(4,128)}) custom-call(bf16[256,512]{1,0:T(8,128)(2,1)S(1)} %collective-permute-done.halo_ref, bf16[512,512]{1,0:T(8,128)(2,1)S(1)} %copy-done, bf16[512,512]{1,0:T(8,128)(2,1)S(1)} %copy-done.1, bf16[256,4096]{1,0:T(8,128)(2,1)} %samples_ref.3, ...), custom_call_target="tpu_custom_call" | custom-call | bytes 4036608 | tf_op jit(solution)/shard_map/last/pallas_call | solution.py:386
  21.0 3.4 %all-to-all-start = ((f32[16,3,4,128]{3,2,1,0:T(4,128)}), f32[16,3,4,128]{3,2,1,0:T(4,128)S(1)}, u32[]{:S(2)}, u32[]{:S(2)}) async-start(f32[16,3,4,128]{3,2,1,0:T(4,128)} %get-tuple-element.27), calls=%async_computation | async-start | bytes 196608 | tf_op jit(solution)/shard_map/all_to_all | solution.py:369
  24.4 0.0 copy-done.2
  24.4 0.0 copy-done.3
  24.5 0.4 start.1
  24.9 7.1 %all-to-all-done.got_ref = f32[16,3,4,128]{3,2,1,0:T(4,128)S(1)} async-done(((f32[16,3,4,128]{3,2,1,0:T(4,128)}), f32[16,3,4,128]{3,2,1,0:T(4,128)S(1)}, u32[]{:S(2)}, u32[]{:S(2)}) %all-to-all-start) | async-done | bytes 98336 | tf_op jit(solution)/shard_map/all_to_all | solution.py:369
  32.0 2.1 %chan.1 = (f32[16,8,128]{2,1,0:T(8,128)S(1)}, f32[64,128]{1,0:T(8,128)S(1)}) custom-call(f32[16,3,4,128]{3,2,1,0:T(4,128)S(1)} %all-to-all-done.got_ref, f32[64,128]{1,0:T(8,128)S(1)} %get-tuple-element.28.gram_freq_ref, f32[128,128]{1,0:T(8,128)S(1)} %get-tuple-element.29.start_ref), custom_call_target="tpu_custom_call" | custom-call | bytes 294912 | tf_op jit(solution)/shard_map/chan/pallas_call | solution.py:386
  34.1 10.3 %all_to_all.30.chan_ref = f32[16,8,128]{2,1,0:T(8,128)S(1)} all-to-all(f32[16,8,128]{2,1,0:T(8,128)S(1)} %get-tuple-element.30), channel_id=1, replica_groups=mesh['chan_0'=4,'chan_1'=8,'tm_0'=8,'tm_1'=2] {'tm_0','tm_1'}, dimensions={0} | all-to-all | bytes 131072 | tf_op jit(solution)/shard_map/all_to_all | solution.py:369
  44.5 0.0 copy-done.4
  44.5 2.6 %freq.1 = (f32[8,512,128]{2,1,0:T(8,128)S(1)}, f32[16,16,128]{2,1,0:T(8,128)}) custom-call(f32[16,8,128]{2,1,0:T(8,128)S(1)} %all_to_all.30.chan_ref, f32[8,128]{1,0:T(8,128)S(1)} %copy-done.4, bf16[512,256]{1,0:T(8,128)(2,1)S(1)} %get-tuple-element.32.last_ref, bf16[7,512,256]{2,1,0:T(8,128)(2,1)} %get-tuple-element.33.early_ref), custom_call_target="tpu_custom_call" | custom-call | bytes 4395008 | tf_op jit(solution)/shard_map/freq/pallas_call | solution.py:386
  47.1 3.4 %all-to-all-start.2 = ((f32[16,16,128]{2,1,0:T(8,128)}), f32[16,16,128]{2,1,0:T(8,128)S(1)}, u32[]{:S(2)}, u32[]{:S(2)}) async-start(f32[16,16,128]{2,1,0:T(8,128)} %get-tuple-element.34), calls=%async_computation.2 | async-start | bytes 262144 | tf_op jit(solution)/shard_map/all_to_all | solution.py:369
  50.5 0.8 chan_out.1
  51.4 8.4 %all-to-all-done.2.got_ref = f32[16,16,128]{2,1,0:T(8,128)S(1)} async-done(((f32[16,16,128]{2,1,0:T(8,128)}), f32[16,16,128]{2,1,0:T(8,128)S(1)}, u32[]{:S(2)}, u32[]{:S(2)}) %all-to-all-start.2) | async-done | bytes 131104 | tf_op jit(solution)/shard_map/all_to_all | solution.py:369
  59.8 23.9 %all_to_all.31.got_ref = f32[32,5,4,128]{3,2,1,0:T(4,128)S(1)} all-to-all(f32[32,5,4,128]{3,2,1,0:T(4,128)S(1)} %spread.1), channel_id=1, replica_groups=mesh['chan_0'=4,'chan_1'=8,'tm_0'=8,'tm_1'=2] {'chan_0','chan_1'}, dimensions={0} | all-to-all | bytes 655360 | tf_op jit(solution)/shard_map/all_to_all | solution.py:369
  83.7 0.1 relay.1
  83.8 13.6 %all_to_all.32.got_ref = f32[16,5,4,128]{3,2,1,0:T(4,128)S(1)} all-to-all(f32[16,5,4,128]{3,2,1,0:T(4,128)S(1)} %relay.1), channel_id=1, replica_groups=mesh['chan_0'=4,'chan_1'=8,'tm_0'=8,'tm_1'=2] {'tm_0','tm_1'}, dimensions={0} | all-to-all | bytes 327680 | tf_op jit(solution)/shard_map/all_to_all | solution.py:369
  97.4 2.9 %freq_admm.1 = (f32[32,4,128]{2,1,0:T(4,128)}, f32[256,128]{1,0:T(8,128)S(1)}, f32[64,128]{1,0:T(8,128)S(1)}) custom-call(f32[16,5,4,128]{3,2,1,0:T(4,128)S(1)} %all_to_all.32.got_ref, f32[64,128]{1,0:T(8,128)S(1)} %get-tuple-element.36.gram_time_ref, f32[256,128]{1,0:T(8,128)S(1)} %get-tuple-element.37.start_ref, f32[8,512,128]{2,1,0:T(8,128)S(1)} %get-tuple-element.38.part_ref), custom_call_target="tpu_custom_call" | custom-call | bytes 2654208 | tf_op jit(solution)/shard_map/freq_admm/pallas_call | solution.py:386
  100.3 5.2 %all-to-all-start.5 = ((f32[32,4,128]{2,1,0:T(4,128)}), f32[32,4,128]{2,1,0:T(4,128)S(1)}, u32[]{:S(2)}, u32[]{:S(2)}) async-start(f32[32,4,128]{2,1,0:T(4,128)} %get-tuple-element.42), calls=%async_computation.5 | async-start | bytes 131072 | tf_op jit(solution)/shard_map/all_to_all | solution.py:369
  105.5 2.1 %freq_out.1 = (f32[128,128]{1,0:T(8,128)S(1)}, f32[1,128]{1,0:T(1,128)S(1)}, f32[64,512]{1,0:T(8,128)}) custom-call(f32[256,128]{1,0:T(8,128)S(1)} %get-tuple-element.39.freq_ref, f32[64,128]{1,0:T(8,128)S(1)} %get-tuple-element.40.gram_chan_ref), custom_call_target="tpu_custom_call" | custom-call | bytes 360960 | tf_op jit(solution)/shard_map/freq_out/pallas_call | solution.py:386
  107.7 6.7 %all-to-all-done.5.got_ref = f32[32,4,128]{2,1,0:T(4,128)S(1)} async-done(((f32[32,4,128]{2,1,0:T(4,128)}), f32[32,4,128]{2,1,0:T(4,128)S(1)}, u32[]{:S(2)}, u32[]{:S(2)}) %all-to-all-start.5) | async-done | bytes 65568 | tf_op jit(solution)/shard_map/all_to_all | solution.py:369
  114.4 1.3 %time_admm.1 = f32[8,64]{1,0:T(8,128)} custom-call(f32[32,4,128]{2,1,0:T(4,128)S(1)} %all-to-all-done.5.got_ref, f32[128,128]{1,0:T(8,128)S(1)} %get-tuple-element.43.inverse_ref, f32[1,128]{1,0:T(1,128)S(1)} %get-tuple-element.44.penalty_ref, f32[8,128]{1,0:T(8,128)S(1)} %copy-done.4), custom_call_target="tpu_custom_call" | custom-call | bytes 137728 | tf_op jit(solution)/shard_map/time_admm/pallas_call | solution.py:386
  (1 shorter events, 0.0 us)
Async XLA Ops:
  0.6 9.8 %copy-start = (bf16[512,512]{1,0:T(8,128)(2,1)S(1)}, bf16[512,512]{1,0:T(8,128)(2,1)}, u32[]{:S(2)}) copy-start(bf16[512,512]{1,0:T(8,128)(2,1)} %constant.6.clone.even_ref) | copy-start | bytes 1572868
  0.6 9.8 %copy-start.1 = (bf16[512,512]{1,0:T(8,128)(2,1)S(1)}, bf16[512,512]{1,0:T(8,128)(2,1)}, u32[]{:S(2)}) copy-start(bf16[512,512]{1,0:T(8,128)(2,1)} %constant.7.clone.odd_ref) | copy-start | bytes 1572868
  1.7 16.7 %collective-permute-start = (bf16[256,512]{1,0:T(8,128)(2,1)S(1)}, bf16[256,512]{1,0:T(8,128)(2,1)S(1)}, u32[]{:S(2)}, u32[]{:S(2)}) collective-permute-start(bf16[256,512]{1,0:T(8,128)(2,1)S(1)} %head.1), channel_id=1, source_target_pairs={{1,0},{2,1},{3,2},{4,3},{5,4},{6,5},{7,6},{8,7},{9,8},{10,9},{11,1... | collective-permute-start | bytes 786440 | tf_op jit(solution)/shard_map/ppermute | solution.py:407
  18.4 6.0 %copy-start.2 = (f32[512,64]{0,1:T(8,128)S(1)}, f32[512,64]{0,1:T(8,128)}, u32[]{:S(2)}) copy-start(f32[512,64]{0,1:T(8,128)} %param.9) | copy-start | bytes 393220
  18.4 6.0 %copy-start.3 = (f32[256,64]{0,1:T(8,128)S(1)}, f32[256,64]{0,1:T(8,128)}, u32[]{:S(2)}) copy-start(f32[256,64]{0,1:T(8,128)} %param.8) | copy-start | bytes 196612
  18.4 26.0 %copy-start.4 = (f32[8,128]{1,0:T(8,128)S(1)}, f32[8,128]{1,0:T(8,128)}, u32[]{:S(2)}) copy-start(f32[8,128]{1,0:T(8,128)} %get-tuple-element.25.time2_in.time2_ref.start2_ref) | copy-start | bytes 12292
  21.0 11.0 %all-to-all-start = ((f32[16,3,4,128]{3,2,1,0:T(4,128)}), f32[16,3,4,128]{3,2,1,0:T(4,128)S(1)}, u32[]{:S(2)}, u32[]{:S(2)}) async-start(f32[16,3,4,128]{3,2,1,0:T(4,128)} %get-tuple-element.27), calls=%async_computation | async-start | bytes 196608 | tf_op jit(solution)/shard_map/all_to_all | solution.py:369
  47.1 12.6 %all-to-all-start.2 = ((f32[16,16,128]{2,1,0:T(8,128)}), f32[16,16,128]{2,1,0:T(8,128)S(1)}, u32[]{:S(2)}, u32[]{:S(2)}) async-start(f32[16,16,128]{2,1,0:T(8,128)} %get-tuple-element.34), calls=%async_computation.2 | async-start | bytes 262144 | tf_op jit(solution)/shard_map/all_to_all | solution.py:369
  100.3 14.1 %all-to-all-start.5 = ((f32[32,4,128]{2,1,0:T(4,128)}), f32[32,4,128]{2,1,0:T(4,128)S(1)}, u32[]{:S(2)}, u32[]{:S(2)}) async-start(f32[32,4,128]{2,1,0:T(4,128)} %get-tuple-element.42), calls=%async_computation.5 | async-start | bytes 131072 | tf_op jit(solution)/shard_map/all_to_all | solution.py:369

commit v6 on v5

--- a/solution.py
+++ b/solution.py
@@ -190,16 +190,9 @@
     sum_ref[...] += chan_term(rows_ref, power, time2_ref[pl.ds(t, 1), :])
 
 
-def last_kernel(halo_ref, even_ref, odd_ref, samples_ref, window_in, rows_in, time2_in, sum_in,
-                power_ref, send_ref, held, window_ref, rows_ref, time2_ref, sum_ref, sems):
-    pairs = ((samples_ref.at[:, EARLY * HALF:], held), (window_in, window_ref),
-             (rows_in, rows_ref), (time2_in, time2_ref), (sum_in, sum_ref))
-    loads = [pltpu.make_async_copy(*pair, sems.at[i]) for i, pair in enumerate(pairs)]
-    for load in loads:
-        load.start()
-    for load in loads:
-        load.wait()
-    power = frame_power(held[...], halo_ref[...], window_ref[...], even_ref, odd_ref)
+def last_kernel(tail_ref, halo_ref, window_ref, even_ref, odd_ref, rows_ref, time2_ref, sum_ref,
+                power_ref, send_ref):
+    power = frame_power(tail_ref[...], halo_ref[...], window_ref[...], even_ref, odd_ref)
     power_ref[...] = power
     total = sum_ref[...] + chan_term(rows_ref, power, time2_ref[EARLY:, :])
     packed = stacked(total[:RANK] + total[RANK:]).T
@@ -211,10 +204,13 @@
         send_ref[d, per // QUAD] = times
 
 
-def head_kernel(samples_ref, out_ref, sem):
-    load = pltpu.make_async_copy(samples_ref.at[:, :HALF], out_ref, sem)
-    load.start()
-    load.wait()
+def ends_kernel(samples_ref, head_ref, tail_ref, sems):
+    loads = [pltpu.make_async_copy(samples_ref.at[:, at:at + HALF], ref, sems.at[i])
+             for i, (at, ref) in enumerate(((0, head_ref), (EARLY * HALF, tail_ref)))]
+    for load in loads:
+        load.start()
+    for load in loads:
+        load.wait()
 
 
 def chan_kernel(got_ref, gram_freq_ref, start_ref, send_ref, gram_time_ref):
@@ -398,11 +394,12 @@
 def local(samples, start_chan, start_freq, start_time):
     even_table, odd_table = (
         pltpu.with_memory_space_constraint(jnp.asarray(t), pltpu.VMEM) for t in half_tables())
-    window = jnp.asarray(window_row())
+    window = pltpu.with_memory_space_constraint(jnp.asarray(window_row()), pltpu.VMEM)
     flag = pltpu.SemaphoreType.DMA
     outside = pl.BlockSpec(memory_space=pltpu.HBM)
-    (head,) = near_call(head_kernel, "head", (shape(CHANS_HERE, HALF, dtype=BF16),), (),
-                        [flag(())], others=(samples,), kinds_of_others=[outside])
+    piece = shape(CHANS_HERE, HALF, dtype=BF16)
+    head, tail = near_call(ends_kernel, "ends", (piece, piece), (), [flag((2,))],
+                           others=(samples,), kinds_of_others=[outside])
     route = [(i, i - 1) for i in range(1, N_TM)]
     following = lax.ppermute(head, TM, route)
     natural = [pltpu.VMEM((BINS, PACK), F32)]
@@ -415,12 +412,11 @@
         grid=(EARLY,),
         in_specs=[pl.BlockSpec((CHANS_HERE, HALF), lambda t: (0, t)),
                   pl.BlockSpec((CHANS_HERE, HALF), lambda t: (0, t + 1)),
-                  fixed(RANK, BINS), fixed(FRAMES_HERE, RANK), fixed(1, HALF),
-                  NEAR, NEAR],
-        out_specs=[pl.BlockSpec((1, BINS, CHANS_HERE), lambda t: (t, 0, 0)),
-                   fixed(PACK, CHANS_HERE), fixed(PACK, BINS), fixed(FRAMES_HERE, PACK)],
-        out_shape=(shape(EARLY, BINS, CHANS_HERE, dtype=BF16), shape(PACK, CHANS_HERE),
-                   shape(PACK, BINS, dtype=BF16), shape(FRAMES_HERE, PACK)),
+                  fixed(RANK, BINS), fixed(FRAMES_HERE, RANK), NEAR, NEAR, NEAR],
+        out_specs=[pl.BlockSpec((1, BINS, CHANS_HERE), lambda t: (t, 0, 0)), NEAR, NEAR, NEAR],
+        out_shape=(shape(EARLY, BINS, CHANS_HERE, dtype=BF16),
+                   pltpu.VMEM((PACK, CHANS_HERE), F32), pltpu.VMEM((PACK, BINS), BF16),
+                   pltpu.VMEM((FRAMES_HERE, PACK), F32)),
         scratch_shapes=natural,
         cost_estimate=pl.CostEstimate(flops=2500000000, bytes_accessed=8000000,
                                       transcendentals=0),
@@ -428,12 +424,7 @@
     )(samples, samples, start_freq.T, start_time, window, even_table, odd_table)
     power_last, to_chan = near_call(
         last_kernel, "last", (shape(BINS, CHANS_HERE, dtype=BF16), shape(N_TM, 3, QUAD, PACK)),
-        (following, even_table, odd_table),
-        [pltpu.VMEM((CHANS_HERE, HALF), BF16), pltpu.VMEM((1, HALF), F32),
-         pltpu.VMEM((PACK, BINS), BF16), pltpu.VMEM((FRAMES_HERE, PACK), F32),
-         pltpu.VMEM((PACK, CHANS_HERE), F32), flag((5,))],
-        far=(1,), others=(samples, window, freq_rows, time2, early_sum),
-        kinds_of_others=[outside] * 5)
+        (tail, following, window, even_table, odd_table, freq_rows, time2, early_sum), far=(1,))
 
     got = exchanged(to_chan, TM)
     gram_freq, freq_packed, chan_packed = near_call(

time: 116 us -> 115 us (level)
  Pallas kernels: 23.9 us -> 22.7 us
where the time goes in v6:
time: 115 us; the launch traced here: 114 us
  blocking collectives  47.9 us (42%)
  Pallas kernels  22.7 us (20%)
  waiting for transfers between devices  22.2 us (19%)
  starting transfers between devices  20.8 us (18%)
    all_to_all x3, blocking collectives, exchanged(): return lax.all_to_all(parts, axis, split_axis=0, concat_axis=0, tiled=True)  47.9 us
    all_to_all x3, waiting for transfers between devices, exchanged(): return lax.all_to_all(parts, axis, split_axis=0, concat_axis=0, tiled=True)  22.2 us
    pallas_call x11, Pallas kernels, near_call(): pl.pallas_call(body, in_specs=[NEAR] * (len(args) - len(others)) + list(k...  14.9 us
    all_to_all x3, starting transfers between devices, exchanged(): return lax.all_to_all(parts, axis, split_axis=0, concat_axis=0, tiled=True)  12.1 us
    ppermute x1, starting transfers between devices, local(): following = lax.ppermute(head, TM, route)  8.75 us
    pallas_call x1, Pallas kernels, local(): pl.pallas_call(early_kernel, grid=(EARLY,), in_specs=[pl.BlockSpec((CHANS...  7.77 us
  transfers between devices with their start and end apart: 4, of which 3 were waited for; matrix products, arithmetic and copies ran while one was open for 0% of the time, Pallas kernels for 10%

profile of v6, /device:TPU:1, one launch (start us, length us, event | category | flops | bytes accessed | tf_op | source)
XLA Modules:
  0.0 114.4 jit_solution(11640181786062932544)
XLA Ops:
  0.6 0.0 copy-start
  0.6 0.0 copy-start.1
  0.7 0.0 copy-start.4
  0.7 1.1 ends.1
  1.8 8.7 %collective-permute-start = (bf16[256,512]{1,0:T(8,128)(2,1)S(1)}, bf16[256,512]{1,0:T(8,128)(2,1)S(1)}, u32[]{:S(2)}, u32[]{:S(2)}) collective-permute-start(bf16[256,512]{1,0:T(8,128)(2,1)S(1)} %get-tuple-element.27), channel_id=1, source_target_pairs={{1,0},{2,1},{3,2},{4,3},{5,4},{6,5},{7,6},{8,7},{9,8},{10,9},{11,1... | collective-permute-start | bytes 786440 | tf_op jit(solution)/shard_map/ppermute | solution.py:404
  10.6 0.0 copy-done
  10.6 0.0 copy-done.1
  10.6 0.0 copy-done.4
  10.6 0.0 copy-start.3
  10.6 7.8 %early.1 = (bf16[7,512,256]{2,1,0:T(8,128)(2,1)}, f32[128,256]{1,0:T(8,128)S(1)}, bf16[128,512]{1,0:T(8,128)(2,1)S(1)}, f32[8,128]{1,0:T(8,128)S(1)}) custom-call(bf16[256,4096]{1,0:T(8,128)(2,1)} %second_ref.1, bf16[256,4096]{1,0:T(8,128)(2,1)} %second_ref.1, f32[64,512]{1,0:T(8,128)} %bitcast.4, f32[8,64]{1,0:T(8,128)} %time_ref.1, ...), custom_call_target="tpu_custom_call" | custom-call | flops 2500000000 | bytes 8000000 | tf_op jit(solution)/shard_map/early/pallas_call | solution.py:410
  18.4 0.0 copy-start.2
  18.4 0.0 collective-permute-done.halo_ref
  18.4 1.4 %last.1 = (bf16[512,256]{1,0:T(8,128)(2,1)S(1)}, f32[16,3,4,128]{3,2,1,0:T(4,128)}) custom-call(bf16[256,512]{1,0:T(8,128)(2,1)S(1)} %get-tuple-element.26.tail_ref, bf16[256,512]{1,0:T(8,128)(2,1)S(1)} %collective-permute-done.halo_ref, f32[1,512]{1,0:T(1,128)S(1)} %copy-done.4, bf16[512,512]{1,0:T(8,128)(2,1)S(1)} %copy-done, ...), custom_call_target="tpu_custom_call" | custom-call | bytes 2201600 | tf_op jit(solution)/shard_map/last/pallas_call | solution.py:382
  19.8 3.4 %all-to-all-start = ((f32[16,3,4,128]{3,2,1,0:T(4,128)}), f32[16,3,4,128]{3,2,1,0:T(4,128)S(1)}, u32[]{:S(2)}, u32[]{:S(2)}) async-start(f32[16,3,4,128]{3,2,1,0:T(4,128)} %get-tuple-element.31), calls=%async_computation | async-start | bytes 196608 | tf_op jit(solution)/shard_map/all_to_all | solution.py:365
  23.2 0.0 copy-done.3
  23.2 0.0 copy-done.2
  23.2 0.5 start.1
  23.7 7.1 %all-to-all-done.got_ref = f32[16,3,4,128]{3,2,1,0:T(4,128)S(1)} async-done(((f32[16,3,4,128]{3,2,1,0:T(4,128)}), f32[16,3,4,128]{3,2,1,0:T(4,128)S(1)}, u32[]{:S(2)}, u32[]{:S(2)}) %all-to-all-start) | async-done | bytes 98336 | tf_op jit(solution)/shard_map/all_to_all | solution.py:365
  30.8 2.1 %chan.1 = (f32[16,8,128]{2,1,0:T(8,128)S(1)}, f32[64,128]{1,0:T(8,128)S(1)}) custom-call(f32[16,3,4,128]{3,2,1,0:T(4,128)S(1)} %all-to-all-done.got_ref, f32[64,128]{1,0:T(8,128)S(1)} %get-tuple-element.32.gram_freq_ref, f32[128,128]{1,0:T(8,128)S(1)} %get-tuple-element.33.start_ref), custom_call_target="tpu_custom_call" | custom-call | bytes 294912 | tf_op jit(solution)/shard_map/chan/pallas_call | solution.py:382
  32.9 10.3 %all_to_all.30.chan_ref = f32[16,8,128]{2,1,0:T(8,128)S(1)} all-to-all(f32[16,8,128]{2,1,0:T(8,128)S(1)} %get-tuple-element.34), channel_id=1, replica_groups=mesh['chan_0'=4,'chan_1'=8,'tm_0'=8,'tm_1'=2] {'tm_0','tm_1'}, dimensions={0} | all-to-all | bytes 131072 | tf_op jit(solution)/shard_map/all_to_all | solution.py:365
  43.2 2.6 %freq.1 = (f32[8,512,128]{2,1,0:T(8,128)S(1)}, f32[16,16,128]{2,1,0:T(8,128)}) custom-call(f32[16,8,128]{2,1,0:T(8,128)S(1)} %all_to_all.30.chan_ref, f32[8,128]{1,0:T(8,128)S(1)} %get-tuple-element.29.time2_ref.start2_ref, bf16[512,256]{1,0:T(8,128)(2,1)S(1)} %get-tuple-element.36.last_ref, bf16[7,512,256]{2,1,0:T(8,128)(2,1)} %get-tuple-element.37.early_ref), custom_call_target="tpu_custom_call" | custom-call | bytes 4395008 | tf_op jit(solution)/shard_map/freq/pallas_call | solution.py:382
  45.9 3.4 %all-to-all-start.2 = ((f32[16,16,128]{2,1,0:T(8,128)}), f32[16,16,128]{2,1,0:T(8,128)S(1)}, u32[]{:S(2)}, u32[]{:S(2)}) async-start(f32[16,16,128]{2,1,0:T(8,128)} %get-tuple-element.38), calls=%async_computation.2 | async-start | bytes 262144 | tf_op jit(solution)/shard_map/all_to_all | solution.py:365
  49.3 0.8 chan_out.1
  50.1 8.4 %all-to-all-done.2.got_ref = f32[16,16,128]{2,1,0:T(8,128)S(1)} async-done(((f32[16,16,128]{2,1,0:T(8,128)}), f32[16,16,128]{2,1,0:T(8,128)S(1)}, u32[]{:S(2)}, u32[]{:S(2)}) %all-to-all-start.2) | async-done | bytes 131104 | tf_op jit(solution)/shard_map/all_to_all | solution.py:365
  58.5 23.9 %all_to_all.31.got_ref = f32[32,5,4,128]{3,2,1,0:T(4,128)S(1)} all-to-all(f32[32,5,4,128]{3,2,1,0:T(4,128)S(1)} %spread.1), channel_id=1, replica_groups=mesh['chan_0'=4,'chan_1'=8,'tm_0'=8,'tm_1'=2] {'chan_0','chan_1'}, dimensions={0} | all-to-all | bytes 655360 | tf_op jit(solution)/shard_map/all_to_all | solution.py:365
  82.5 0.1 relay.1
  82.5 13.6 %all_to_all.32.got_ref = f32[16,5,4,128]{3,2,1,0:T(4,128)S(1)} all-to-all(f32[16,5,4,128]{3,2,1,0:T(4,128)S(1)} %relay.1), channel_id=1, replica_groups=mesh['chan_0'=4,'chan_1'=8,'tm_0'=8,'tm_1'=2] {'tm_0','tm_1'}, dimensions={0} | all-to-all | bytes 327680 | tf_op jit(solution)/shard_map/all_to_all | solution.py:365
  96.2 2.9 %freq_admm.1 = (f32[32,4,128]{2,1,0:T(4,128)}, f32[256,128]{1,0:T(8,128)S(1)}, f32[64,128]{1,0:T(8,128)S(1)}) custom-call(f32[16,5,4,128]{3,2,1,0:T(4,128)S(1)} %all_to_all.32.got_ref, f32[64,128]{1,0:T(8,128)S(1)} %get-tuple-element.40.gram_time_ref, f32[256,128]{1,0:T(8,128)S(1)} %get-tuple-element.41.start_ref, f32[8,512,128]{2,1,0:T(8,128)S(1)} %get-tuple-element.42.part_ref), custom_call_target="tpu_custom_call" | custom-call | bytes 2654208 | tf_op jit(solution)/shard_map/freq_admm/pallas_call | solution.py:382
  99.0 5.2 %all-to-all-start.5 = ((f32[32,4,128]{2,1,0:T(4,128)}), f32[32,4,128]{2,1,0:T(4,128)S(1)}, u32[]{:S(2)}, u32[]{:S(2)}) async-start(f32[32,4,128]{2,1,0:T(4,128)} %get-tuple-element.46), calls=%async_computation.5 | async-start | bytes 131072 | tf_op jit(solution)/shard_map/all_to_all | solution.py:365
  104.3 2.1 %freq_out.1 = (f32[128,128]{1,0:T(8,128)S(1)}, f32[1,128]{1,0:T(1,128)S(1)}, f32[64,512]{1,0:T(8,128)}) custom-call(f32[256,128]{1,0:T(8,128)S(1)} %get-tuple-element.43.freq_ref, f32[64,128]{1,0:T(8,128)S(1)} %get-tuple-element.44.gram_chan_ref), custom_call_target="tpu_custom_call" | custom-call | bytes 360960 | tf_op jit(solution)/shard_map/freq_out/pallas_call | solution.py:382
  106.4 6.7 %all-to-all-done.5.got_ref = f32[32,4,128]{2,1,0:T(4,128)S(1)} async-done(((f32[32,4,128]{2,1,0:T(4,128)}), f32[32,4,128]{2,1,0:T(4,128)S(1)}, u32[]{:S(2)}, u32[]{:S(2)}) %all-to-all-start.5) | async-done | bytes 65568 | tf_op jit(solution)/shard_map/all_to_all | solution.py:365
  113.1 1.3 %time_admm.1 = f32[8,64]{1,0:T(8,128)} custom-call(f32[32,4,128]{2,1,0:T(4,128)S(1)} %all-to-all-done.5.got_ref, f32[128,128]{1,0:T(8,128)S(1)} %get-tuple-element.47.inverse_ref, f32[1,128]{1,0:T(1,128)S(1)} %get-tuple-element.48.penalty_ref, f32[8,128]{1,0:T(8,128)S(1)} %get-tuple-element.29.time2_ref.start2_ref), custom_call_target="tpu_custom_call" | custom-call | bytes 137728 | tf_op jit(solution)/shard_map/time_admm/pallas_call | solution.py:382
  (1 shorter events, 0.0 us)
Async XLA Ops:
  0.6 9.9 %copy-start = (bf16[512,512]{1,0:T(8,128)(2,1)S(1)}, bf16[512,512]{1,0:T(8,128)(2,1)}, u32[]{:S(2)}) copy-start(bf16[512,512]{1,0:T(8,128)(2,1)} %constant.6.clone.even_ref) | copy-start | bytes 1572868
  0.6 9.9 %copy-start.1 = (bf16[512,512]{1,0:T(8,128)(2,1)S(1)}, bf16[512,512]{1,0:T(8,128)(2,1)}, u32[]{:S(2)}) copy-start(bf16[512,512]{1,0:T(8,128)(2,1)} %constant.7.clone.odd_ref) | copy-start | bytes 1572868
  0.7 9.9 %copy-start.4 = (f32[1,512]{1,0:T(1,128)S(1)}, f32[1,512]{1,0:T(1,128)}, u32[]{:S(2)}) copy-start(f32[1,512]{1,0:T(1,128)} %constant.8.clone.window_ref) | copy-start | bytes 6148
  1.8 16.6 %collective-permute-start = (bf16[256,512]{1,0:T(8,128)(2,1)S(1)}, bf16[256,512]{1,0:T(8,128)(2,1)S(1)}, u32[]{:S(2)}, u32[]{:S(2)}) collective-permute-start(bf16[256,512]{1,0:T(8,128)(2,1)S(1)} %get-tuple-element.27), channel_id=1, source_target_pairs={{1,0},{2,1},{3,2},{4,3},{5,4},{6,5},{7,6},{8,7},{9,8},{10,9},{11,1... | collective-permute-start | bytes 786440 | tf_op jit(solution)/shard_map/ppermute | solution.py:404
  10.6 12.6 %copy-start.3 = (f32[256,64]{0,1:T(8,128)S(1)}, f32[256,64]{0,1:T(8,128)}, u32[]{:S(2)}) copy-start(f32[256,64]{0,1:T(8,128)} %param.8) | copy-start | bytes 196612
  18.4 4.8 %copy-start.2 = (f32[512,64]{0,1:T(8,128)S(1)}, f32[512,64]{0,1:T(8,128)}, u32[]{:S(2)}) copy-start(f32[512,64]{0,1:T(8,128)} %param.9) | copy-start | bytes 393220
  19.8 11.0 %all-to-all-start = ((f32[16,3,4,128]{3,2,1,0:T(4,128)}), f32[16,3,4,128]{3,2,1,0:T(4,128)S(1)}, u32[]{:S(2)}, u32[]{:S(2)}) async-start(f32[16,3,4,128]{3,2,1,0:T(4,128)} %get-tuple-element.31), calls=%async_computation | async-start | bytes 196608 | tf_op jit(solution)/shard_map/all_to_all | solution.py:365
  45.9 12.6 %all-to-all-start.2 = ((f32[16,16,128]{2,1,0:T(8,128)}), f32[16,16,128]{2,1,0:T(8,128)S(1)}, u32[]{:S(2)}, u32[]{:S(2)}) async-start(f32[16,16,128]{2,1,0:T(8,128)} %get-tuple-element.38), calls=%async_computation.2 | async-start | bytes 262144 | tf_op jit(solution)/shard_map/all_to_all | solution.py:365
  99.0 14.1 %all-to-all-start.5 = ((f32[32,4,128]{2,1,0:T(4,128)}), f32[32,4,128]{2,1,0:T(4,128)S(1)}, u32[]{:S(2)}, u32[]{:S(2)}) async-start(f32[32,4,128]{2,1,0:T(4,128)} %get-tuple-element.46), calls=%async_computation.5 | async-start | bytes 131072 | tf_op jit(solution)/shard_map/all_to_all | solution.py:365

commit v7 on v6

--- a/solution.py
+++ b/solution.py
@@ -170,8 +170,11 @@
 EARLY = FRAMES_HERE - 1
 
 
+FAR = 4
+
+
 def early_kernel(first_ref, second_ref, freq_ref, time_ref, window_ref, even_ref, odd_ref,
-                 power_ref, sum_ref, rows_ref, time2_ref, natural):
+                 power_ref, near_ref, sum_ref, rows_ref, time2_ref, natural):
     t = pl.program_id(0)
 
     @pl.when(t == 0)
@@ -187,6 +190,7 @@
 
     power = frame_power(first_ref[...], second_ref[...], window_ref[...], even_ref, odd_ref)
     power_ref[0] = power
+    near_ref[jnp.maximum(t - FAR, 0)] = power
     sum_ref[...] += chan_term(rows_ref, power, time2_ref[pl.ds(t, 1), :])
 
 
@@ -228,18 +232,17 @@
     send_ref[...] = jnp.broadcast_to(new[None], send_ref.shape)
 
 
-FIRST_PART = 3
 TILE = 256
 
 
-def freq_kernel(chan_ref, time2_ref, last_ref, early_ref, part_ref, send_ref, sides, held, sems):
-    loads = [pltpu.make_async_copy(early_ref.at[t], held.at[t], sems.at[t])
-             for t in range(EARLY)]
+def freq_kernel(chan_ref, time2_ref, last_ref, near_ref, far_ref, part_ref, send_ref,
+                sides, held, sems):
+    loads = [pltpu.make_async_copy(far_ref.at[t], held.at[t], sems.at[t]) for t in range(FAR)]
     for load in loads:
         load.start()
     side = high_low(both_halves(chan_ref[...].reshape(CHANS_HERE // 2, PACK)))
     sides[...] = jnp.concatenate([side, side], axis=1)
-    order = [EARLY] + list(range(EARLY))
+    order = list(range(FAR, FRAMES_HERE)) + list(range(FAR))
 
     def body(*accs):
         for m in (0, 1):
@@ -247,18 +250,15 @@
 
         def multiply(i):
             t, m = order[i], i % 2
-            power = last_ref[...] if t == EARLY else held[t]
+            power = last_ref[...] if t == EARLY else near_ref[t - FAR] if t >= FAR else held[t]
             pltpu.matmul_acc_lhs(accs[i % 4], power, load_staged_rhs=0 if i < 2 else None)
 
         def collect(i):
             part_ref[order[i]] = pltpu.matmul_pop(accs[i % 4])[:, :PACK]
 
         for i in range(FRAMES_HERE):
-            if i == 1:
-                for load in loads[:FIRST_PART]:
-                    load.wait()
-            if i == 1 + FIRST_PART:
-                for load in loads[FIRST_PART:]:
+            if order[i] == 0:
+                for load in loads:
                     load.wait()
             multiply(i)
             if i >= 2:
@@ -407,14 +407,16 @@
     def fixed(*dims):
         return pl.BlockSpec(dims, lambda t: (0,) * len(dims))
 
-    power, early_sum, freq_rows, time2 = pl.pallas_call(
+    power, power_near, early_sum, freq_rows, time2 = pl.pallas_call(
         early_kernel,
         grid=(EARLY,),
         in_specs=[pl.BlockSpec((CHANS_HERE, HALF), lambda t: (0, t)),
                   pl.BlockSpec((CHANS_HERE, HALF), lambda t: (0, t + 1)),
                   fixed(RANK, BINS), fixed(FRAMES_HERE, RANK), NEAR, NEAR, NEAR],
-        out_specs=[pl.BlockSpec((1, BINS, CHANS_HERE), lambda t: (t, 0, 0)), NEAR, NEAR, NEAR],
-        out_shape=(shape(EARLY, BINS, CHANS_HERE, dtype=BF16),
+        out_specs=[pl.BlockSpec((1, BINS, CHANS_HERE),
+                                lambda t: (jnp.minimum(t, FAR), 0, 0))] + [NEAR] * 4,
+        out_shape=(shape(FAR + 1, BINS, CHANS_HERE, dtype=BF16),
+                   pltpu.VMEM((EARLY - FAR, BINS, CHANS_HERE), BF16),
                    pltpu.VMEM((PACK, CHANS_HERE), F32), pltpu.VMEM((PACK, BINS), BF16),
                    pltpu.VMEM((FRAMES_HERE, PACK), F32)),
         scratch_shapes=natural,
@@ -438,9 +440,9 @@
 
     part, to_freq = near_call(
         freq_kernel, "freq", (shape(FRAMES_HERE, BINS, PACK), shape(N_TM, 16, PACK)),
-        (chan_all, time2, power_last),
-        [pltpu.VMEM((CHANS_HERE, TILE), BF16), pltpu.VMEM((EARLY, BINS, CHANS_HERE), BF16),
-         flag((EARLY,))], far=(1,), others=(power,), kinds_of_others=[outside])
+        (chan_all, time2, power_last, power_near),
+        [pltpu.VMEM((CHANS_HERE, TILE), BF16), pltpu.VMEM((FAR, BINS, CHANS_HERE), BF16),
+         flag((FAR,))], far=(1,), others=(power,), kinds_of_others=[outside])
     got = exchanged(to_freq, TM)
     gram_part, chan_out = near_call(
         chan_out_kernel, "chan_out", (shape(N_GRAM, QUAD, PACK), shape(RANK, CHANS_HERE)),

time: 115 us -> 115 us (level)
  no operation moved by 1% of the time
where the time goes in v7:
time: 115 us; the launch traced here: 114 us
  blocking collectives  47.9 us (42%)
  Pallas kernels  22.5 us (20%)
  waiting for transfers between devices  22.2 us (19%)
  starting transfers between devices  20.8 us (18%)
    all_to_all x3, blocking collectives, exchanged(): return lax.all_to_all(parts, axis, split_axis=0, concat_axis=0, tiled=True)  47.9 us
    all_to_all x3, waiting for transfers between devices, exchanged(): return lax.all_to_all(parts, axis, split_axis=0, concat_axis=0, tiled=True)  22.2 us
    pallas_call x11, Pallas kernels, near_call(): pl.pallas_call(body, in_specs=[NEAR] * (len(args) - len(others)) + list(k...  14.6 us
    all_to_all x3, starting transfers between devices, exchanged(): return lax.all_to_all(parts, axis, split_axis=0, concat_axis=0, tiled=True)  12.1 us
    ppermute x1, starting transfers between devices, local(): following = lax.ppermute(head, TM, route)  8.75 us
    pallas_call x1, Pallas kernels, local(): pl.pallas_call(early_kernel, grid=(EARLY,), in_specs=[pl.BlockSpec((CHANS...  7.85 us
  transfers between devices with their start and end apart: 4, of which 3 were waited for; matrix products, arithmetic and copies ran while one was open for 0% of the time, Pallas kernels for 10%

profile of v7, /device:TPU:1, one launch (start us, length us, event | category | flops | bytes accessed | tf_op | source)
XLA Modules:
  0.0 114.2 jit_solution(7719398007822300595)
XLA Ops:
  0.6 0.0 copy-start.4
  0.6 0.0 copy-start
  0.7 0.0 copy-start.1
  0.7 1.1 ends.1
  1.8 8.7 %collective-permute-start = (bf16[256,512]{1,0:T(8,128)(2,1)S(1)}, bf16[256,512]{1,0:T(8,128)(2,1)S(1)}, u32[]{:S(2)}, u32[]{:S(2)}) collective-permute-start(bf16[256,512]{1,0:T(8,128)(2,1)S(1)} %get-tuple-element.28), channel_id=1, source_target_pairs={{1,0},{2,1},{3,2},{4,3},{5,4},{6,5},{7,6},{8,7},{9,8},{10,9},{11,1... | collective-permute-start | bytes 786440 | tf_op jit(solution)/shard_map/ppermute | solution.py:404
  10.6 0.0 copy-done.4
  10.6 0.0 copy-done
  10.6 0.0 copy-done.1
  10.6 0.0 copy-start.3
  10.6 7.8 %early.1 = (bf16[5,512,256]{2,1,0:T(8,128)(2,1)}, bf16[3,512,256]{2,1,0:T(8,128)(2,1)S(1)}, f32[128,256]{1,0:T(8,128)S(1)}, bf16[128,512]{1,0:T(8,128)(2,1)S(1)}, f32[8,128]{1,0:T(8,128)S(1)}) custom-call(bf16[256,4096]{1,0:T(8,128)(2,1)} %second_ref.1, bf16[256,4096]{1,0:T(8,128)(2,1)} %second_ref.1, f32[64,512]{1,0:T(8,128)} %bitcast.4, f32[8,64]{1,0:T(8,128)} %time_ref.1, ...), custom_call_target="tpu_custom_call" | custom-call | flops 2500000000 | bytes 8000000 | tf_op jit(solution)/shard_map/early/pallas_call | solution.py:410
  18.5 0.0 copy-start.2
  18.5 0.0 collective-permute-done.halo_ref
  18.5 1.4 %last.1 = (bf16[512,256]{1,0:T(8,128)(2,1)S(1)}, f32[16,3,4,128]{3,2,1,0:T(4,128)}) custom-call(bf16[256,512]{1,0:T(8,128)(2,1)S(1)} %get-tuple-element.27.tail_ref, bf16[256,512]{1,0:T(8,128)(2,1)S(1)} %collective-permute-done.halo_ref, f32[1,512]{1,0:T(1,128)S(1)} %copy-done.4, bf16[512,512]{1,0:T(8,128)(2,1)S(1)} %copy-done.1, ...), custom_call_target="tpu_custom_call" | custom-call | bytes 2201600 | tf_op jit(solution)/shard_map/last/pallas_call | solution.py:382
  19.8 3.4 %all-to-all-start = ((f32[16,3,4,128]{3,2,1,0:T(4,128)}), f32[16,3,4,128]{3,2,1,0:T(4,128)S(1)}, u32[]{:S(2)}, u32[]{:S(2)}) async-start(f32[16,3,4,128]{3,2,1,0:T(4,128)} %get-tuple-element.32), calls=%async_computation | async-start | bytes 196608 | tf_op jit(solution)/shard_map/all_to_all | solution.py:365
  23.3 0.0 copy-done.3
  23.3 0.0 copy-done.2
  23.3 0.4 start.1
  23.7 7.1 %all-to-all-done.got_ref = f32[16,3,4,128]{3,2,1,0:T(4,128)S(1)} async-done(((f32[16,3,4,128]{3,2,1,0:T(4,128)}), f32[16,3,4,128]{3,2,1,0:T(4,128)S(1)}, u32[]{:S(2)}, u32[]{:S(2)}) %all-to-all-start) | async-done | bytes 98336 | tf_op jit(solution)/shard_map/all_to_all | solution.py:365
  30.9 2.1 %chan.1 = (f32[16,8,128]{2,1,0:T(8,128)S(1)}, f32[64,128]{1,0:T(8,128)S(1)}) custom-call(f32[16,3,4,128]{3,2,1,0:T(4,128)S(1)} %all-to-all-done.got_ref, f32[64,128]{1,0:T(8,128)S(1)} %get-tuple-element.33.gram_freq_ref, f32[128,128]{1,0:T(8,128)S(1)} %get-tuple-element.34.start_ref), custom_call_target="tpu_custom_call" | custom-call | bytes 294912 | tf_op jit(solution)/shard_map/chan/pallas_call | solution.py:382
  33.0 10.3 %all_to_all.30.chan_ref = f32[16,8,128]{2,1,0:T(8,128)S(1)} all-to-all(f32[16,8,128]{2,1,0:T(8,128)S(1)} %get-tuple-element.35), channel_id=1, replica_groups=mesh['chan_0'=4,'chan_1'=8,'tm_0'=8,'tm_1'=2] {'tm_0','tm_1'}, dimensions={0} | all-to-all | bytes 131072 | tf_op jit(solution)/shard_map/all_to_all | solution.py:365
  43.3 2.4 %freq.1 = (f32[8,512,128]{2,1,0:T(8,128)S(1)}, f32[16,16,128]{2,1,0:T(8,128)}) custom-call(f32[16,8,128]{2,1,0:T(8,128)S(1)} %all_to_all.30.chan_ref, f32[8,128]{1,0:T(8,128)S(1)} %get-tuple-element.30.time2_ref.start2_ref, bf16[512,256]{1,0:T(8,128)(2,1)S(1)} %get-tuple-element.37.last_ref, bf16[3,512,256]{2,1,0:T(8,128)(2,1)S(1)} %get-tuple-element.38.near_ref, ...), custom_call_target="tpu_custom_call" | custom-call | bytes 4657152 | tf_op jit(solution)/shard_map/freq/pallas_call | solution.py:382
  45.7 3.4 %all-to-all-start.2 = ((f32[16,16,128]{2,1,0:T(8,128)}), f32[16,16,128]{2,1,0:T(8,128)S(1)}, u32[]{:S(2)}, u32[]{:S(2)}) async-start(f32[16,16,128]{2,1,0:T(8,128)} %get-tuple-element.40), calls=%async_computation.2 | async-start | bytes 262144 | tf_op jit(solution)/shard_map/all_to_all | solution.py:365
  49.1 0.8 chan_out.1
  49.9 8.4 %all-to-all-done.2.got_ref = f32[16,16,128]{2,1,0:T(8,128)S(1)} async-done(((f32[16,16,128]{2,1,0:T(8,128)}), f32[16,16,128]{2,1,0:T(8,128)S(1)}, u32[]{:S(2)}, u32[]{:S(2)}) %all-to-all-start.2) | async-done | bytes 131104 | tf_op jit(solution)/shard_map/all_to_all | solution.py:365
  58.3 23.9 %all_to_all.31.got_ref = f32[32,5,4,128]{3,2,1,0:T(4,128)S(1)} all-to-all(f32[32,5,4,128]{3,2,1,0:T(4,128)S(1)} %spread.1), channel_id=1, replica_groups=mesh['chan_0'=4,'chan_1'=8,'tm_0'=8,'tm_1'=2] {'chan_0','chan_1'}, dimensions={0} | all-to-all | bytes 655360 | tf_op jit(solution)/shard_map/all_to_all | solution.py:365
  82.3 0.1 relay.1
  82.3 13.6 %all_to_all.32.got_ref = f32[16,5,4,128]{3,2,1,0:T(4,128)S(1)} all-to-all(f32[16,5,4,128]{3,2,1,0:T(4,128)S(1)} %relay.1), channel_id=1, replica_groups=mesh['chan_0'=4,'chan_1'=8,'tm_0'=8,'tm_1'=2] {'tm_0','tm_1'}, dimensions={0} | all-to-all | bytes 327680 | tf_op jit(solution)/shard_map/all_to_all | solution.py:365
  96.0 2.9 %freq_admm.1 = (f32[32,4,128]{2,1,0:T(4,128)}, f32[256,128]{1,0:T(8,128)S(1)}, f32[64,128]{1,0:T(8,128)S(1)}) custom-call(f32[16,5,4,128]{3,2,1,0:T(4,128)S(1)} %all_to_all.32.got_ref, f32[64,128]{1,0:T(8,128)S(1)} %get-tuple-element.42.gram_time_ref, f32[256,128]{1,0:T(8,128)S(1)} %get-tuple-element.43.start_ref, f32[8,512,128]{2,1,0:T(8,128)S(1)} %get-tuple-element.44.part_ref), custom_call_target="tpu_custom_call" | custom-call | bytes 2654208 | tf_op jit(solution)/shard_map/freq_admm/pallas_call | solution.py:382
  98.8 5.2 %all-to-all-start.5 = ((f32[32,4,128]{2,1,0:T(4,128)}), f32[32,4,128]{2,1,0:T(4,128)S(1)}, u32[]{:S(2)}, u32[]{:S(2)}) async-start(f32[32,4,128]{2,1,0:T(4,128)} %get-tuple-element.48), calls=%async_computation.5 | async-start | bytes 131072 | tf_op jit(solution)/shard_map/all_to_all | solution.py:365
  104.1 2.1 %freq_out.1 = (f32[128,128]{1,0:T(8,128)S(1)}, f32[1,128]{1,0:T(1,128)S(1)}, f32[64,512]{1,0:T(8,128)}) custom-call(f32[256,128]{1,0:T(8,128)S(1)} %get-tuple-element.45.freq_ref, f32[64,128]{1,0:T(8,128)S(1)} %get-tuple-element.46.gram_chan_ref), custom_call_target="tpu_custom_call" | custom-call | bytes 360960 | tf_op jit(solution)/shard_map/freq_out/pallas_call | solution.py:382
  106.2 6.7 %all-to-all-done.5.got_ref = f32[32,4,128]{2,1,0:T(4,128)S(1)} async-done(((f32[32,4,128]{2,1,0:T(4,128)}), f32[32,4,128]{2,1,0:T(4,128)S(1)}, u32[]{:S(2)}, u32[]{:S(2)}) %all-to-all-start.5) | async-done | bytes 65568 | tf_op jit(solution)/shard_map/all_to_all | solution.py:365
  112.9 1.3 %time_admm.1 = f32[8,64]{1,0:T(8,128)} custom-call(f32[32,4,128]{2,1,0:T(4,128)S(1)} %all-to-all-done.5.got_ref, f32[128,128]{1,0:T(8,128)S(1)} %get-tuple-element.49.inverse_ref, f32[1,128]{1,0:T(1,128)S(1)} %get-tuple-element.50.penalty_ref, f32[8,128]{1,0:T(8,128)S(1)} %get-tuple-element.30.time2_ref.start2_ref), custom_call_target="tpu_custom_call" | custom-call | bytes 137728 | tf_op jit(solution)/shard_map/time_admm/pallas_call | solution.py:382
  (1 shorter events, 0.0 us)
Async XLA Ops:
  0.6 9.9 %copy-start.4 = (f32[1,512]{1,0:T(1,128)S(1)}, f32[1,512]{1,0:T(1,128)}, u32[]{:S(2)}) copy-start(f32[1,512]{1,0:T(1,128)} %constant.8.clone.window_ref) | copy-start | bytes 6148
  0.6 9.9 %copy-start = (bf16[512,512]{1,0:T(8,128)(2,1)S(1)}, bf16[512,512]{1,0:T(8,128)(2,1)}, u32[]{:S(2)}) copy-start(bf16[512,512]{1,0:T(8,128)(2,1)} %constant.7.clone.odd_ref) | copy-start | bytes 1572868
  0.7 9.9 %copy-start.1 = (bf16[512,512]{1,0:T(8,128)(2,1)S(1)}, bf16[512,512]{1,0:T(8,128)(2,1)}, u32[]{:S(2)}) copy-start(bf16[512,512]{1,0:T(8,128)(2,1)} %constant.6.clone.even_ref) | copy-start | bytes 1572868
  1.8 16.6 %collective-permute-start = (bf16[256,512]{1,0:T(8,128)(2,1)S(1)}, bf16[256,512]{1,0:T(8,128)(2,1)S(1)}, u32[]{:S(2)}, u32[]{:S(2)}) collective-permute-start(bf16[256,512]{1,0:T(8,128)(2,1)S(1)} %get-tuple-element.28), channel_id=1, source_target_pairs={{1,0},{2,1},{3,2},{4,3},{5,4},{6,5},{7,6},{8,7},{9,8},{10,9},{11,1... | collective-permute-start | bytes 786440 | tf_op jit(solution)/shard_map/ppermute | solution.py:404
  10.6 12.7 %copy-start.3 = (f32[256,64]{0,1:T(8,128)S(1)}, f32[256,64]{0,1:T(8,128)}, u32[]{:S(2)}) copy-start(f32[256,64]{0,1:T(8,128)} %param.8) | copy-start | bytes 196612
  18.5 4.8 %copy-start.2 = (f32[512,64]{0,1:T(8,128)S(1)}, f32[512,64]{0,1:T(8,128)}, u32[]{:S(2)}) copy-start(f32[512,64]{0,1:T(8,128)} %param.9) | copy-start | bytes 393220
  19.8 11.0 %all-to-all-start = ((f32[16,3,4,128]{3,2,1,0:T(4,128)}), f32[16,3,4,128]{3,2,1,0:T(4,128)S(1)}, u32[]{:S(2)}, u32[]{:S(2)}) async-start(f32[16,3,4,128]{3,2,1,0:T(4,128)} %get-tuple-element.32), calls=%async_computation | async-start | bytes 196608 | tf_op jit(solution)/shard_map/all_to_all | solution.py:365
  45.7 12.6 %all-to-all-start.2 = ((f32[16,16,128]{2,1,0:T(8,128)}), f32[16,16,128]{2,1,0:T(8,128)S(1)}, u32[]{:S(2)}, u32[]{:S(2)}) async-start(f32[16,16,128]{2,1,0:T(8,128)} %get-tuple-element.40), calls=%async_computation.2 | async-start | bytes 262144 | tf_op jit(solution)/shard_map/all_to_all | solution.py:365
  98.8 14.1 %all-to-all-start.5 = ((f32[32,4,128]{2,1,0:T(4,128)}), f32[32,4,128]{2,1,0:T(4,128)S(1)}, u32[]{:S(2)}, u32[]{:S(2)}) async-start(f32[32,4,128]{2,1,0:T(4,128)} %get-tuple-element.48), calls=%async_computation.5 | async-start | bytes 131072 | tf_op jit(solution)/shard_map/all_to_all | solution.py:365
